TPU v7x, 32 devices: a whole 2x2x4 slice. The times are simulated.
32 devices in a mesh: pool: 8 (over y, x, core), mp: 4 (over z).
Axes of the slice: x: 2, y: 2, z: 4, core: 2. Of those that a mesh axis runs over, the one named last changes fastest.
Arguments:
- hidden_in: bfloat16 [32, 2048], P('pool')
- mix_gain: float32 [2048], replicated, may hold values from 0.25 to 1.75
- project_in: bfloat16 [2048, 1920], P(None, 'mp'), may hold values from -0.125 to 0.125
- query_gain: float32 [64], replicated, may hold values from 0.1 to 1.9
- key_gain: float32 [64], replicated, may hold values from 0.1 to 1.9
- page_cache: bfloat16 [512, 128, 640], P(('pool', 'mp')), may hold values from -2.5 to 2.5
- page_table: int32 [32, 64], replicated, may hold values from -1 to 511, as said below
- lengths: int32 [32], replicated, may hold values from 1 to 8192, as said below
- row_order: int32 [32], replicated, may hold values from 0 to 31, each once
- out_weight: bfloat16 [1280, 2048], P('mp'), may hold values from -0.75 to 0.75
- feed_gain: float32 [2048], replicated, may hold values from 0.25 to 1.75
- gate_weight: bfloat16 [2048, 5120], P(None, 'mp'), may hold values from -0.125 to 0.125
- up_weight: bfloat16 [2048, 5120], P(None, 'mp'), may hold values from -0.125 to 0.125
- down_weight: bfloat16 [5120, 2048], P('mp'), may hold values from -0.078125 to 0.078125
Outputs:
- hidden_out: bfloat16 [32, 2048], P(('pool', 'mp'))
- new_entries: bfloat16 [32, 640], P(('pool', 'mp'))
Inputs may be any that keep to these rules, and one draw needn't show every extreme that they name: Request r has lengths[r] cached tokens; one request in every draw has exactly 8192. `page_table`: entries j of request r with j * 128 < lengths[r] hold page numbers, no page appearing twice in the table; all other entries are -1. Row i of hidden_in serves request row_order[i].
All inputs are finite; a program needn't handle non-finite values.
Results may differ from a plain program's by a relative error of at most 0.014.
Values may be sent and summed in bfloat16 or wider, within the bound.
No kernel may reach another device: no remote copies, remote signals or barrier semaphores. Data moves between devices by JAX's collectives and lax.ppermute only.
A program may use at most 64 MiB of HBM per device.

v0:
```python
import jax
import jax.numpy as jnp
from jax import lax
from jax.sharding import PartitionSpec as P

H = 20
KVH = 5
HD = 64
PAGE = 128
MAXP = 64


EPS_WIDE = 1e-05
EPS_HEAD = 1e-06


def rms_scale(values, scaling, epsilon):
    mean_square = jnp.mean(values * values, axis=-1, keepdims=True)
    return values * lax.rsqrt(mean_square + epsilon) * scaling


def rotate(head_rows, positions):
    middle = head_rows.shape[-1] // 2
    frequency = 10000.0 ** (-(2.0 * jnp.arange(middle, dtype=jnp.float32)) / head_rows.shape[-1])
    angles = positions.astype(jnp.float32)[..., None, None] * frequency
    cosines = jnp.cos(angles)
    sine_term = jnp.sin(angles)
    low_half = head_rows[..., :middle]
    high_half = head_rows[..., middle:]
    return jnp.concatenate(
        [low_half * cosines - high_half * sine_term, high_half * cosines + low_half * sine_term],
        axis=-1,
    )


def shards(
    hidden_in,
    mix_gain,
    project_in,
    query_gain,
    key_gain,
    page_cache,
    page_table,
    lengths,
    row_order,
    out_weight,
    feed_gain,
    gate_weight,
    up_weight,
    down_weight,
):
    pool_count = lax.axis_size("pool")
    mp_count = lax.axis_size("mp")
    pool_index = lax.axis_index("pool")
    mp_index = lax.axis_index("mp")
    group_rows = hidden_in.shape[0]
    local_pages = page_cache.shape[0]
    head_cols = H * HD // mp_count
    groups = H // KVH
    inv_root = HD ** (-0.5)
    highest = lax.Precision.HIGHEST
    wide_rows = hidden_in.astype(jnp.float32)
    normed = rms_scale(wide_rows, mix_gain, EPS_WIDE).astype(jnp.bfloat16)
    packed_part = jnp.dot(normed, project_in, preferred_element_type=jnp.float32).astype(
        jnp.bfloat16
    )
    gathered = lax.all_gather(packed_part, ("pool", "mp"), axis=1, tiled=True)
    packed = gathered.reshape(group_rows, pool_count, (H + 2 * KVH) * HD)
    request_ids = row_order.reshape(pool_count, group_rows).T
    row_lengths = lengths[request_ids]
    row_tables = page_table[request_ids]
    queries = packed[..., : H * HD].astype(jnp.float32).reshape(group_rows, pool_count, H, HD)
    queries = rotate(rms_scale(queries, query_gain, EPS_HEAD), row_lengths).astype(jnp.bfloat16)
    own_packed = lax.dynamic_index_in_dim(packed, pool_index, 1, keepdims=False)
    own_lengths = lax.dynamic_index_in_dim(row_lengths, pool_index, 1, keepdims=False)
    own_queries = lax.dynamic_index_in_dim(queries, pool_index, 1, keepdims=False)
    key_new = (
        own_packed[:, H * HD : (H + KVH) * HD].astype(jnp.float32).reshape(group_rows, KVH, HD)
    )
    key_new = rotate(rms_scale(key_new, key_gain, EPS_HEAD), own_lengths).astype(jnp.bfloat16)
    value_new = own_packed[:, (H + KVH) * HD :].reshape(group_rows, KVH, HD)
    own_score = (
        jnp.einsum(
            "qkgd,qkd->qkg",
            own_queries.reshape(group_rows, KVH, groups, HD),
            key_new,
            preferred_element_type=jnp.float32,
        )
        * inv_root
    )
    own_weight = jnp.exp(own_score)
    own_numerator = jnp.einsum(
        "qkg,qkd->qkgd",
        own_weight.astype(jnp.bfloat16),
        value_new,
        preferred_element_type=jnp.float32,
    ).reshape(group_rows, H * HD)
    own_weight = own_weight.reshape(group_rows, H)
    page_ids = (pool_index * mp_count + mp_index) * local_pages + jnp.arange(
        local_pages, dtype=jnp.int32
    )
    matches = row_tables[None] == page_ids[:, None, None, None]
    chosen = jnp.any(matches, axis=-1)
    blocks = jnp.sum(jnp.where(matches, jnp.arange(MAXP, dtype=jnp.int32), 0), axis=(1, 2, 3))
    page_length = jnp.sum(jnp.where(chosen, row_lengths[None], 0), axis=(1, 2))
    chosen_half = chosen.astype(jnp.bfloat16)
    chosen_full = chosen.astype(jnp.float32)
    page_queries = jnp.einsum(
        "sqp,qphd->shd", chosen_half, queries, preferred_element_type=jnp.float32
    ).astype(jnp.bfloat16)
    key_rows = page_cache[..., : KVH * HD].reshape(local_pages, PAGE, KVH, HD)
    value_rows = page_cache[..., KVH * HD :].reshape(local_pages, PAGE, KVH, HD)
    scores = (
        jnp.einsum(
            "skgd,stkd->skgt",
            page_queries.reshape(local_pages, KVH, groups, HD),
            key_rows,
            preferred_element_type=jnp.float32,
        )
        * inv_root
    )
    in_range = (
        blocks[:, None] * PAGE + jnp.arange(PAGE, dtype=jnp.int32)[None, :] < page_length[:, None]
    )
    weights = jnp.where(in_range[:, None, None, :], jnp.exp(scores), 0.0)
    page_total = jnp.sum(weights, axis=-1).reshape(local_pages, H)
    page_weighted = jnp.einsum(
        "skgt,stkd->skgd",
        weights.astype(jnp.bfloat16),
        value_rows,
        preferred_element_type=jnp.float32,
    ).reshape(local_pages, H * HD)
    split_numerator = jnp.einsum(
        "sqp,smc->pmqc",
        chosen_full,
        page_weighted.reshape(local_pages, mp_count, head_cols),
        precision=highest,
    )
    split_numerator = split_numerator.reshape(pool_count * mp_count, group_rows, head_cols)
    split_denominator = jnp.einsum("sqp,sh->pqh", chosen_full, page_total, precision=highest)
    split_denominator = jnp.broadcast_to(
        split_denominator[:, None], (pool_count, mp_count, group_rows, H)
    ).reshape(pool_count * mp_count, group_rows, H)
    column_numerator, column_denominator = (
        lax.psum_scatter(split_numerator, ("pool", "mp"), scatter_dimension=0, tiled=True),
        lax.psum_scatter(split_denominator, ("pool", "mp"), scatter_dimension=0, tiled=True),
    )
    own_columns = lax.dynamic_slice_in_dim(own_numerator, mp_index * head_cols, head_cols, 1)
    denominator_cols = lax.dynamic_slice_in_dim(
        jnp.repeat(column_denominator[0] + own_weight, HD, axis=1),
        mp_index * head_cols,
        head_cols,
        1,
    )
    attended = ((column_numerator[0] + own_columns) / denominator_cols).astype(jnp.bfloat16)
    projected = jnp.dot(attended, out_weight, preferred_element_type=jnp.float32)
    summed = lax.psum(projected, "mp")
    mixed_rows = (wide_rows + summed).astype(jnp.bfloat16)
    normed_two = rms_scale(mixed_rows.astype(jnp.float32), feed_gain, EPS_WIDE).astype(jnp.bfloat16)
    gate_values = jnp.dot(normed_two, gate_weight, preferred_element_type=jnp.float32)
    up_values = jnp.dot(normed_two, up_weight, preferred_element_type=jnp.float32)
    hidden = (jax.nn.silu(gate_values) * up_values).astype(jnp.bfloat16)
    feed_row = lax.psum_scatter(
        jnp.dot(hidden, down_weight, preferred_element_type=jnp.float32).astype(jnp.bfloat16),
        "mp",
        scatter_dimension=0,
        tiled=True,
    ).astype(jnp.float32)
    own_mixed = lax.dynamic_slice_in_dim(mixed_rows, mp_index, 1, 0)
    hidden_out = (own_mixed.astype(jnp.float32) + feed_row).astype(jnp.bfloat16)
    own_key = lax.dynamic_slice_in_dim(key_new.reshape(group_rows, KVH * HD), mp_index, 1, 0)
    own_value = lax.dynamic_slice_in_dim(value_new.reshape(group_rows, KVH * HD), mp_index, 1, 0)
    new_entries = jnp.concatenate([own_key, own_value], axis=1)
    return (hidden_out, new_entries)


def solution(mesh):
    in_specs = (
        P("pool", None),
        P(),
        P(None, "mp"),
        P(),
        P(),
        P(("pool", "mp"), None, None),
        P(),
        P(),
        P(),
        P("mp", None),
        P(),
        P(None, "mp"),
        P(None, "mp"),
        P("mp", None),
    )
    out_specs = (P(("pool", "mp"), None), P(("pool", "mp"), None))
    return jax.shard_map(shards, mesh=mesh, in_specs=in_specs, out_specs=out_specs, check_vma=False)
```

profile of v0, /device:TPU:0, one launch (start us, length us, event | category | flops | bytes accessed | tf_op | source)
XLA Modules:
  0.0 280.0 jit_solution(718425119413541022)
XLA Ops:
  7.8 0.7 reshape.228
  8.7 1.3 gather_fusion
  10.5 1.3 compare_reduce_fusion
  11.7 1.4 gather_fusion.1
  13.8 1.0 select_reduce_fusion
  16.8 70.7 %all-gather = bf16[32,480,4]{1,2,0:T(4,128)(2,1)S(1)} all-gather(bf16[1,480,4]{1,2,0:T(4,128)(2,1)S(1)} %fusion.4), channel_id=1, replica_groups=mesh['pool'=8,'mp'=4] {'pool','mp'}, dimensions={0}, use_global_device_ids=true | all-gather | bytes 126720 | tf_op jit(solution)/shard_map/all_gather | solution.py:67
  90.0 4.0 %fusion.55 = (bf16[16,128,320]{2,1,0:T(8,128)(2,1)}, bf16[16,128,320]{2,1,0:T(8,128)(2,1)S(1)}) fusion(bf16[16,128,640]{2,1,0:T(8,128)(2,1)} %param.19), kind=kLoop, calls=%fused_computation.108 | loop fusion | bytes 5242880 | tf_op jit(solution)/shard_map/slice | solution.py:112
  94.0 2.5 copy.61
  96.5 1.6 copy.59
  98.1 0.9 add_compare_fusion
  99.0 0.8 multiply_cosine_fusion
  99.8 1.2 fusion.5
  101.2 1.0 fusion.3
  102.2 1.8 fusion.57
  104.1 0.8 fusion.12
  106.2 0.9 constant_dynamic-slice_fusion.1
  108.9 37.3 %all-reduce.1 = f32[32,4,20]{2,1,0:T(4,128)S(1)} all-reduce(f32[32,4,20]{2,1,0:T(4,128)S(1)} %bitcast.83), channel_id=3, replica_groups=mesh['pool'=8,'mp'=4] {'pool','mp'}, use_global_device_ids=true, to_apply=%region_8.9.clone | all-reduce | flops 2560 | bytes 20480
  147.7 77.8 %all-reduce.5.cloned.1.call-done = f32[32,4,320]{2,1,0:T(4,128)} async-done(((f32[32,4,320]{2,1,0:T(4,128)}), f32[32,4,320]{2,1,0:T(4,128)}) %all-reduce.5.cloned.1.call-update) | async-done | bytes 163856
  225.5 1.7 fusion.41
  227.2 19.9 %psum.7 = f32[4,2048]{1,0:T(4,128)S(1)} all-reduce(f32[4,2048]{1,0:T(4,128)S(1)} %fusion.41), channel_id=1, replica_groups=mesh['pool'=8,'mp'=4] {'mp'}, use_global_device_ids=true, to_apply=%region_9.10 | all-reduce | flops 8192 | bytes 65536 | tf_op jit(solution)/shard_map/psum | solution.py:157
  247.2 3.3 %fusion.52 = f32[4,1280]{1,0:T(4,128)S(1)} fusion(bf16[2048,1280]{1,0:T(8,128)(2,1)} %param.25, bf16[4,2048]{1,0:T(4,128)(2,1)S(1)} %get-tuple-element.3, f32[2048]{0:T(1024)S(1)} %copy-done.8, f32[4]{0:T(128)S(1)} %add_rsqrt_fusion.2), kind=kOutput, calls=%fused_computation.107 | convolution fusion | flops 21004288 | bytes 5287952 | tf_op jit(solution)/shard_map/dot_general | solution.py:160
  250.5 5.8 %convolution_convert_fusion = bf16[4,2048]{1,0:T(4,128)(2,1)S(1)} fusion(bf16[1280,2048]{1,0:T(8,128)(2,1)} %param.27, bf16[2048,1280]{1,0:T(8,128)(2,1)} %param.26, f32[4,1280]{1,0:T(4,128)S(1)} %fusion.52, bf16[4,2048]{1,0:T(4,128)(2,1)S(1)} %get-tuple-element.3, f32[2048]{0:T(1024)S(1)} %copy-done.8, f32[4]{0:T(128)S(1)} %add_rsqrt_fusion.2), kind=kOutput, calls=%fused_computation.3 | convolution fusion | flops 42014720 | bytes 10547216 | tf_op jit(solution)/shard_map/dot_general | solution.py:164
  256.3 15.5 %all-reduce.2 = bf16[4,2048]{1,0:T(4,128)(2,1)S(1)} all-reduce(bf16[4,2048]{1,0:T(4,128)(2,1)S(1)} %convolution_convert_fusion), channel_id=4, replica_groups=mesh['pool'=8,'mp'=4] {'mp'}, use_global_device_ids=true, to_apply=%region_11.12.clone | all-reduce | flops 8192 | bytes 32768
  271.9 1.2 fusion.37
  (86 shorter events, 11.2 us)
Async XLA Ops:
  7.2 9.0 %copy-start = (bf16[2048,480]{0,1:T(8,128)(2,1)S(1)}, bf16[2048,480]{0,1:T(8,128)(2,1)}, u32[]{:S(2)}) copy-start(bf16[2048,480]{0,1:T(8,128)(2,1)} %param.16) | copy-start | bytes 5898244
  7.2 8.2 %copy-start.4 = (bf16[4,2048]{1,0:T(4,128)(2,1)S(1)}, bf16[4,2048]{1,0:T(4,128)(2,1)}, u32[]{:S(2)}) copy-start(bf16[4,2048]{1,0:T(4,128)(2,1)} %param.14) | copy-start | bytes 49156
  7.2 9.0 %copy-start.9 = (f32[2048]{0:T(1024)S(1)}, f32[2048]{0:T(1024)}, u32[]{:S(2)}) copy-start(f32[2048]{0:T(1024)} %param.15) | copy-start | bytes 24580
  7.2 218.3 %all-reduce.5.cloned.1.call-start = ((), (), s32[]{:S(2)}) async-start(), calls=%async_computation | async-start | bytes 393216
  13.2 3.6 %copy-start.6 = (s32[4,8]{1,0:T(4,128)}, s32[4,8]{1,0:T(4,128)S(1)}, u32[]{:S(2)}) copy-start(s32[4,8]{1,0:T(4,128)S(1)} %reshape.259) | copy-start | bytes 388
  87.8 0.6 copy-start.3
  88.6 0.8 copy-start.2
  98.1 5.9 %copy-start.1 = (bf16[16,128,320]{1,2,0:T(8,128)(2,1)S(1)}, bf16[16,128,320]{1,2,0:T(8,128)(2,1)}, u32[]{:S(2)}) copy-start(bf16[16,128,320]{1,2,0:T(8,128)(2,1)} %copy.61) | copy-start | bytes 3932164
  101.2 3.9 %copy-start.5 = (pred[16,4,8]{0,2,1:T(8,128)(4,1)S(1)}, pred[16,4,8]{0,2,1:T(8,128)(4,1)}, u32[]{:S(2)}) copy-start(pred[16,4,8]{0,2,1:T(8,128)(4,1)} %copy.58) | copy-start | bytes 1540
  102.2 3.8 %copy-start.7 = (s32[4,8]{1,0:T(4,128)S(1)}, s32[4,8]{1,0:T(4,128)}, u32[]{:S(2)}) copy-start(s32[4,8]{1,0:T(4,128)} %copy-done.6) | copy-start | bytes 388
  102.2 5.0 %copy-start.10 = (f32[32]{0:T(128)S(1)}, f32[32]{0:T(128)}, u32[]{:S(2)}) copy-start(f32[32]{0:T(128)} %multiply_power_fusion) | copy-start | bytes 388
  102.2 5.4 %copy-start.11 = (f32[64]{0:T(128)S(1)}, f32[64]{0:T(128)}, u32[]{:S(2)}) copy-start(f32[64]{0:T(128)} %param.18) | copy-start | bytes 772
  104.1 42.2 %copy-start.12 = (u32[32]{0:T(128)S(1)}, u32[32]{0:T(128)}, u32[]{:S(2)}) copy-start(u32[32]{0:T(128)} %constant.77) | copy-start | bytes 388
  105.0 142.2 %copy-start.8 = (f32[2048]{0:T(1024)S(1)}, f32[2048]{0:T(1024)}, u32[]{:S(2)}) copy-start(f32[2048]{0:T(1024)} %param.24) | copy-start | bytes 24580
Sparse Core Ops, SparseCore 0:
  106.1 119.3 all-reduce.4
where the time goes:
time: 281 us; the launch traced here: 280 us
  blocking collectives  143 us (51%)
  waiting for transfers between devices  77.8 us (28%)
  local copies, waits for them, and re-layouts  18 us (6%)
  matrix products  15.6 us (6%)
  between operations  14.3 us (5%)
  other arithmetic  10.8 us (4%)
    unnamed x2, waiting for transfers between devices  77.8 us
    all_gather x1, blocking collectives, shards(): gathered = lax.all_gather(packed_part, ('pool', 'mp'), axis=1, tiled=True)  70.7 us
    unnamed x2, blocking collectives  52.9 us
    psum x1, blocking collectives, shards(): summed = lax.psum(projected, 'mp')  19.9 us
    slice x2, local copies, waits for them, and re-layouts, shards(): value_rows = page_cache[..., KVH * HD:].reshape(local_pages, PAGE, KVH, HD)  6.5 us
    dot_general x1, matrix products, shards(): jnp.dot(hidden, down_weight, preferred_element_type=jnp.float32)  5.83 us
  transfers between devices with their start and end apart: 1, of which 1 were waited for; matrix products, arithmetic and copies ran while one was open for 2% of the time, Pallas kernels for 0%

commit v1 on v0

--- a/solution.py
+++ b/solution.py
@@ -64,8 +64,19 @@
     packed_part = jnp.dot(normed, project_in, preferred_element_type=jnp.float32).astype(
         jnp.bfloat16
     )
-    gathered = lax.all_gather(packed_part, ("pool", "mp"), axis=1, tiled=True)
-    packed = gathered.reshape(group_rows, pool_count, (H + 2 * KVH) * HD)
+    device_count = pool_count * mp_count
+    gathered = lax.all_to_all(
+        jnp.broadcast_to(packed_part[None], (device_count,) + packed_part.shape),
+        ("pool", "mp"),
+        0,
+        0,
+        tiled=True,
+    )
+    packed = (
+        gathered.reshape(pool_count, mp_count, group_rows, -1)
+        .transpose(2, 0, 1, 3)
+        .reshape(group_rows, pool_count, (H + 2 * KVH) * HD)
+    )
     request_ids = row_order.reshape(pool_count, group_rows).T
     row_lengths = lengths[request_ids]
     row_tables = page_table[request_ids]
@@ -141,10 +152,19 @@
     split_denominator = jnp.broadcast_to(
         split_denominator[:, None], (pool_count, mp_count, group_rows, H)
     ).reshape(pool_count * mp_count, group_rows, H)
-    column_numerator, column_denominator = (
-        lax.psum_scatter(split_numerator, ("pool", "mp"), scatter_dimension=0, tiled=True),
-        lax.psum_scatter(split_denominator, ("pool", "mp"), scatter_dimension=0, tiled=True),
-    )
+    denominator_high = split_denominator.astype(jnp.bfloat16)
+    denominator_low = (split_denominator - denominator_high.astype(jnp.float32)).astype(
+        jnp.bfloat16
+    )
+    sums = jnp.concatenate(
+        [split_numerator.astype(jnp.bfloat16), denominator_high, denominator_low], axis=2
+    )
+    sums = lax.all_to_all(sums, ("pool", "mp"), 0, 0, tiled=True).astype(jnp.float32)
+    sums = jnp.sum(sums, axis=0)
+    column_numerator = sums[None, :, :head_cols]
+    column_denominator = (
+        sums[:, head_cols : head_cols + H] + sums[:, head_cols + H : head_cols + 2 * H]
+    )[None]
     own_columns = lax.dynamic_slice_in_dim(own_numerator, mp_index * head_cols, head_cols, 1)
     denominator_cols = lax.dynamic_slice_in_dim(
         jnp.repeat(column_denominator[0] + own_weight, HD, axis=1),
@@ -154,18 +174,23 @@
     )
     attended = ((column_numerator[0] + own_columns) / denominator_cols).astype(jnp.bfloat16)
     projected = jnp.dot(attended, out_weight, preferred_element_type=jnp.float32)
-    summed = lax.psum(projected, "mp")
+    sent = projected.astype(jnp.bfloat16)
+    summed = projected
+    for step in range(1, mp_count):
+        ring = [(i, (i + step) % mp_count) for i in range(mp_count)]
+        summed = summed + lax.ppermute(sent, "mp", ring).astype(jnp.float32)
     mixed_rows = (wide_rows + summed).astype(jnp.bfloat16)
     normed_two = rms_scale(mixed_rows.astype(jnp.float32), feed_gain, EPS_WIDE).astype(jnp.bfloat16)
     gate_values = jnp.dot(normed_two, gate_weight, preferred_element_type=jnp.float32)
     up_values = jnp.dot(normed_two, up_weight, preferred_element_type=jnp.float32)
     hidden = (jax.nn.silu(gate_values) * up_values).astype(jnp.bfloat16)
-    feed_row = lax.psum_scatter(
-        jnp.dot(hidden, down_weight, preferred_element_type=jnp.float32).astype(jnp.bfloat16),
-        "mp",
-        scatter_dimension=0,
-        tiled=True,
-    ).astype(jnp.float32)
+    feed_part = jnp.dot(hidden, down_weight, preferred_element_type=jnp.float32)
+    feed_sent = feed_part.astype(jnp.bfloat16)
+    feed_row = lax.dynamic_slice_in_dim(feed_part, mp_index, 1, 0)
+    for step in range(1, mp_count):
+        ring = [(i, (i + step) % mp_count) for i in range(mp_count)]
+        row = lax.dynamic_slice_in_dim(feed_sent, (mp_index + step) % mp_count, 1, 0)
+        feed_row = feed_row + lax.ppermute(row, "mp", ring).astype(jnp.float32)
     own_mixed = lax.dynamic_slice_in_dim(mixed_rows, mp_index, 1, 0)
     hidden_out = (own_mixed.astype(jnp.float32) + feed_row).astype(jnp.bfloat16)
     own_key = lax.dynamic_slice_in_dim(key_new.reshape(group_rows, KVH * HD), mp_index, 1, 0)

time: 281 us -> 83.5 us (0.30)
  blocking collectives: 143 us -> 0 us
  waiting for transfers between devices: 77.8 us -> 15.3 us
  starting transfers between devices: 0.04 us -> 19.5 us
  between operations: 14.3 us -> 0.91 us
  other arithmetic: 10.8 us -> 14.9 us
    unnamed x2 -> x0, waiting for transfers between devices: 77.8 us -> none
    all_gather x1 -> x0, blocking collectives: 70.7 us -> none  [shards(): gathered = lax.all_gather(packed_part, ('pool', 'mp'), axis=1, tiled=True)]
    unnamed x2 -> x0, blocking collectives: 52.9 us -> none
    psum x1 -> x0, blocking collectives: 19.9 us -> none  [shards(): summed = lax.psum(projected, 'mp')]
    all_to_all x0 -> x2, starting transfers between devices: none -> 13.2 us  [the longest x1 7.43 us: shards(): lax.all_to_all(jnp.broadcast_to(packed_part[None], (device_count,) + pack...]
    ppermute x0 -> x6, waiting for transfers between devices: none -> 8.3 us  [the longest x3 4.4 us: shards(): summed = summed + lax.ppermute(sent, 'mp', ring).astype(jnp.float32)]
    all_to_all x0 -> x2, waiting for transfers between devices: none -> 7.03 us  [the longest x1 7.02 us: shards(): lax.all_to_all(sums, ('pool', 'mp'), 0, 0, tiled=True).astype(jnp.float32)]
    ppermute x0 -> x6, starting transfers between devices: none -> 6.3 us  [the longest x3 3.87 us: shards(): feed_row = feed_row + lax.ppermute(row, 'mp', ring).astype(jnp.float32)]
  transfers between devices with their start and end apart: 1 -> 8, of which waited for: 1 -> 6; matrix products, arithmetic and copies ran while one was open for 2% -> 19% of each run, Pallas kernels for 0% -> 0%
where the time goes in v1:
time: 83.5 us; the launch traced here: 82.7 us
  starting transfers between devices  19.5 us (23%)
  matrix products  16.2 us (19%)
  local copies, waits for them, and re-layouts  16 us (19%)
  waiting for transfers between devices  15.3 us (18%)
  other arithmetic  14.9 us (18%)
  between operations  0.91 us (1%)
    all_to_all x1, starting transfers between devices, shards(): lax.all_to_all(jnp.broadcast_to(packed_part[None], (device_count,) + pack...  7.43 us
    all_to_all x1, waiting for transfers between devices, shards(): lax.all_to_all(sums, ('pool', 'mp'), 0, 0, tiled=True).astype(jnp.float32)  7.02 us
    slice x2, local copies, waits for them, and re-layouts, shards(): value_rows = page_cache[..., KVH * HD:].reshape(local_pages, PAGE, KVH, HD)  6.5 us
    dot_general x1, matrix products, shards(): feed_part = jnp.dot(hidden, down_weight, preferred_element_type=jnp.float32)  5.83 us
    all_to_all x1, starting transfers between devices, shards(): lax.all_to_all(sums, ('pool', 'mp'), 0, 0, tiled=True).astype(jnp.float32)  5.76 us
    ppermute x3, waiting for transfers between devices, shards(): summed = summed + lax.ppermute(sent, 'mp', ring).astype(jnp.float32)  4.4 us
    ppermute x3, waiting for transfers between devices, shards(): feed_row = feed_row + lax.ppermute(row, 'mp', ring).astype(jnp.float32)  3.89 us
    ppermute x3, starting transfers between devices, shards(): feed_row = feed_row + lax.ppermute(row, 'mp', ring).astype(jnp.float32)  3.87 us
  transfers between devices with their start and end apart: 8, of which 6 were waited for; matrix products, arithmetic and copies ran while one was open for 19% of the time, Pallas kernels for 0%

profile of v1, /device:TPU:0, one launch (start us, length us, event | category | flops | bytes accessed | tf_op | source)
XLA Modules:
  0.0 82.7 jit_solution(3051335927334892461)
XLA Ops:
  0.7 1.0 %fusion.20 = f32[4]{0:T(128)S(1)} fusion(bf16[4,2048]{1,0:T(4,128)(2,1)} %param.14), kind=kLoop, calls=%fused_computation.46 | loop fusion | flops 24572 | bytes 16400 | tf_op jit(solution)/shard_map/reduce_sum | solution.py:18
  2.2 1.3 %convolution_convert_fusion.1 = bf16[4,480]{1,0:T(4,128)(2,1)S(1)} fusion(bf16[2048,480]{0,1:T(8,128)(2,1)S(1)} %copy-done, bf16[4,2048]{1,0:T(4,128)(2,1)} %param.14, f32[2048]{0:T(1024)} %param.15, f32[4]{0:T(128)S(1)} %add_rsqrt_fusion.3), kind=kOutput, calls=%fused_computation.12 | convolution fusion | flops 7899008 | bytes 1994512 | tf_op jit(solution)/shard_map/dot_general | solution.py:64
  4.3 7.4 %all-to-all-start = ((bf16[32,4,480]{2,1,0:T(4,128)(2,1)}), bf16[32,4,480]{2,1,0:T(4,128)(2,1)}, u32[]{:S(2)}, u32[]{:S(2)}) async-start(bf16[32,4,480]{2,1,0:T(4,128)(2,1)} %broadcast_in_dim.46), calls=%async_computation | async-start | bytes 262144 | tf_op jit(solution)/shard_map/all_to_all | solution.py:68
  13.1 1.3 %compare_reduce_fusion = pred[16,4,8]{2,1,0:T(4,128)(4,1)S(1)} fusion(s32[4,8,64]{2,1,0:T(8,128)S(1)} %bitcast.65, s32[16]{0:T(128)S(1)} %iota_add_fusion), kind=kLoop, calls=%fused_computation.15 | loop fusion | flops 65024 | bytes 8768 | tf_op jit(solution)/shard_map/reduce_or | solution.py:114
  15.7 4.0 %fusion.52 = (bf16[16,128,320]{2,1,0:T(8,128)(2,1)}, bf16[16,128,320]{2,1,0:T(8,128)(2,1)S(1)}) fusion(bf16[16,128,640]{2,1,0:T(8,128)(2,1)} %param.19), kind=kLoop, calls=%fused_computation.110 | loop fusion | bytes 5242880 | tf_op jit(solution)/shard_map/slice | solution.py:123
  21.1 2.5 %copy.60 = bf16[16,128,320]{1,2,0:T(8,128)(2,1)} copy(bf16[16,128,320]{2,1,0:T(8,128)(2,1)} %get-tuple-element.4) | data formatting | bytes 2621440 | tf_op jit(solution)/shard_map/slice | solution.py:123
  23.7 1.6 %copy.58 = bf16[16,128,320]{1,2,0:T(8,128)(2,1)} copy(bf16[16,128,320]{2,1,0:T(8,128)(2,1)S(1)} %get-tuple-element.5) | data formatting | bytes 2621440 | tf_op jit(solution)/shard_map/slice | solution.py:122
  26.0 1.0 %copy.54 = bf16[4,8,4,480]{3,2,1,0:T(4,128)(2,1)S(1)} copy(bf16[4,8,4,480]{3,0,2,1:T(4,128)(2,1)} %bitcast.4) | data formatting | bytes 245760 | tf_op jit(solution)/shard_map/transpose | solution.py:77
  32.1 1.8 %fusion.54 = (f32[16,5,4]{2,1,0:T(8,128)S(1)}, bf16[16,5,4,128]{3,2,1,0:T(4,128)(2,1)S(1)}) fusion(bf16[16,128,5,64]{1,3,2,0:T(8,128)(2,1)} %bitcast.60, bf16[16,5,4,64]{3,0,2,1:T(8,128)(2,1)S(1)} %bitcast.63, pred[16,128]{1,0:T(8,128)(4,1)S(1)} %add_compare_fusion), kind=kOutput, calls=%fused_computation.112 | convolution fusion | flops 5406400 | bytes 1436928 | tf_op jit(solution)/shard_map/skgd,stkd->skgt/dot_general | solution.py:125
  37.5 0.8 fusion.27
  40.3 1.5 %pad_maximum_fusion = bf16[32,4,360]{2,1,0:T(4,128)(2,1)} fusion(bf16[32,4,20]{2,1,0:T(4,128)(2,1)} %fusion.15, bf16[32,4,20]{2,1,0:T(4,128)(2,1)} %bitcast_convert_fusion, bf16[32,4,320]{2,1,0:T(4,128)(2,1)S(1)} %bitcast.61), kind=kLoop, calls=%fused_computation.28 | loop fusion | flops 276480 | bytes 184320 | tf_op jit(solution)/shard_map/concatenate | solution.py:159
  41.8 5.8 %all-to-all-start.1 = ((bf16[32,4,360]{2,1,0:T(4,128)(2,1)}), bf16[32,4,360]{2,1,0:T(4,128)(2,1)S(1)}, u32[]{:S(2)}, u32[]{:S(2)}) async-start(bf16[32,4,360]{2,1,0:T(4,128)(2,1)} %pad_maximum_fusion), calls=%async_computation.1 | async-start | bytes 196608 | tf_op jit(solution)/shard_map/all_to_all | solution.py:162
  48.5 7.0 %all-to-all-done.1 = bf16[32,4,360]{2,1,0:T(4,128)(2,1)S(1)} async-done(((bf16[32,4,360]{2,1,0:T(4,128)(2,1)}), bf16[32,4,360]{2,1,0:T(4,128)(2,1)S(1)}, u32[]{:S(2)}, u32[]{:S(2)}) %all-to-all-start.1) | async-done | bytes 92192 | tf_op jit(solution)/shard_map/all_to_all | solution.py:162
  55.8 1.6 %fusion.55 = (bf16[4,2048]{1,0:T(4,128)(2,1)S(1)}, f32[4,2048]{1,0:T(4,128)S(1)}) fusion(bf16[320,2048]{1,0:T(8,128)(2,1)} %param.23, f32[4,1280]{1,0:T(4,128)S(1)} %reshape.247, s32[]{:T(128)S(6)} %select_n.63, f32[4,1280]{1,0:T(4,128)S(1)} %reshape.245, f32[4,360]{1,0:T(4,128)S(1)} %convert_reduce_fusion), kind=kOutput, calls=%fused_computation.113 | convolution fusion | flops 5254912 | bytes 1378308 | tf_op jit(solution)/shard_map/dot_general | solution.py:176
  57.5 1.0 %collective-permute-start.2 = (bf16[4,2048]{1,0:T(4,128)(2,1)S(1)}, bf16[4,2048]{1,0:T(4,128)(2,1)S(1)}, u32[]{:S(2)}, u32[]{:S(2)}) collective-permute-start(bf16[4,2048]{1,0:T(4,128)(2,1)S(1)} %get-tuple-element.24), channel_id=1, source_target_pairs={{0,3},{1,0},{2,1},{3,2},{4,7},{5,4},{6,5},{7,6},{8,11},{9,8},{10,9... | collective-permute-start | bytes 49160 | tf_op jit(solution)/shard_map/ppermute | solution.py:181
  58.8 1.1 %collective-permute-start = (bf16[4,2048]{1,0:T(4,128)(2,1)S(1)}, bf16[4,2048]{1,0:T(4,128)(2,1)S(1)}, u32[]{:S(2)}, u32[]{:S(2)}) collective-permute-start(bf16[4,2048]{1,0:T(4,128)(2,1)S(1)} %get-tuple-element.24), channel_id=1, source_target_pairs={{0,1},{1,2},{2,3},{3,0},{4,5},{5,6},{6,7},{7,4},{8,9},{9,10},{10,1... | collective-permute-start | bytes 49160 | tf_op jit(solution)/shard_map/ppermute | solution.py:181
  59.9 1.3 %collective-permute-done.2 = bf16[4,2048]{1,0:T(4,128)(2,1)S(1)} collective-permute-done((bf16[4,2048]{1,0:T(4,128)(2,1)S(1)}, bf16[4,2048]{1,0:T(4,128)(2,1)S(1)}, u32[]{:S(2)}, u32[]{:S(2)}) %collective-permute-start.2) | collective-permute-done | bytes 16416 | tf_op jit(solution)/shard_map/ppermute | solution.py:181
  61.2 1.9 %collective-permute-done.1 = bf16[4,2048]{1,0:T(4,128)(2,1)S(1)} collective-permute-done((bf16[4,2048]{1,0:T(4,128)(2,1)S(1)}, bf16[4,2048]{1,0:T(4,128)(2,1)S(1)}, u32[]{:S(2)}, u32[]{:S(2)}) %collective-permute-start.1) | collective-permute-done | bytes 16416 | tf_op jit(solution)/shard_map/ppermute | solution.py:181
  63.2 1.2 %collective-permute-done = bf16[4,2048]{1,0:T(4,128)(2,1)S(1)} collective-permute-done((bf16[4,2048]{1,0:T(4,128)(2,1)S(1)}, bf16[4,2048]{1,0:T(4,128)(2,1)S(1)}, u32[]{:S(2)}, u32[]{:S(2)}) %collective-permute-start) | collective-permute-done | bytes 16416 | tf_op jit(solution)/shard_map/ppermute | solution.py:181
  64.5 3.3 %fusion.49 = f32[4,1280]{1,0:T(4,128)S(1)} fusion(bf16[2048,1280]{1,0:T(8,128)(2,1)} %param.25, bf16[4,2048]{1,0:T(4,128)(2,1)S(1)} %get-tuple-element.3, f32[2048]{0:T(1024)S(1)} %copy-done.5, f32[4]{0:T(128)S(1)} %add_rsqrt_fusion.2), kind=kOutput, calls=%fused_computation.109 | convolution fusion | flops 21004288 | bytes 5287952 | tf_op jit(solution)/shard_map/dot_general | solution.py:184
  67.8 5.8 %fusion.56 = (bf16[4,2048]{1,0:T(4,128)(2,1)S(1)}, f32[4,2048]{1,0:T(4,128)S(1)}) fusion(bf16[1280,2048]{1,0:T(8,128)(2,1)} %param.27, bf16[2048,1280]{1,0:T(8,128)(2,1)} %param.26, f32[4,1280]{1,0:T(4,128)S(1)} %fusion.49, bf16[4,2048]{1,0:T(4,128)(2,1)S(1)} %get-tuple-element.3, f32[2048]{0:T(1024)S(1)} %copy-done.5, f32[4]{0:T(128)S(1)} %add_rsqrt_fusion.2), kind=kOutput, calls=%fused_computation.114 | convolution fusion | flops 42014720 | bytes 10579984 | tf_op jit(solution)/shard_map/dot_general | solution.py:187
  73.8 3.8 %collective-permute-start.5 = (bf16[1,2048]{1,0:T(2,128)(2,1)S(1)}, bf16[1,2048]{1,0:T(2,128)(2,1)S(1)}, u32[]{:S(2)}, u32[]{:S(2)}) collective-permute-start(bf16[1,2048]{1,0:T(2,128)(2,1)S(1)} %get-tuple-element.11), channel_id=1, source_target_pairs={{0,3},{1,0},{2,1},{3,2},{4,7},{5,4},{6,5},{7,6},{8,11},{9,8},{10,9... | collective-permute-start | bytes 12296 | tf_op jit(solution)/shard_map/ppermute | solution.py:193
  78.2 1.0 %collective-permute-done.3 = bf16[1,2048]{1,0:T(2,128)(2,1)S(1)} collective-permute-done((bf16[1,2048]{1,0:T(2,128)(2,1)S(1)}, bf16[1,2048]{1,0:T(2,128)(2,1)S(1)}, u32[]{:S(2)}, u32[]{:S(2)}) %collective-permute-start.3) | collective-permute-done | bytes 4128 | tf_op jit(solution)/shard_map/ppermute | solution.py:193
  79.2 2.9 %collective-permute-done.4 = bf16[1,2048]{1,0:T(2,128)(2,1)S(1)} collective-permute-done((bf16[1,2048]{1,0:T(2,128)(2,1)S(1)}, bf16[1,2048]{1,0:T(2,128)(2,1)S(1)}, u32[]{:S(2)}, u32[]{:S(2)}) %collective-permute-start.4) | collective-permute-done | bytes 4128 | tf_op jit(solution)/shard_map/ppermute | solution.py:193
  (98 shorter events, 19.8 us)
Async XLA Ops:
  0.6 1.6 %copy-start = (bf16[2048,480]{0,1:T(8,128)(2,1)S(1)}, bf16[2048,480]{0,1:T(8,128)(2,1)}, u32[]{:S(2)}) copy-start(bf16[2048,480]{0,1:T(8,128)(2,1)} %param.16) | copy-start | bytes 5898244
  0.6 11.1 %copy-start.11 = (s32[32]{0:T(128)S(1)}, s32[32]{0:T(128)}, u32[]{:S(2)}) copy-start(s32[32]{0:T(128)} %param.22) | copy-start | bytes 388
  0.7 11.4 %copy-start.3 = (s32[32,64]{1,0:T(8,128)S(1)}, s32[32,64]{1,0:T(8,128)}, u32[]{:S(2)}) copy-start(s32[32,64]{1,0:T(8,128)} %param.20) | copy-start | bytes 24580
  0.7 13.7 %copy-start.1 = (s32[32]{0:T(128)S(1)}, s32[32]{0:T(128)}, u32[]{:S(2)}) copy-start(s32[32]{0:T(128)} %param.21) | copy-start | bytes 388
  4.3 21.7 %all-to-all-start = ((bf16[32,4,480]{2,1,0:T(4,128)(2,1)}), bf16[32,4,480]{2,1,0:T(4,128)(2,1)}, u32[]{:S(2)}, u32[]{:S(2)}) async-start(bf16[32,4,480]{2,1,0:T(4,128)(2,1)} %broadcast_in_dim.46), calls=%async_computation | async-start | bytes 262144 | tf_op jit(solution)/shard_map/all_to_all | solution.py:68
  11.7 7.9 %copy-start.10 = (f32[32]{0:T(128)}, f32[32]{0:T(128)S(1)}, u32[]{:S(2)}) copy-start(f32[32]{0:T(128)S(1)} %multiply_power_fusion) | copy-start | bytes 388
  23.6 1.6 %copy-start.6 = (f32[4,8]{1,0:T(4,128)S(1)}, f32[4,8]{1,0:T(4,128)}, u32[]{:S(2)}) copy-start(f32[4,8]{1,0:T(4,128)} %convert_element_type.116) | copy-start | bytes 388
  23.7 5.1 %copy-start.7 = (f32[4,32]{1,0:T(4,128)S(1)}, f32[4,32]{1,0:T(4,128)}, u32[]{:S(2)}) copy-start(f32[4,32]{1,0:T(4,128)} %get-tuple-element.20) | copy-start | bytes 1540
  25.2 5.5 %copy-start.12 = (f32[64]{0:T(128)S(1)}, f32[64]{0:T(128)}, u32[]{:S(2)}) copy-start(f32[64]{0:T(128)} %param.17) | copy-start | bytes 772
  30.9 8.2 %copy-start.2 = (bf16[16,128,320]{1,2,0:T(8,128)(2,1)S(1)}, bf16[16,128,320]{1,2,0:T(8,128)(2,1)}, u32[]{:S(2)}) copy-start(bf16[16,128,320]{1,2,0:T(8,128)(2,1)} %copy.60) | copy-start | bytes 3932164
  39.1 25.3 %copy-start.4 = (bf16[4,2048]{1,0:T(4,128)(2,1)S(1)}, bf16[4,2048]{1,0:T(4,128)(2,1)}, u32[]{:S(2)}) copy-start(bf16[4,2048]{1,0:T(4,128)(2,1)} %param.14) | copy-start | bytes 49156
  39.1 25.4 %copy-start.5 = (f32[2048]{0:T(1024)S(1)}, f32[2048]{0:T(1024)}, u32[]{:S(2)}) copy-start(f32[2048]{0:T(1024)} %param.24) | copy-start | bytes 24580
  39.8 20.1 %copy-start.8 = (bf16[4,320]{1,0:T(4,128)(2,1)S(1)}, bf16[4,320]{1,0:T(4,128)(2,1)}, u32[]{:S(2)}) copy-start(bf16[4,320]{1,0:T(4,128)(2,1)} %convert_element_type.145) | copy-start | bytes 7684
  39.8 20.1 %copy-start.9 = (bf16[4,320]{1,0:T(4,128)(2,1)S(1)}, bf16[4,320]{1,0:T(4,128)(2,1)}, u32[]{:S(2)}) copy-start(bf16[4,320]{1,0:T(4,128)(2,1)} %get-tuple-element.13) | copy-start | bytes 7684
  41.8 13.7 %all-to-all-start.1 = ((bf16[32,4,360]{2,1,0:T(4,128)(2,1)}), bf16[32,4,360]{2,1,0:T(4,128)(2,1)S(1)}, u32[]{:S(2)}, u32[]{:S(2)}) async-start(bf16[32,4,360]{2,1,0:T(4,128)(2,1)} %pad_maximum_fusion), calls=%async_computation.1 | async-start | bytes 196608 | tf_op jit(solution)/shard_map/all_to_all | solution.py:162
  57.5 3.8 %collective-permute-start.2 = (bf16[4,2048]{1,0:T(4,128)(2,1)S(1)}, bf16[4,2048]{1,0:T(4,128)(2,1)S(1)}, u32[]{:S(2)}, u32[]{:S(2)}) collective-permute-start(bf16[4,2048]{1,0:T(4,128)(2,1)S(1)} %get-tuple-element.24), channel_id=1, source_target_pairs={{0,3},{1,0},{2,1},{3,2},{4,7},{5,4},{6,5},{7,6},{8,11},{9,8},{10,9... | collective-permute-start | bytes 49160 | tf_op jit(solution)/shard_map/ppermute | solution.py:181
  58.5 4.6 %collective-permute-start.1 = (bf16[4,2048]{1,0:T(4,128)(2,1)S(1)}, bf16[4,2048]{1,0:T(4,128)(2,1)S(1)}, u32[]{:S(2)}, u32[]{:S(2)}) collective-permute-start(bf16[4,2048]{1,0:T(4,128)(2,1)S(1)} %get-tuple-element.24), channel_id=1, source_target_pairs={{0,2},{1,3},{2,0},{3,1},{4,6},{5,7},{6,4},{7,5},{8,10},{9,11},{10,... | collective-permute-start | bytes 49160 | tf_op jit(solution)/shard_map/ppermute | solution.py:181
  58.8 5.5 %collective-permute-start = (bf16[4,2048]{1,0:T(4,128)(2,1)S(1)}, bf16[4,2048]{1,0:T(4,128)(2,1)S(1)}, u32[]{:S(2)}, u32[]{:S(2)}) collective-permute-start(bf16[4,2048]{1,0:T(4,128)(2,1)S(1)} %get-tuple-element.24), channel_id=1, source_target_pairs={{0,1},{1,2},{2,3},{3,0},{4,5},{5,6},{6,7},{7,4},{8,9},{9,10},{10,1... | collective-permute-start | bytes 49160 | tf_op jit(solution)/shard_map/ppermute | solution.py:181
  73.7 5.5 %collective-permute-start.3 = (bf16[1,2048]{1,0:T(2,128)(2,1)S(1)}, bf16[1,2048]{1,0:T(2,128)(2,1)S(1)}, u32[]{:S(2)}, u32[]{:S(2)}) collective-permute-start(bf16[1,2048]{1,0:T(2,128)(2,1)S(1)} %get-tuple-element.10), channel_id=1, source_target_pairs={{0,1},{1,2},{2,3},{3,0},{4,5},{5,6},{6,7},{7,4},{8,9},{9,10},{10,1... | collective-permute-start | bytes 12296 | tf_op jit(solution)/shard_map/ppermute | solution.py:193
  73.8 5.4 %collective-permute-start.5 = (bf16[1,2048]{1,0:T(2,128)(2,1)S(1)}, bf16[1,2048]{1,0:T(2,128)(2,1)S(1)}, u32[]{:S(2)}, u32[]{:S(2)}) collective-permute-start(bf16[1,2048]{1,0:T(2,128)(2,1)S(1)} %get-tuple-element.11), channel_id=1, source_target_pairs={{0,3},{1,0},{2,1},{3,2},{4,7},{5,4},{6,5},{7,6},{8,11},{9,8},{10,9... | collective-permute-start | bytes 12296 | tf_op jit(solution)/shard_map/ppermute | solution.py:193
  77.6 4.5 %collective-permute-start.4 = (bf16[1,2048]{1,0:T(2,128)(2,1)S(1)}, bf16[1,2048]{1,0:T(2,128)(2,1)S(1)}, u32[]{:S(2)}, u32[]{:S(2)}) collective-permute-start(bf16[1,2048]{1,0:T(2,128)(2,1)S(1)} %get-tuple-element.12), channel_id=1, source_target_pairs={{0,2},{1,3},{2,0},{3,1},{4,6},{5,7},{6,4},{7,5},{8,10},{9,11},{10,... | collective-permute-start | bytes 12296 | tf_op jit(solution)/shard_map/ppermute | solution.py:193

commit v2 on v0

v2 whole, which is shorter than its diff:
```python
import jax
import jax.numpy as jnp
import numpy as np
from jax import lax
from jax.experimental import pallas as pl
from jax.experimental.pallas import tpu as pltpu
from jax.sharding import PartitionSpec as P

H = 20
KVH = 5
HD = 64
GROUPS = H // KVH
PAGE = 128
LANES = 128
KEYS = KVH * HD
ENTRY = 2 * KEYS
EPS_WIDE = 1e-05
EPS_HEAD = 1e-06
MIB = 1 << 20

BF16 = jnp.bfloat16
F32 = jnp.float32
I32 = jnp.int32


def up_to(value, step):
    return (value + step - 1) // step * step


def dot(left, right):
    return jnp.dot(left, right, preferred_element_type=F32)


def dot_rows(left, right):
    return lax.dot_general(left, right, (((1,), (1,)), ((), ())), preferred_element_type=F32)


def two_halves(values):
    high = values.astype(BF16)
    return high, (values - high.astype(F32)).astype(BF16)


def lane_iota(shape):
    return lax.broadcasted_iota(I32, shape, len(shape) - 1)


def sublane_iota(shape):
    return lax.broadcasted_iota(I32, shape, len(shape) - 2)


def move_lanes(tile, shift):
    shift %= LANES
    return tile if shift == 0 else pltpu.roll(tile, shift, 1)


def lane_tile(tiles, start, source, step=16):
    spans = []
    for lane in range(0, LANES, step):
        found = source(start + lane)
        piece = None if found is None else (found[0], (lane - found[1]) % LANES)
        if spans and spans[-1][0] == piece:
            spans[-1][2] = lane + step
        else:
            spans.append([piece, lane, lane + step])
    ranges = {}
    for piece, low, high in spans:
        ranges.setdefault(piece, []).append((low, high))
    values = {
        piece: None if piece is None else move_lanes(tiles(piece[0]), piece[1]) for piece in ranges
    }
    like = next(value for value in values.values() if value is not None)
    result = None
    for piece, value in values.items():
        value = jnp.zeros_like(like) if value is None else value
        if result is None:
            result = value
            continue
        lanes = lane_iota(like.shape)
        inside = None
        for low, high in ranges[piece]:
            here = (lanes >= low) & (lanes < high)
            inside = here if inside is None else inside | here
        result = jnp.where(inside, value, result)
    return result


def swap_halves(tile):
    lanes = lane_iota(tile.shape) % HD
    return jnp.where(
        lanes < HD // 2, move_lanes(tile, LANES - HD // 2), move_lanes(tile, HD // 2)
    )


def rms_scale(values, scaling, epsilon):
    mean_square = jnp.mean(values * values, axis=-1, keepdims=True)
    return values * lax.rsqrt(mean_square + epsilon) * scaling


def project_kernel(rows_ref, gain_ref, weight_ref, out_ref):
    normed = rms_scale(rows_ref[...].astype(F32), gain_ref[...], EPS_WIDE).astype(BF16)
    packed = dot_rows(normed, weight_ref[...])
    count, columns = packed.shape
    if count < 8:
        packed = jnp.concatenate([packed] * (8 // count), axis=0)
    out_ref[:, :, :columns] = jnp.broadcast_to(
        packed[None], (out_ref.shape[0],) + packed.shape
    ).astype(BF16)
    rest = out_ref.shape[2] - columns
    if rest:
        out_ref[:, :, columns:] = jnp.zeros((out_ref.shape[0], 8, rest), BF16)


def lookup_kernel(
    place_ref,
    table_ref,
    length_ref,
    order_ref,
    frequency_ref,
    query_gain_ref,
    key_gain_ref,
    query_cos_ref,
    query_sin_ref,
    key_cos_ref,
    key_sin_ref,
    row_ref,
    valid_ref,
    *,
    pages,
):
    slots = row_ref.shape[0]
    requests, blocks = table_ref.shape
    table = table_ref[...]
    first_page, own_row = place_ref[0], place_ref[1]
    entry = (sublane_iota(table.shape) * blocks + lane_iota(table.shape) + 1).astype(F32)
    found = [
        jnp.sum(jnp.where(table == first_page + slot, entry, 0.0), axis=0, keepdims=True)
        for slot in range(pages)
    ]
    found.append(jnp.zeros((slots - pages, blocks), F32))
    found = jnp.sum(jnp.concatenate(found, axis=0), axis=1, keepdims=True).astype(I32) - 1
    slot = sublane_iota((slots, 1))
    order = order_ref[...]
    lanes = lane_iota(order.shape)
    own_request = jnp.sum(
        jnp.where(lanes == own_row, order, 0).astype(F32), axis=1, keepdims=True
    ).astype(I32)
    request = jnp.where(slot == pages, own_request, jnp.where(found < 0, -1, found // blocks))
    block = jnp.where(found < 0, 0, found % blocks)
    lane_full = lane_iota((slots, requests))
    length = jnp.sum(
        jnp.where(lane_full == request, length_ref[...].astype(F32), 0.0), axis=1, keepdims=True
    )
    row = jnp.sum(
        jnp.where(order == request, lane_full.astype(F32), 0.0), axis=1, keepdims=True
    ).astype(I32)
    row = jnp.where(request < 0, -1, row)
    valid = jnp.clip(length.astype(I32) - block * PAGE, 0, PAGE)
    valid = jnp.where(slot == pages, 1, jnp.where(request < 0, 0, valid))
    angles = length * frequency_ref[...]
    cosines, sines = jnp.cos(angles), jnp.sin(angles)
    half = lane_iota(angles.shape) % HD
    sines = jnp.where(half < HD // 2, -sines, sines)
    for gain_ref, cos_ref, sin_ref, factor in (
        (query_gain_ref, query_cos_ref, query_sin_ref, HD ** (-0.5)),
        (key_gain_ref, key_cos_ref, key_sin_ref, 1.0),
    ):
        gain = jnp.broadcast_to(gain_ref[...] * factor, (8, HD))
        gain = jnp.concatenate([gain, gain], axis=1)
        cos_ref[...] = cosines * gain[:1]
        sin_ref[...] = sines * swap_halves(gain)[:1]
    row_ref[...] = jnp.broadcast_to(row, row_ref.shape)
    valid_ref[...] = jnp.broadcast_to(valid, valid_ref.shape)


def attend_kernel(
    packed_ref,
    page_ref,
    query_cos_ref,
    query_sin_ref,
    key_cos_ref,
    key_sin_ref,
    row_ref,
    valid_ref,
    sums_ref,
    entry_ref,
    query_ref,
    fresh_ref,
    partial_ref,
    *,
    pool_count,
    mp_count,
    group_rows,
    columns,
):
    pages = page_ref.shape[0]
    slots = row_ref.shape[0]
    row = row_ref[...][:, :1]
    total_rows = packed_ref.shape[0]
    source = lane_iota((slots, total_rows))
    source_row = source // (mp_count * group_rows) * group_rows + source % group_rows
    source_part = source // group_rows % mp_count
    hit = source_row == row
    choose = jnp.concatenate(
        [jnp.where(hit & (source_part == part), 1.0, 0.0) for part in range(mp_count)], axis=0
    ).astype(BF16)
    chosen = dot(choose, packed_ref[...])

    def part_tile(key):
        part, tile = key
        return chosen[part * slots : (part + 1) * slots, tile * LANES : (tile + 1) * LANES]

    def part_source(column):
        part, local = divmod(column, columns)
        return (part, local // LANES), local % LANES

    tile_count = (H * HD + ENTRY) // LANES
    query_tiles = H * HD // LANES
    key_tiles = up_to(KEYS, LANES) // LANES
    tiles = [lane_tile(part_tile, t * LANES, part_source) for t in range(tile_count)]
    stacked = jnp.concatenate(tiles[: query_tiles + key_tiles], axis=0)
    ones = jnp.where(
        sublane_iota((LANES, LANES)) // HD == lane_iota((LANES, LANES)) // HD, 1.0, 0.0
    ).astype(BF16)
    high, low = two_halves(stacked * stacked)
    scale = lax.rsqrt((dot(high, ones) + dot(low, ones)) * (1.0 / HD) + EPS_HEAD)
    swapped = swap_halves(stacked)
    split = query_tiles * slots

    def turned(low, high, cos_ref, sin_ref):
        shape = ((high - low) // slots, slots, LANES)
        value = stacked[low:high].reshape(shape) * cos_ref[...][None]
        value = value + swapped[low:high].reshape(shape) * sin_ref[...][None]
        return (value * scale[low:high].reshape(shape)).astype(BF16).astype(F32)

    queries = turned(0, split, query_cos_ref, query_sin_ref)
    keys = turned(split, stacked.shape[0], key_cos_ref, key_sin_ref)
    middle = jnp.where(lane_iota((slots, LANES)) < KEYS % LANES, keys[-1], tiles[-key_tiles])
    entries = [keys[t] for t in range(key_tiles - 1)] + [middle] + tiles[-(key_tiles - 1) :]
    fresh = jnp.concatenate(entries, axis=1)[pages : pages + 8]
    entry_ref[...] = fresh[:1].astype(BF16)
    fresh = jnp.where(sublane_iota(fresh.shape) == 0, fresh, 0.0)
    fresh_ref[...] = jnp.concatenate([fresh, jnp.zeros_like(fresh)], axis=0).astype(BF16)

    wide = key_tiles * LANES
    for member in range(GROUPS):

        def query_source(column):
            kv = column // HD
            if kv >= KVH:
                return None
            head = kv * GROUPS + member
            return head // 2, head % 2 * HD + column % HD

        query_ref[member] = jnp.concatenate(
            [
                lane_tile(lambda t: queries[t], t * LANES, query_source)
                for t in range(key_tiles)
            ],
            axis=1,
        )

    key_mask = lane_iota((8, wide)) // HD == sublane_iota((8, wide))
    value_skip = wide - KEYS
    value_mask = (lane_iota((8, wide)) + (HD - value_skip)) // HD == sublane_iota((8, wide)) + 1
    total_mask = (lane_iota((8, wide)) == sublane_iota((8, wide))) & (
        sublane_iota((8, wide)) < KVH
    )
    value_mask = value_mask & (sublane_iota((8, wide)) < KVH)
    for slot in range(pages + 1):
        spread = jnp.concatenate(
            [
                jnp.where(
                    key_mask,
                    jnp.broadcast_to(query_ref[member, slot : slot + 1, :], (8, wide)),
                    0.0,
                )
                for member in range(GROUPS)
            ],
            axis=0,
        ).astype(BF16)
        if slot < pages:
            key_rows = page_ref[slot, :, :wide]
            value_rows = page_ref[slot, :, ENTRY - wide :]
        else:
            key_rows = fresh_ref[:, :wide]
            value_rows = fresh_ref[:, ENTRY - wide :]
        scores = dot_rows(spread, key_rows)
        count = valid_ref[slot : slot + 1, : scores.shape[1]]
        weights = jnp.where(lane_iota(scores.shape) < count, jnp.exp(scores), 0.0)
        totals = jnp.sum(weights, axis=1, keepdims=True)
        weighted = dot(weights.astype(BF16), value_rows)
        for member in range(GROUPS):
            low = member * 8
            kept = jnp.where(value_mask, weighted[low : low + 8], 0.0)
            kept = jnp.where(total_mask, totals[low : low + 8], kept)
            partial_ref[member, slot * 8 : slot * 8 + 8, :] = kept

    depth = partial_ref.shape[1]
    spread_row = jnp.sum(
        jnp.where(
            lane_iota((slots, depth)) // 8 == sublane_iota((slots, depth)),
            jnp.broadcast_to(row, (slots, depth)).astype(F32),
            0.0,
        ),
        axis=0,
        keepdims=True,
    ).astype(I32)
    copies = 8 // group_rows
    place = sublane_iota((pool_count * 8, depth))
    place = place // 8 * group_rows + place % group_rows
    collect = jnp.where(place == spread_row, 1.0, 0.0).astype(BF16)
    summed = []
    for member in range(GROUPS):
        high, low = two_halves(partial_ref[member])
        summed.append(dot(collect, high) + dot(collect, low))
    first = lane_iota((pool_count * 8, LANES)) < KVH
    totals = None
    for member in range(GROUPS):
        moved = move_lanes(jnp.where(first, summed[member][:, :LANES], 0.0), KVH * member)
        totals = moved if totals is None else totals + moved
    rounded = totals.astype(BF16).astype(F32)
    totals = rounded + move_lanes(totals - rounded, H)

    head_cols = H * HD // mp_count
    width = sums_ref.shape[3]

    def sum_tile(key):
        if key == "totals":
            return totals
        member, tile = key
        return summed[member][:, tile * LANES : (tile + 1) * LANES]

    for pair in range(mp_count // copies):
        parts = []
        for part in range(pair * copies, (pair + 1) * copies):

            def sum_source(column):
                if column >= head_cols:
                    lane = column - head_cols
                    return ("totals", lane) if lane < 2 * H else None
                kv, member = divmod((part * head_cols + column) // HD, GROUPS)
                lane = value_skip + kv * HD + (part * head_cols + column) % HD
                return (member, lane // LANES), lane % LANES

            parts.append(
                jnp.concatenate(
                    [lane_tile(sum_tile, start, sum_source) for start in range(0, width, LANES)],
                    axis=1,
                )
            )
        block = parts[0]
        for index in range(1, copies):
            block = jnp.where(
                sublane_iota(block.shape) % 8 >= index * group_rows, parts[index], block
            )
        sums_ref[:, pair] = block.reshape(pool_count, 8, width).astype(BF16)


def mix_kernel(place_ref, sums_ref, hidden_ref, weight_ref, kept_ref, sent_ref):
    total_rows, width = sums_ref.shape
    head_cols = weight_ref.shape[0]
    group_rows = hidden_ref.shape[0]
    part = place_ref[2]
    same = jnp.where(
        lane_iota((8, total_rows)) % group_rows == sublane_iota((8, total_rows)) % group_rows,
        1.0,
        0.0,
    ).astype(BF16)
    sums = dot(same, sums_ref[...])
    tile = head_cols // LANES * LANES
    totals = sums[:, tile : tile + LANES]
    column = lane_iota((LANES, head_cols)) + part * head_cols
    head = column // HD
    lane = sublane_iota((LANES, head_cols)) - (head_cols - tile)
    index = head % GROUPS * KVH + head // GROUPS
    spread = jnp.where((lane == index) | (lane == index + H), 1.0, 0.0).astype(BF16)
    high = totals.astype(BF16)
    middle, low = two_halves(totals - high.astype(F32))
    denominator = dot(high, spread) + dot(middle, spread) + dot(low, spread)
    attended = (sums[:, :head_cols] / denominator).astype(BF16)
    projected = dot(attended, weight_ref[...])[:group_rows]
    kept_ref[...] = projected + hidden_ref[...].astype(F32)
    sent_ref[...] = projected.astype(BF16)


def feed_kernel(place_ref, *refs, steps):
    kept_ref, *arrived = refs[: steps + 1]
    gain_ref, gate_ref, up_ref, down_ref = refs[steps + 1 : steps + 5]
    base_ref, *sent = refs[steps + 5 : 2 * steps + 6]
    part_ref = refs[-1]
    group_rows = kept_ref.shape[0]
    part = place_ref[2]
    mixed = kept_ref[...]
    for ref in arrived:
        mixed = mixed + ref[...].astype(F32)
    mixed = mixed.astype(BF16).astype(F32)
    normed = rms_scale(mixed, gain_ref[...], EPS_WIDE).astype(BF16)
    gate = dot(normed, gate_ref[...])
    up = dot(normed, up_ref[...])
    hidden = (gate * jax.nn.sigmoid(gate) * up).astype(BF16)
    part_ref[:group_rows] = dot(hidden, down_ref[...])
    own = part_ref[pl.ds(part, 1), :]
    for step, ref in enumerate(sent):
        target = lax.rem(part + (step + 1), steps + 1)
        ref[...] = part_ref[pl.ds(target, 1), :].astype(BF16)
    part_ref[:group_rows] = mixed
    base_ref[...] = own + part_ref[pl.ds(part, 1), :]


def in_vmem(count):
    return [pl.BlockSpec(memory_space=pltpu.VMEM)] * count


SCALARS = pl.BlockSpec(memory_space=pltpu.SMEM)


def params(limit):
    return pltpu.CompilerParams(vmem_limit_bytes=limit * MIB)


def shards(
    hidden_in,
    mix_gain,
    project_in,
    query_gain,
    key_gain,
    page_cache,
    page_table,
    lengths,
    row_order,
    out_weight,
    feed_gain,
    gate_weight,
    up_weight,
    down_weight,
):
    pool_count = lax.axis_size("pool")
    mp_count = lax.axis_size("mp")
    devices = pool_count * mp_count
    device = lax.axis_index("pool") * mp_count + lax.axis_index("mp")
    group_rows, model = hidden_in.shape
    pages = page_cache.shape[0]
    requests = lengths.shape[0]
    columns = project_in.shape[1]
    padded = up_to(columns, LANES)
    head_cols = H * HD // mp_count
    width = up_to(head_cols + 2 * H, LANES)
    slots = up_to(pages + 1, 8)
    total_rows = devices * group_rows
    everyone = ("pool", "mp")
    place = jnp.stack([device * pages, device, lax.axis_index("mp")]).astype(I32)
    exponent = np.arange(LANES) % (HD // 2) * (-2.0 / HD)
    frequency = jnp.asarray((10000.0**exponent).astype(np.float32)[None])

    packed = pl.pallas_call(
        project_kernel,
        out_shape=jax.ShapeDtypeStruct((total_rows // 8, 8, padded), BF16),
        in_specs=in_vmem(3),
        out_specs=in_vmem(1)[0],
        compiler_params=params(8),
        name="project",
    )(hidden_in, mix_gain[None], project_in.T)
    packed = lax.all_to_all(
        packed.reshape(devices, group_rows, padded), everyone, 0, 0, tiled=True
    )

    table = jax.ShapeDtypeStruct((slots, LANES), F32)
    index = jax.ShapeDtypeStruct((slots, LANES), I32)
    found = pl.pallas_call(
        lambda *refs: lookup_kernel(*refs, pages=pages),
        out_shape=(table, table, table, table, index, index),
        in_specs=[SCALARS] + in_vmem(6),
        out_specs=in_vmem(6),
        compiler_params=params(4),
        cost_estimate=pl.CostEstimate(flops=10_000_000, bytes_accessed=10_000_000, transcendentals=0),
        name="lookup",
    )(
        place,
        page_table,
        lengths[None],
        row_order[None],
        frequency,
        query_gain[None],
        key_gain[None],
    )

    copies = 8 // group_rows
    wide = up_to(KEYS, LANES)
    sums, new_entries = pl.pallas_call(
        lambda *refs: attend_kernel(
            *refs,
            pool_count=pool_count,
            mp_count=mp_count,
            group_rows=group_rows,
            columns=columns,
        ),
        out_shape=(
            jax.ShapeDtypeStruct((pool_count, mp_count // copies, 8, width), BF16),
            jax.ShapeDtypeStruct((1, ENTRY), BF16),
        ),
        in_specs=in_vmem(8),
        out_specs=in_vmem(2),
        scratch_shapes=[
            pltpu.VMEM((GROUPS, slots, wide), F32),
            pltpu.VMEM((16, ENTRY), BF16),
            pltpu.VMEM((GROUPS, (pages + 1) * 8, wide), F32),
        ],
        compiler_params=params(16),
        name="attend",
    )(packed.reshape(total_rows, padded), page_cache, *found)
    sums = lax.all_to_all(
        sums.reshape(devices, group_rows, width), everyone, 0, 0, tiled=True
    )

    kept, sent = pl.pallas_call(
        mix_kernel,
        out_shape=(
            jax.ShapeDtypeStruct((group_rows, model), F32),
            jax.ShapeDtypeStruct((group_rows, model), BF16),
        ),
        in_specs=[SCALARS] + in_vmem(3),
        out_specs=in_vmem(2),
        compiler_params=params(8),
        name="mix",
    )(place, sums.reshape(total_rows, width), hidden_in, out_weight)

    def ring(value, step):
        return lax.ppermute(value, "mp", [(i, (i + step) % mp_count) for i in range(mp_count)])

    steps = mp_count - 1
    arrived = [ring(sent, step) for step in range(1, mp_count)]
    base, *rows = pl.pallas_call(
        lambda *refs: feed_kernel(*refs, steps=steps),
        out_shape=(jax.ShapeDtypeStruct((1, model), F32),)
        + (jax.ShapeDtypeStruct((1, model), BF16),) * steps,
        in_specs=[SCALARS] + in_vmem(steps + 5),
        out_specs=in_vmem(steps + 1),
        scratch_shapes=[pltpu.VMEM((8, model), F32)],
        compiler_params=params(24),
        name="feed",
    )(place, kept, *arrived, feed_gain[None], gate_weight, up_weight, down_weight)
    for step, row in enumerate(rows):
        base = base + ring(row, step + 1).astype(F32)
    return (base.astype(BF16), new_entries)


def solution(mesh):
    in_specs = (
        P("pool", None),
        P(),
        P(None, "mp"),
        P(),
        P(),
        P(("pool", "mp"), None, None),
        P(),
        P(),
        P(),
        P("mp", None),
        P(),
        P(None, "mp"),
        P(None, "mp"),
        P("mp", None),
    )
    out_specs = (P(("pool", "mp"), None), P(("pool", "mp"), None))
    return jax.shard_map(shards, mesh=mesh, in_specs=in_specs, out_specs=out_specs, check_vma=False)
```

time: 281 us -> 64.7 us (0.23)
  blocking collectives: 143 us -> 10.1 us
  waiting for transfers between devices: 77.8 us -> 10.8 us
  matrix products: 15.6 us -> 0 us
  starting transfers between devices: 0.04 us -> 15.1 us
  between operations: 14.3 us -> 0.72 us
  other arithmetic: 10.8 us -> 0.7 us
  Pallas kernels: 0 us -> 9.83 us
    unnamed x2 -> x0, waiting for transfers between devices: 77.8 us -> none
    all_gather x1 -> x0, blocking collectives: 70.7 us -> none  [shards(): gathered = lax.all_gather(packed_part, ('pool', 'mp'), axis=1, tiled=True)]
    unnamed x2 -> x0, blocking collectives: 52.9 us -> none
    psum x1 -> x0, blocking collectives: 19.9 us -> none  [shards(): summed = lax.psum(projected, 'mp')]
    dot_general x9 -> x0, matrix products: 15.4 us -> none  [the longest x1 5.83 us: shards(): jnp.dot(hidden, down_weight, preferred_element_type=jnp.float32)]
    unnamed x31 -> x32, local copies, waits for them, and re-layouts: 2.2 us -> 16.1 us
    all_to_all x0 -> x1, blocking collectives: none -> 10.1 us  [shards(): lax.all_to_all(sums.reshape(devices, group_rows, width), everyone, 0, 0,...]
    pallas_call x0 -> x5, Pallas kernels: none -> 9.83 us  [the longest x1 4.4 us: shards(): pl.pallas_call(lambda *refs: attend_kernel(*refs, pool_count=pool_count,...]
  transfers between devices with their start and end apart: 1 -> 7, of which waited for: 1 -> 6; matrix products, arithmetic and copies ran while one was open for 2% -> 0% of each run, Pallas kernels for 0% -> 1%
where the time goes in v2:
time: 64.7 us; the launch traced here: 64.2 us
  local copies, waits for them, and re-layouts  16.9 us (26%)
  starting transfers between devices  15.1 us (23%)
  waiting for transfers between devices  10.8 us (17%)
  blocking collectives  10.1 us (16%)
  Pallas kernels  9.83 us (15%)
  between operations  0.72 us (1%)
  other arithmetic  0.7 us (1%)
    unnamed x32, local copies, waits for them, and re-layouts  16.1 us
    all_to_all x1, blocking collectives, shards(): lax.all_to_all(sums.reshape(devices, group_rows, width), everyone, 0, 0,...  10.1 us
    ppermute x6, starting transfers between devices, ring(): lax.ppermute(value, 'mp', [(i, (i + step) % mp_count) for i in range(mp_c...  7.79 us
    ppermute x6, waiting for transfers between devices, ring(): lax.ppermute(value, 'mp', [(i, (i + step) % mp_count) for i in range(mp_c...  7.31 us
    all_to_all x1, starting transfers between devices, shards(): lax.all_to_all(packed.reshape(devices, group_rows, padded), everyone, 0,...  7.3 us
    pallas_call x1, Pallas kernels, shards(): pl.pallas_call(lambda *refs: attend_kernel(*refs, pool_count=pool_count,...  4.4 us
    all_to_all x1, waiting for transfers between devices, shards(): lax.all_to_all(packed.reshape(devices, group_rows, padded), everyone, 0,...  3.49 us
    pallas_call x1, Pallas kernels, shards(): pl.pallas_call(lambda *refs: feed_kernel(*refs, steps=steps), out_shape=(...  2.8 us
  transfers between devices with their start and end apart: 7, of which 6 were waited for; matrix products, arithmetic and copies ran while one was open for 0% of the time, Pallas kernels for 1%

profile of v2, /device:TPU:0, one launch (start us, length us, event | category | flops | bytes accessed | tf_op | source)
XLA Modules:
  0.0 64.2 jit_solution(9630739403562001109)
XLA Ops:
  0.6 1.5 %copy-done.4 = bf16[2048,480]{0,1:T(8,128)(2,1)S(1)} copy-done((bf16[2048,480]{0,1:T(8,128)(2,1)S(1)}, bf16[2048,480]{0,1:T(8,128)(2,1)}, u32[]{:S(2)}) %copy-start.4) | copy-done | bytes 1966104
  2.2 0.7 %copy-done.6 = bf16[4,2048]{1,0:T(4,128)(2,1)S(1)} copy-done((bf16[4,2048]{1,0:T(4,128)(2,1)S(1)}, bf16[4,2048]{1,0:T(4,128)(2,1)}, u32[]{:S(2)}) %copy-start.6) | copy-done | bytes 16408
  2.9 0.7 %copy-done.9 = f32[2048]{0:T(1024)S(1)} copy-done((f32[2048]{0:T(1024)S(1)}, f32[2048]{0:T(1024)}, u32[]{:S(2)}) %copy-start.9) | copy-done | bytes 8216
  3.6 0.7 %project.1 = bf16[16,8,512]{2,1,0:T(8,128)(2,1)S(1)} custom-call(bf16[4,2048]{1,0:T(4,128)(2,1)S(1)} %copy-done.6, f32[1,2048]{1,0:T(1,128)S(1)} %bitcast.14, bf16[480,2048]{1,0:T(8,128)(2,1)S(1)} %bitcast.12), custom_call_target="tpu_custom_call" | custom-call | tf_op jit(solution)/shard_map/project/pallas_call | solution.py:455
  4.3 0.7 %reshape.16 = bf16[32,4,512]{2,1,0:T(4,128)(2,1)} reshape(bf16[16,8,512]{2,1,0:T(8,128)(2,1)S(1)} %project.1) | data formatting | bytes 262144 | tf_op jit(solution)/shard_map/reshape | solution.py:464
  5.0 7.3 %all-to-all-start = ((bf16[32,4,512]{2,1,0:T(4,128)(2,1)}), bf16[32,4,512]{2,1,0:T(4,128)(2,1)S(1)}, u32[]{:S(2)}, u32[]{:S(2)}) async-start(bf16[32,4,512]{2,1,0:T(4,128)(2,1)} %reshape.16), calls=%async_computation | async-start | bytes 262144 | tf_op jit(solution)/shard_map/all_to_all | solution.py:463
  12.4 0.7 %copy-done.10 = s32[32,64]{1,0:T(8,128)S(1)} copy-done((s32[32,64]{1,0:T(8,128)S(1)}, s32[32,64]{1,0:T(8,128)}, u32[]{:S(2)}) %copy-start.10) | copy-done | bytes 8216
  16.4 0.8 %lookup.1 = (f32[24,128]{1,0:T(8,128)S(1)}, f32[24,128]{1,0:T(8,128)S(1)}, f32[24,128]{1,0:T(8,128)S(1)}, f32[24,128]{1,0:T(8,128)S(1)}, s32[24,128]{1,0:T(8,128)S(1)}, /*index=5*/s32[24,128]{1,0:T(8,128)S(1)}) custom-call(s32[3]{0:T(128)S(1)} %pad_add_fusion.refs_0_.place_ref, s32[32,64]{1,0:T(8,128)S(1)} %copy-done.10, s32[1,32]{1,0:T(1,128)S(1)} %bitcast.15, ...), custom_call_target="tpu_custom_call" | custom-call | flops 10000000 | bytes 10000000 | tf_op jit(solution)/shard_map/lookup/pallas_call | solution.py:469
  17.2 3.5 %all-to-all-done = bf16[32,4,512]{2,1,0:T(4,128)(2,1)S(1)} async-done(((bf16[32,4,512]{2,1,0:T(4,128)(2,1)}), bf16[32,4,512]{2,1,0:T(4,128)(2,1)S(1)}, u32[]{:S(2)}, u32[]{:S(2)}) %all-to-all-start) | async-done | bytes 131104 | tf_op jit(solution)/shard_map/all_to_all | solution.py:463
  20.7 1.7 %copy-done.3 = bf16[16,128,640]{2,1,0:T(8,128)(2,1)S(1)} copy-done((bf16[16,128,640]{2,1,0:T(8,128)(2,1)S(1)}, bf16[16,128,640]{2,1,0:T(8,128)(2,1)}, u32[]{:S(2)}) %copy-start.3) | copy-done | bytes 2621464
  22.5 4.4 %attend.1 = (bf16[8,2,8,384]{3,2,1,0:T(8,128)(2,1)S(1)}, bf16[1,640]{1,0:T(2,128)(2,1)}) custom-call(bf16[128,512]{1,0:T(8,128)(2,1)S(1)} %reshape.17.refs_0_, bf16[16,128,640]{2,1,0:T(8,128)(2,1)S(1)} %copy-done.3, f32[24,128]{1,0:T(8,128)S(1)} %get-tuple-element.16.refs_2_, f32[24,128]{1,0:T(8,128)S(1)} %get-tuple-element.17.refs_3_, ...), custom_call_target="tpu_custom_call" | custom-call | tf_op jit(solution)/shard_map/attend/pallas_call | solution.py:489
  26.9 10.1 %all_to_all.10 = bf16[32,4,384]{2,1,0:T(4,128)(2,1)S(1)} all-to-all(bf16[32,4,384]{2,1,0:T(4,128)(2,1)S(1)} %reshape.18), channel_id=1, replica_groups=mesh['pool'=8,'mp'=4] {'pool','mp'}, dimensions={0} | all-to-all | bytes 196608 | tf_op jit(solution)/shard_map/all_to_all | solution.py:511
  37.1 1.1 %mix.1 = (f32[4,2048]{1,0:T(4,128)S(1)}, bf16[4,2048]{1,0:T(4,128)(2,1)S(1)}) custom-call(s32[3]{0:T(128)S(1)} %pad_add_fusion.refs_0_.place_ref, bf16[128,384]{1,0:T(8,128)(2,1)S(1)} %reshape.19.sums_ref, bf16[4,2048]{1,0:T(4,128)(2,1)S(1)} %copy-done.7, bf16[320,2048]{1,0:T(8,128)(2,1)S(1)} %copy-done.5), custom_call_target="tpu_custom_call" | custom-call | tf_op jit(solution)/shard_map/mix/pallas_call | solution.py:515
  38.2 1.6 %collective-permute-start.1 = (bf16[4,2048]{1,0:T(4,128)(2,1)S(1)}, bf16[4,2048]{1,0:T(4,128)(2,1)S(1)}, u32[]{:S(2)}, u32[]{:S(2)}) collective-permute-start(bf16[4,2048]{1,0:T(4,128)(2,1)S(1)} %get-tuple-element.24), channel_id=1, source_target_pairs={{0,2},{1,3},{2,0},{3,1},{4,6},{5,7},{6,4},{7,5},{8,10},{9,11},{10,... | collective-permute-start | bytes 49160 | tf_op jit(solution)/shard_map/ppermute | solution.py:528
  39.8 2.2 %collective-permute-start.2 = (bf16[4,2048]{1,0:T(4,128)(2,1)S(1)}, bf16[4,2048]{1,0:T(4,128)(2,1)S(1)}, u32[]{:S(2)}, u32[]{:S(2)}) collective-permute-start(bf16[4,2048]{1,0:T(4,128)(2,1)S(1)} %get-tuple-element.24), channel_id=1, source_target_pairs={{0,3},{1,0},{2,1},{3,2},{4,7},{5,4},{6,5},{7,6},{8,11},{9,8},{10,9... | collective-permute-start | bytes 49160 | tf_op jit(solution)/shard_map/ppermute | solution.py:528
  42.0 1.8 %collective-permute-done.refs_2_ = bf16[4,2048]{1,0:T(4,128)(2,1)S(1)} collective-permute-done((bf16[4,2048]{1,0:T(4,128)(2,1)S(1)}, bf16[4,2048]{1,0:T(4,128)(2,1)S(1)}, u32[]{:S(2)}, u32[]{:S(2)}) %collective-permute-start) | collective-permute-done | bytes 16416 | tf_op jit(solution)/shard_map/ppermute | solution.py:528
  44.3 2.5 %copy-done = bf16[2048,1280]{1,0:T(8,128)(2,1)S(1)} copy-done((bf16[2048,1280]{1,0:T(8,128)(2,1)S(1)}, bf16[2048,1280]{1,0:T(8,128)(2,1)}, u32[]{:S(2)}) %copy-start) | copy-done | bytes 5242904
  46.8 2.5 %copy-done.1 = bf16[2048,1280]{1,0:T(8,128)(2,1)S(1)} copy-done((bf16[2048,1280]{1,0:T(8,128)(2,1)S(1)}, bf16[2048,1280]{1,0:T(8,128)(2,1)}, u32[]{:S(2)}) %copy-start.1) | copy-done | bytes 5242904
  49.3 2.5 %copy-done.2 = bf16[1280,2048]{1,0:T(8,128)(2,1)S(1)} copy-done((bf16[1280,2048]{1,0:T(8,128)(2,1)S(1)}, bf16[1280,2048]{1,0:T(8,128)(2,1)}, u32[]{:S(2)}) %copy-start.2) | copy-done | bytes 5242904
  51.8 2.8 %feed.1 = (f32[1,2048]{1,0:T(1,128)S(1)}, bf16[1,2048]{1,0:T(2,128)(2,1)S(1)}, bf16[1,2048]{1,0:T(2,128)(2,1)S(1)}, bf16[1,2048]{1,0:T(2,128)(2,1)S(1)}) custom-call(s32[3]{0:T(128)S(1)} %pad_add_fusion.refs_0_.place_ref, f32[4,2048]{1,0:T(4,128)S(1)} %get-tuple-element.23.refs_1_, bf16[4,2048]{1,0:T(4,128)(2,1)S(1)} %collective-permute-done.refs_2_, ...), custom_call_target="tpu_custom_call" | custom-call | tf_op jit(solution)/shard_map/feed/pallas_call | solution.py:532
  54.6 3.3 %collective-permute-start.5 = (bf16[1,2048]{1,0:T(2,128)(2,1)S(1)}, bf16[1,2048]{1,0:T(2,128)(2,1)S(1)}, u32[]{:S(2)}, u32[]{:S(2)}) collective-permute-start(bf16[1,2048]{1,0:T(2,128)(2,1)S(1)} %get-tuple-element.28), channel_id=1, source_target_pairs={{0,3},{1,0},{2,1},{3,2},{4,7},{5,4},{6,5},{7,6},{8,11},{9,8},{10,9... | collective-permute-start | bytes 12296 | tf_op jit(solution)/shard_map/ppermute | solution.py:528
  58.5 0.7 %collective-permute-done.5 = bf16[1,2048]{1,0:T(2,128)(2,1)S(1)} collective-permute-done((bf16[1,2048]{1,0:T(2,128)(2,1)S(1)}, bf16[1,2048]{1,0:T(2,128)(2,1)S(1)}, u32[]{:S(2)}, u32[]{:S(2)}) %collective-permute-start.5) | collective-permute-done | bytes 4128 | tf_op jit(solution)/shard_map/ppermute | solution.py:528
  59.2 3.2 %collective-permute-done.4 = bf16[1,2048]{1,0:T(2,128)(2,1)S(1)} collective-permute-done((bf16[1,2048]{1,0:T(2,128)(2,1)S(1)}, bf16[1,2048]{1,0:T(2,128)(2,1)S(1)}, u32[]{:S(2)}, u32[]{:S(2)}) %collective-permute-start.4) | collective-permute-done | bytes 4128 | tf_op jit(solution)/shard_map/ppermute | solution.py:528
  62.4 1.1 %collective-permute-done.3 = bf16[1,2048]{1,0:T(2,128)(2,1)S(1)} collective-permute-done((bf16[1,2048]{1,0:T(2,128)(2,1)S(1)}, bf16[1,2048]{1,0:T(2,128)(2,1)S(1)}, u32[]{:S(2)}, u32[]{:S(2)}) %collective-permute-start.3) | collective-permute-done | bytes 4128 | tf_op jit(solution)/shard_map/ppermute | solution.py:528
  (34 shorter events, 5.2 us)
Async XLA Ops:
  0.6 1.5 %copy-start.4 = (bf16[2048,480]{0,1:T(8,128)(2,1)S(1)}, bf16[2048,480]{0,1:T(8,128)(2,1)}, u32[]{:S(2)}) copy-start(bf16[2048,480]{0,1:T(8,128)(2,1)} %param.17) | copy-start | bytes 5898244
  2.2 0.7 %copy-start.6 = (bf16[4,2048]{1,0:T(4,128)(2,1)S(1)}, bf16[4,2048]{1,0:T(4,128)(2,1)}, u32[]{:S(2)}) copy-start(bf16[4,2048]{1,0:T(4,128)(2,1)} %hidden_ref.1) | copy-start | bytes 49156
  2.9 0.7 %copy-start.9 = (f32[2048]{0:T(1024)S(1)}, f32[2048]{0:T(1024)}, u32[]{:S(2)}) copy-start(f32[2048]{0:T(1024)} %param.16) | copy-start | bytes 24580
  3.6 33.5 %copy-start.5 = (bf16[320,2048]{1,0:T(8,128)(2,1)S(1)}, bf16[320,2048]{1,0:T(8,128)(2,1)}, u32[]{:S(2)}) copy-start(bf16[320,2048]{1,0:T(8,128)(2,1)} %weight_ref.1) | copy-start | bytes 3932164
  3.6 33.5 %copy-start.7 = (bf16[4,2048]{1,0:T(4,128)(2,1)S(1)}, bf16[4,2048]{1,0:T(4,128)(2,1)}, u32[]{:S(2)}) copy-start(bf16[4,2048]{1,0:T(4,128)(2,1)} %hidden_ref.1) | copy-start | bytes 49156
  3.6 40.7 %copy-start.8 = (f32[2048]{0:T(1024)S(1)}, f32[2048]{0:T(1024)}, u32[]{:S(2)}) copy-start(f32[2048]{0:T(1024)} %param.25) | copy-start | bytes 24580
  5.0 15.7 %all-to-all-start = ((bf16[32,4,512]{2,1,0:T(4,128)(2,1)}), bf16[32,4,512]{2,1,0:T(4,128)(2,1)S(1)}, u32[]{:S(2)}, u32[]{:S(2)}) async-start(bf16[32,4,512]{2,1,0:T(4,128)(2,1)} %reshape.16), calls=%async_computation | async-start | bytes 262144 | tf_op jit(solution)/shard_map/all_to_all | solution.py:463
  12.4 0.7 %copy-start.10 = (s32[32,64]{1,0:T(8,128)S(1)}, s32[32,64]{1,0:T(8,128)}, u32[]{:S(2)}) copy-start(s32[32,64]{1,0:T(8,128)} %refs_1_.2) | copy-start | bytes 24580
  13.1 0.7 %copy-start.11 = (s32[32]{0:T(128)S(1)}, s32[32]{0:T(128)}, u32[]{:S(2)}) copy-start(s32[32]{0:T(128)} %param.22) | copy-start | bytes 388
  13.8 0.7 %copy-start.12 = (s32[32]{0:T(128)S(1)}, s32[32]{0:T(128)}, u32[]{:S(2)}) copy-start(s32[32]{0:T(128)} %param.23) | copy-start | bytes 388
  14.4 0.7 %copy-start.13 = (f32[64]{0:T(128)S(1)}, f32[64]{0:T(128)}, u32[]{:S(2)}) copy-start(f32[64]{0:T(128)} %param.18) | copy-start | bytes 772
  15.1 0.7 %copy-start.14 = (f32[64]{0:T(128)S(1)}, f32[64]{0:T(128)}, u32[]{:S(2)}) copy-start(f32[64]{0:T(128)} %param.19) | copy-start | bytes 772
  15.7 0.7 %copy-start.15 = (f32[1,128]{1,0:T(1,128)S(1)}, f32[1,128]{1,0:T(1,128)}, u32[]{:S(2)}) copy-start(f32[1,128]{1,0:T(1,128)} %constant.15.clone.refs_4_) | copy-start | bytes 1540
  20.7 1.7 %copy-start.3 = (bf16[16,128,640]{2,1,0:T(8,128)(2,1)S(1)}, bf16[16,128,640]{2,1,0:T(8,128)(2,1)}, u32[]{:S(2)}) copy-start(bf16[16,128,640]{2,1,0:T(8,128)(2,1)} %refs_1_.3) | copy-start | bytes 7864324
  38.2 5.7 %collective-permute-start = (bf16[4,2048]{1,0:T(4,128)(2,1)S(1)}, bf16[4,2048]{1,0:T(4,128)(2,1)S(1)}, u32[]{:S(2)}, u32[]{:S(2)}) collective-permute-start(bf16[4,2048]{1,0:T(4,128)(2,1)S(1)} %get-tuple-element.24), channel_id=1, source_target_pairs={{0,1},{1,2},{2,3},{3,0},{4,5},{5,6},{6,7},{7,4},{8,9},{9,10},{10,1... | collective-permute-start | bytes 49160 | tf_op jit(solution)/shard_map/ppermute | solution.py:528
  38.2 5.6 %collective-permute-start.1 = (bf16[4,2048]{1,0:T(4,128)(2,1)S(1)}, bf16[4,2048]{1,0:T(4,128)(2,1)S(1)}, u32[]{:S(2)}, u32[]{:S(2)}) collective-permute-start(bf16[4,2048]{1,0:T(4,128)(2,1)S(1)} %get-tuple-element.24), channel_id=1, source_target_pairs={{0,2},{1,3},{2,0},{3,1},{4,6},{5,7},{6,4},{7,5},{8,10},{9,11},{10,... | collective-permute-start | bytes 49160 | tf_op jit(solution)/shard_map/ppermute | solution.py:528
  39.8 4.5 %collective-permute-start.2 = (bf16[4,2048]{1,0:T(4,128)(2,1)S(1)}, bf16[4,2048]{1,0:T(4,128)(2,1)S(1)}, u32[]{:S(2)}, u32[]{:S(2)}) collective-permute-start(bf16[4,2048]{1,0:T(4,128)(2,1)S(1)} %get-tuple-element.24), channel_id=1, source_target_pairs={{0,3},{1,0},{2,1},{3,2},{4,7},{5,4},{6,5},{7,6},{8,11},{9,8},{10,9... | collective-permute-start | bytes 49160 | tf_op jit(solution)/shard_map/ppermute | solution.py:528
  44.3 2.5 %copy-start = (bf16[2048,1280]{1,0:T(8,128)(2,1)S(1)}, bf16[2048,1280]{1,0:T(8,128)(2,1)}, u32[]{:S(2)}) copy-start(bf16[2048,1280]{1,0:T(8,128)(2,1)} %refs_6_.1) | copy-start | bytes 15728644
  46.8 2.5 %copy-start.1 = (bf16[2048,1280]{1,0:T(8,128)(2,1)S(1)}, bf16[2048,1280]{1,0:T(8,128)(2,1)}, u32[]{:S(2)}) copy-start(bf16[2048,1280]{1,0:T(8,128)(2,1)} %refs_7_.1) | copy-start | bytes 15728644
  49.3 2.5 %copy-start.2 = (bf16[1280,2048]{1,0:T(8,128)(2,1)S(1)}, bf16[1280,2048]{1,0:T(8,128)(2,1)}, u32[]{:S(2)}) copy-start(bf16[1280,2048]{1,0:T(8,128)(2,1)} %refs_8_.1) | copy-start | bytes 15728644
  54.6 4.7 %collective-permute-start.5 = (bf16[1,2048]{1,0:T(2,128)(2,1)S(1)}, bf16[1,2048]{1,0:T(2,128)(2,1)S(1)}, u32[]{:S(2)}, u32[]{:S(2)}) collective-permute-start(bf16[1,2048]{1,0:T(2,128)(2,1)S(1)} %get-tuple-element.28), channel_id=1, source_target_pairs={{0,3},{1,0},{2,1},{3,2},{4,7},{5,4},{6,5},{7,6},{8,11},{9,8},{10,9... | collective-permute-start | bytes 12296 | tf_op jit(solution)/shard_map/ppermute | solution.py:528
  57.9 4.5 %collective-permute-start.4 = (bf16[1,2048]{1,0:T(2,128)(2,1)S(1)}, bf16[1,2048]{1,0:T(2,128)(2,1)S(1)}, u32[]{:S(2)}, u32[]{:S(2)}) collective-permute-start(bf16[1,2048]{1,0:T(2,128)(2,1)S(1)} %get-tuple-element.27), channel_id=1, source_target_pairs={{0,2},{1,3},{2,0},{3,1},{4,6},{5,7},{6,4},{7,5},{8,10},{9,11},{10,... | collective-permute-start | bytes 12296 | tf_op jit(solution)/shard_map/ppermute | solution.py:528
  58.1 5.4 %collective-permute-start.3 = (bf16[1,2048]{1,0:T(2,128)(2,1)S(1)}, bf16[1,2048]{1,0:T(2,128)(2,1)S(1)}, u32[]{:S(2)}, u32[]{:S(2)}) collective-permute-start(bf16[1,2048]{1,0:T(2,128)(2,1)S(1)} %get-tuple-element.26), channel_id=1, source_target_pairs={{0,1},{1,2},{2,3},{3,0},{4,5},{5,6},{6,7},{7,4},{8,9},{9,10},{10,1... | collective-permute-start | bytes 12296 | tf_op jit(solution)/shard_map/ppermute | solution.py:528

commit v3 on v2

--- a/solution.py
+++ b/solution.py
@@ -96,41 +96,76 @@
     return values * lax.rsqrt(mean_square + epsilon) * scaling
 
 
-def project_kernel(rows_ref, gain_ref, weight_ref, out_ref):
+def copy_in(source, target, semaphore):
+    copy = pltpu.make_async_copy(source, target, semaphore)
+    copy.start()
+    return copy
+
+
+def project_kernel(
+    rows_hbm, gain_hbm, weight_hbm, out_ref, rows_ref, gain_ref, weight_ref, semaphores
+):
+    columns = weight_ref.shape[0]
+    chunk = up_to(columns // 4, 16)
+    first = [
+        copy_in(rows_hbm, rows_ref, semaphores.at[0]),
+        copy_in(gain_hbm, gain_ref, semaphores.at[1]),
+    ]
+    starts = range(0, columns, chunk)
+    copies = []
+    for index, start in enumerate(starts):
+        part = pl.ds(start, min(chunk, columns - start))
+        copies.append(
+            copy_in(weight_hbm.at[part], weight_ref.at[part], semaphores.at[2 + index])
+        )
+    for copy in first:
+        copy.wait()
     normed = rms_scale(rows_ref[...].astype(F32), gain_ref[...], EPS_WIDE).astype(BF16)
-    packed = dot_rows(normed, weight_ref[...])
-    count, columns = packed.shape
-    if count < 8:
-        packed = jnp.concatenate([packed] * (8 // count), axis=0)
-    out_ref[:, :, :columns] = jnp.broadcast_to(
-        packed[None], (out_ref.shape[0],) + packed.shape
-    ).astype(BF16)
-    rest = out_ref.shape[2] - columns
-    if rest:
-        out_ref[:, :, columns:] = jnp.zeros((out_ref.shape[0], 8, rest), BF16)
-
-
-def lookup_kernel(
-    place_ref,
-    table_ref,
-    length_ref,
-    order_ref,
-    frequency_ref,
-    query_gain_ref,
-    key_gain_ref,
-    query_cos_ref,
-    query_sin_ref,
-    key_cos_ref,
-    key_sin_ref,
-    row_ref,
-    valid_ref,
-    *,
-    pages,
-):
+    devices, count, padded = out_ref.shape
+    if padded > columns:
+        out_ref[:, :, columns:] = jnp.zeros((devices, count, padded - columns), BF16)
+    for copy, start in zip(copies, starts):
+        copy.wait()
+        stop = min(start + chunk, columns)
+        packed = dot_rows(normed, weight_ref[start:stop])
+        out_ref[:, :, start:stop] = jnp.broadcast_to(
+            packed.astype(BF16)[None], (devices, count, stop - start)
+        )
+
+
+def lookup_kernel(*refs, pages):
+    sources, outputs, scratch = refs[:7], refs[7:14], refs[14:]
+    (
+        query_cos_ref,
+        query_sin_ref,
+        key_cos_ref,
+        key_sin_ref,
+        row_ref,
+        valid_ref,
+        page_ref,
+    ) = outputs
+    table_ref, length_ref, order_ref, frequency_ref, query_gain_ref, key_gain_ref = scratch[:6]
+    semaphores = scratch[6]
+    small = [
+        copy_in(source, target, semaphores.at[index])
+        for index, (source, target) in enumerate(zip(sources[:6], scratch[:6]))
+    ]
+    step = up_to(pages, 4) // 4
+    large = [
+        copy_in(
+            sources[6].at[pl.ds(start, step)],
+            page_ref.at[pl.ds(start, step)],
+            semaphores.at[6 + start // step],
+        )
+        for start in range(0, pages, step)
+    ]
+    for copy in small:
+        copy.wait()
+    device = lax.axis_index("pool") * lax.axis_size("mp") + lax.axis_index("mp")
     slots = row_ref.shape[0]
     requests, blocks = table_ref.shape
     table = table_ref[...]
-    first_page, own_row = place_ref[0], place_ref[1]
+    first_page, own_row = device * pages, device
     entry = (sublane_iota(table.shape) * blocks + lane_iota(table.shape) + 1).astype(F32)
     found = [
         jnp.sum(jnp.where(table == first_page + slot, entry, 0.0), axis=0, keepdims=True)
@@ -170,6 +205,8 @@
         sin_ref[...] = sines * swap_halves(gain)[:1]
     row_ref[...] = jnp.broadcast_to(row, row_ref.shape)
     valid_ref[...] = jnp.broadcast_to(valid, valid_ref.shape)
+    for copy in large:
+        copy.wait()
 
 
 def attend_kernel(
@@ -195,7 +232,8 @@
     pages = page_ref.shape[0]
     slots = row_ref.shape[0]
     row = row_ref[...][:, :1]
-    total_rows = packed_ref.shape[0]
+    total_rows = packed_ref.shape[0] * packed_ref.shape[1]
+    packed = packed_ref[...].reshape(total_rows, packed_ref.shape[2])
     source = lane_iota((slots, total_rows))
     source_row = source // (mp_count * group_rows) * group_rows + source % group_rows
     source_part = source // group_rows % mp_count
@@ -203,7 +241,7 @@
     choose = jnp.concatenate(
         [jnp.where(hit & (source_part == part), 1.0, 0.0) for part in range(mp_count)], axis=0
     ).astype(BF16)
-    chosen = dot(choose, packed_ref[...])
+    chosen = dot(choose, packed)
 
     def part_tile(key):
         part, tile = key
@@ -305,7 +343,6 @@
         axis=0,
         keepdims=True,
     ).astype(I32)
-    copies = 8 // group_rows
     place = sublane_iota((pool_count * 8, depth))
     place = place // 8 * group_rows + place % group_rows
     collect = jnp.where(place == spread_row, 1.0, 0.0).astype(BF16)
@@ -330,43 +367,28 @@
         member, tile = key
         return summed[member][:, tile * LANES : (tile + 1) * LANES]
 
-    for pair in range(mp_count // copies):
-        parts = []
-        for part in range(pair * copies, (pair + 1) * copies):
-
-            def sum_source(column):
-                if column >= head_cols:
-                    lane = column - head_cols
-                    return ("totals", lane) if lane < 2 * H else None
-                kv, member = divmod((part * head_cols + column) // HD, GROUPS)
-                lane = value_skip + kv * HD + (part * head_cols + column) % HD
-                return (member, lane // LANES), lane % LANES
-
-            parts.append(
-                jnp.concatenate(
-                    [lane_tile(sum_tile, start, sum_source) for start in range(0, width, LANES)],
-                    axis=1,
-                )
-            )
-        block = parts[0]
-        for index in range(1, copies):
-            block = jnp.where(
-                sublane_iota(block.shape) % 8 >= index * group_rows, parts[index], block
-            )
-        sums_ref[:, pair] = block.reshape(pool_count, 8, width).astype(BF16)
-
-
-def mix_kernel(place_ref, sums_ref, hidden_ref, weight_ref, kept_ref, sent_ref):
-    total_rows, width = sums_ref.shape
+    for part in range(mp_count):
+
+        def sum_source(column):
+            if column >= head_cols:
+                lane = column - head_cols
+                return ("totals", lane) if lane < 2 * H else None
+            kv, member = divmod((part * head_cols + column) // HD, GROUPS)
+            lane = value_skip + kv * HD + (part * head_cols + column) % HD
+            return (member, lane // LANES), lane % LANES
+
+        block = jnp.concatenate(
+            [lane_tile(sum_tile, start, sum_source) for start in range(0, width, LANES)], axis=1
+        )
+        block = block.reshape(pool_count, 8, width)[:, :group_rows]
+        sums_ref[:, part] = block.astype(BF16)
+
+
+def mix_kernel(sums_ref, hidden_ref, weight_ref, kept_ref, sent_ref):
     head_cols = weight_ref.shape[0]
     group_rows = hidden_ref.shape[0]
-    part = place_ref[2]
-    same = jnp.where(
-        lane_iota((8, total_rows)) % group_rows == sublane_iota((8, total_rows)) % group_rows,
-        1.0,
-        0.0,
-    ).astype(BF16)
-    sums = dot(same, sums_ref[...])
+    part = lax.axis_index("mp")
+    sums = jnp.sum(sums_ref[...].astype(F32), axis=0)
     tile = head_cols // LANES * LANES
     totals = sums[:, tile : tile + LANES]
     column = lane_iota((LANES, head_cols)) + part * head_cols
@@ -378,18 +400,18 @@
     middle, low = two_halves(totals - high.astype(F32))
     denominator = dot(high, spread) + dot(middle, spread) + dot(low, spread)
     attended = (sums[:, :head_cols] / denominator).astype(BF16)
-    projected = dot(attended, weight_ref[...])[:group_rows]
+    projected = dot(attended, weight_ref[...])
     kept_ref[...] = projected + hidden_ref[...].astype(F32)
     sent_ref[...] = projected.astype(BF16)
 
 
-def feed_kernel(place_ref, *refs, steps):
+def feed_kernel(*refs, steps):
     kept_ref, *arrived = refs[: steps + 1]
     gain_ref, gate_ref, up_ref, down_ref = refs[steps + 1 : steps + 5]
     base_ref, *sent = refs[steps + 5 : 2 * steps + 6]
     part_ref = refs[-1]
     group_rows = kept_ref.shape[0]
-    part = place_ref[2]
+    part = lax.axis_index("mp")
     mixed = kept_ref[...]
     for ref in arrived:
         mixed = mixed + ref[...].astype(F32)
@@ -411,11 +433,32 @@
     return [pl.BlockSpec(memory_space=pltpu.VMEM)] * count
 
 
-SCALARS = pl.BlockSpec(memory_space=pltpu.SMEM)
+def in_hbm(count):
+    return [pl.BlockSpec(memory_space=pltpu.HBM)] * count
 
 
 def params(limit):
     return pltpu.CompilerParams(vmem_limit_bytes=limit * MIB)
+
+
+def cost(count):
+    return pl.CostEstimate(flops=count, bytes_accessed=0, transcendentals=0)
+
+
+def like(array):
+    return jax.ShapeDtypeStruct(array.shape, array.dtype)
+
+
+def far(*arrays):
+    return [pltpu.with_memory_space_constraint(array, pltpu.HBM) for array in arrays]
+
+
+def near(*arrays):
+    return [pltpu.with_memory_space_constraint(array, pltpu.VMEM) for array in arrays]
+
+
+def room(array):
+    return pltpu.VMEM(array.shape, array.dtype)
 
 
 def shards(
@@ -437,45 +480,32 @@
     pool_count = lax.axis_size("pool")
     mp_count = lax.axis_size("mp")
     devices = pool_count * mp_count
-    device = lax.axis_index("pool") * mp_count + lax.axis_index("mp")
     group_rows, model = hidden_in.shape
     pages = page_cache.shape[0]
-    requests = lengths.shape[0]
     columns = project_in.shape[1]
     padded = up_to(columns, LANES)
     head_cols = H * HD // mp_count
     width = up_to(head_cols + 2 * H, LANES)
     slots = up_to(pages + 1, 8)
-    total_rows = devices * group_rows
     everyone = ("pool", "mp")
-    place = jnp.stack([device * pages, device, lax.axis_index("mp")]).astype(I32)
     exponent = np.arange(LANES) % (HD // 2) * (-2.0 / HD)
     frequency = jnp.asarray((10000.0**exponent).astype(np.float32)[None])
 
+    operands = (hidden_in, mix_gain[None], project_in.T)
     packed = pl.pallas_call(
         project_kernel,
-        out_shape=jax.ShapeDtypeStruct((total_rows // 8, 8, padded), BF16),
-        in_specs=in_vmem(3),
+        out_shape=jax.ShapeDtypeStruct((devices, group_rows, padded), BF16),
+        in_specs=in_hbm(3),
         out_specs=in_vmem(1)[0],
+        scratch_shapes=[room(x) for x in operands] + [pltpu.SemaphoreType.DMA((8,))],
         compiler_params=params(8),
         name="project",
-    )(hidden_in, mix_gain[None], project_in.T)
-    packed = lax.all_to_all(
-        packed.reshape(devices, group_rows, padded), everyone, 0, 0, tiled=True
-    )
+    )(*far(*operands))
+    packed = lax.all_to_all(packed, everyone, 0, 0, tiled=True)
 
     table = jax.ShapeDtypeStruct((slots, LANES), F32)
     index = jax.ShapeDtypeStruct((slots, LANES), I32)
-    found = pl.pallas_call(
-        lambda *refs: lookup_kernel(*refs, pages=pages),
-        out_shape=(table, table, table, table, index, index),
-        in_specs=[SCALARS] + in_vmem(6),
-        out_specs=in_vmem(6),
-        compiler_params=params(4),
-        cost_estimate=pl.CostEstimate(flops=10_000_000, bytes_accessed=10_000_000, transcendentals=0),
-        name="lookup",
-    )(
-        place,
+    operands = (
         page_table,
         lengths[None],
         row_order[None],
@@ -483,8 +513,17 @@
         query_gain[None],
         key_gain[None],
     )
-
-    copies = 8 // group_rows
+    *found, cached = pl.pallas_call(
+        lambda *refs: lookup_kernel(*refs, pages=pages),
+        out_shape=(table, table, table, table, index, index, room(page_cache)),
+        in_specs=in_hbm(7),
+        out_specs=in_vmem(7),
+        scratch_shapes=[room(x) for x in operands] + [pltpu.SemaphoreType.DMA((10,))],
+        compiler_params=params(8),
+        cost_estimate=cost(10_000_000),
+        name="lookup",
+    )(*far(*operands, page_cache))
+
     wide = up_to(KEYS, LANES)
     sums, new_entries = pl.pallas_call(
         lambda *refs: attend_kernel(
@@ -495,7 +534,7 @@
             columns=columns,
         ),
         out_shape=(
-            jax.ShapeDtypeStruct((pool_count, mp_count // copies, 8, width), BF16),
+            jax.ShapeDtypeStruct((pool_count, mp_count, group_rows, width), BF16),
             jax.ShapeDtypeStruct((1, ENTRY), BF16),
         ),
         in_specs=in_vmem(8),
@@ -506,8 +545,13 @@
             pltpu.VMEM((GROUPS, (pages + 1) * 8, wide), F32),
         ],
         compiler_params=params(16),
+        cost_estimate=cost(20_000_000_000),
         name="attend",
-    )(packed.reshape(total_rows, padded), page_cache, *found)
+    )(
+        packed,
+        *near(cached),
+        *found,
+    )
     sums = lax.all_to_all(
         sums.reshape(devices, group_rows, width), everyone, 0, 0, tiled=True
     )
@@ -518,11 +562,12 @@
             jax.ShapeDtypeStruct((group_rows, model), F32),
             jax.ShapeDtypeStruct((group_rows, model), BF16),
         ),
-        in_specs=[SCALARS] + in_vmem(3),
+        in_specs=in_vmem(3),
         out_specs=in_vmem(2),
         compiler_params=params(8),
+        cost_estimate=cost(20_000_000_000),
         name="mix",
-    )(place, sums.reshape(total_rows, width), hidden_in, out_weight)
+    )(sums, hidden_in, out_weight)
 
     def ring(value, step):
         return lax.ppermute(value, "mp", [(i, (i + step) % mp_count) for i in range(mp_count)])
@@ -533,12 +578,12 @@
         lambda *refs: feed_kernel(*refs, steps=steps),
         out_shape=(jax.ShapeDtypeStruct((1, model), F32),)
         + (jax.ShapeDtypeStruct((1, model), BF16),) * steps,
-        in_specs=[SCALARS] + in_vmem(steps + 5),
+        in_specs=in_vmem(steps + 5),
         out_specs=in_vmem(steps + 1),
         scratch_shapes=[pltpu.VMEM((8, model), F32)],
         compiler_params=params(24),
         name="feed",
-    )(place, kept, *arrived, feed_gain[None], gate_weight, up_weight, down_weight)
+    )(kept, *arrived, feed_gain[None], gate_weight, up_weight, down_weight)
     for step, row in enumerate(rows):
         base = base + ring(row, step + 1).astype(F32)
     return (base.astype(BF16), new_entries)

time: 64.7 us -> 50.8 us (0.79)
  local copies, waits for them, and re-layouts: 16.9 us -> 0.04 us
  Pallas kernels: 9.83 us -> 12.3 us
  waiting for transfers between devices: 10.8 us -> 13.1 us
  starting transfers between devices: 15.1 us -> 13.6 us
    unnamed x32 -> x18, local copies, waits for them, and re-layouts: 16.1 us -> 0.04 us
    all_to_all x1, waiting for transfers between devices: 3.49 us -> 6.53 us  [shards(): packed = lax.all_to_all(packed, everyone, 0, 0, tiled=True)]
    pallas_call x1, Pallas kernels: 0.7 us -> 3.28 us  [shards(): pl.pallas_call(project_kernel, out_shape=jax.ShapeDtypeStruct((devices, g...]
    ppermute x6, starting transfers between devices: 7.79 us -> 6.3 us  [ring(): lax.ppermute(value, 'mp', [(i, (i + step) % mp_count) for i in range(mp_c...]
    pallas_call x1, Pallas kernels: 0.83 us -> 1.87 us  [shards(): pl.pallas_call(lambda *refs: lookup_kernel(*refs, pages=pages), out_shape...]
    reshape x4 -> x0, local copies, waits for them, and re-layouts: 0.79 us -> none  [the longest x1 0.69 us: shards(): packed.reshape(devices, group_rows, padded)]
    ppermute x6, waiting for transfers between devices: 7.31 us -> 6.61 us  [ring(): lax.ppermute(value, 'mp', [(i, (i + step) % mp_count) for i in range(mp_c...]
  transfers between devices with their start and end apart: 7 -> 7, of which waited for: 6 -> 6; matrix products, arithmetic and copies ran while one was open for 0% -> 0% of each run, Pallas kernels for 1% -> 4%
where the time goes in v3:
time: 50.8 us; the launch traced here: 50.4 us
  starting transfers between devices  13.6 us (27%)
  waiting for transfers between devices  13.1 us (26%)
  Pallas kernels  12.3 us (24%)
  blocking collectives  9.88 us (19%)
  between operations  0.76 us (1%)
  other arithmetic  0.62 us (1%)
    all_to_all x1, blocking collectives, shards(): lax.all_to_all(sums.reshape(devices, group_rows, width), everyone, 0, 0,...  9.88 us
    all_to_all x1, starting transfers between devices, shards(): packed = lax.all_to_all(packed, everyone, 0, 0, tiled=True)  7.3 us
    ppermute x6, waiting for transfers between devices, ring(): lax.ppermute(value, 'mp', [(i, (i + step) % mp_count) for i in range(mp_c...  6.61 us
    all_to_all x1, waiting for transfers between devices, shards(): packed = lax.all_to_all(packed, everyone, 0, 0, tiled=True)  6.53 us
    ppermute x6, starting transfers between devices, ring(): lax.ppermute(value, 'mp', [(i, (i + step) % mp_count) for i in range(mp_c...  6.3 us
    pallas_call x1, Pallas kernels, shards(): pl.pallas_call(lambda *refs: attend_kernel(*refs, pool_count=pool_count,...  4.4 us
    pallas_call x1, Pallas kernels, shards(): pl.pallas_call(project_kernel, out_shape=jax.ShapeDtypeStruct((devices, g...  3.28 us
    pallas_call x1, Pallas kernels, shards(): pl.pallas_call(lambda *refs: feed_kernel(*refs, steps=steps), out_shape=(...  2.26 us
  transfers between devices with their start and end apart: 7, of which 6 were waited for; matrix products, arithmetic and copies ran while one was open for 0% of the time, Pallas kernels for 4%

profile of v3, /device:TPU:0, one launch (start us, length us, event | category | flops | bytes accessed | tf_op | source)
XLA Modules:
  0.0 50.4 jit_solution(8987682103333109982)
XLA Ops:
  0.6 3.3 %project.1 = bf16[32,4,512]{2,1,0:T(4,128)(2,1)} custom-call(bf16[4,2048]{1,0:T(4,128)(2,1)} %hidden_ref.1, f32[1,2048]{1,0:T(1,128)} %bitcast.17, bf16[480,2048]{1,0:T(8,128)(2,1)} %bitcast.16), custom_call_target="tpu_custom_call" | custom-call | tf_op jit(solution)/shard_map/project/pallas_call | solution.py:495
  3.9 7.3 %all-to-all-start = ((bf16[32,4,512]{2,1,0:T(4,128)(2,1)}), bf16[32,4,512]{2,1,0:T(4,128)(2,1)S(1)}, u32[]{:S(2)}, u32[]{:S(2)}) async-start(bf16[32,4,512]{2,1,0:T(4,128)(2,1)} %project.1), calls=%async_computation | async-start | bytes 262144 | tf_op jit(solution)/shard_map/all_to_all | solution.py:504
  11.2 1.9 %lookup.1 = (f32[24,128]{1,0:T(8,128)S(1)}, f32[24,128]{1,0:T(8,128)S(1)}, f32[24,128]{1,0:T(8,128)S(1)}, f32[24,128]{1,0:T(8,128)S(1)}, s32[24,128]{1,0:T(8,128...) custom-call(s32[32,64]{1,0:T(8,128)} %refs_0_.1, s32[1,32]{1,0:T(1,128)} %bitcast.18, s32[1,32]{1,0:T(1,128)} %bitcast.19, ...), custom_call_target="tpu_custom_call" | custom-call | flops 10000000 | tf_op jit(solution)/shard_map/lookup/pallas_call | solution.py:516
  13.1 6.5 %all-to-all-done.refs_0_ = bf16[32,4,512]{2,1,0:T(4,128)(2,1)S(1)} async-done(((bf16[32,4,512]{2,1,0:T(4,128)(2,1)}), bf16[32,4,512]{2,1,0:T(4,128)(2,1)S(1)}, u32[]{:S(2)}, u32[]{:S(2)}) %all-to-all-start) | async-done | bytes 131104 | tf_op jit(solution)/shard_map/all_to_all | solution.py:504
  19.6 4.4 %attend.1 = (bf16[8,4,4,384]{3,2,1,0:T(4,128)(2,1)S(1)}, bf16[1,640]{1,0:T(2,128)(2,1)}) custom-call(bf16[32,4,512]{2,1,0:T(4,128)(2,1)S(1)} %all-to-all-done.refs_0_, bf16[16,128,640]{2,1,0:T(8,128)(2,1)S(1)} %get-tuple-element.17.refs_1_, f32[24,128]{1,0:T(8,128)S(1)} %get-tuple-element.18.refs_2_, f32[24,128]{1,0:T(8,128)S(1)} %get-tuple-element.19.refs_3_, ...), custom_call_target="tpu_custom_call" | custom-call | flops 20000000000 | tf_op jit(solution)/shard_map/attend/pallas_call | solution.py:528
  24.0 9.9 %all_to_all.10.sums_ref = bf16[32,4,384]{2,1,0:T(4,128)(2,1)S(1)} all-to-all(bf16[32,4,384]{2,1,0:T(4,128)(2,1)S(1)} %bitcast.14), channel_id=1, replica_groups=mesh['pool'=8,'mp'=4] {'pool','mp'}, dimensions={0} | all-to-all | bytes 196608 | tf_op jit(solution)/shard_map/all_to_all | solution.py:555
  33.9 0.0 copy-done.2
  33.9 0.0 slice-start.5
  34.0 0.0 copy-start.1
  34.0 0.5 %mix.1 = (f32[4,2048]{1,0:T(4,128)S(1)}, bf16[4,2048]{1,0:T(4,128)(2,1)S(1)}) custom-call(bf16[32,4,384]{2,1,0:T(4,128)(2,1)S(1)} %all_to_all.10.sums_ref, bf16[4,2048]{1,0:T(4,128)(2,1)S(1)} %copy-done, bf16[320,2048]{1,0:T(8,128)(2,1)S(1)} %copy-done.2), custom_call_target="tpu_custom_call" | custom-call | flops 20000000000 | tf_op jit(solution)/shard_map/mix/pallas_call | solution.py:559
  34.5 1.0 %collective-permute-start.2 = (bf16[4,2048]{1,0:T(4,128)(2,1)S(1)}, bf16[4,2048]{1,0:T(4,128)(2,1)S(1)}, u32[]{:S(2)}, u32[]{:S(2)}) collective-permute-start(bf16[4,2048]{1,0:T(4,128)(2,1)S(1)} %get-tuple-element.26), channel_id=1, source_target_pairs={{0,3},{1,0},{2,1},{3,2},{4,7},{5,4},{6,5},{7,6},{8,11},{9,8},{10,9... | collective-permute-start | bytes 49160 | tf_op jit(solution)/shard_map/ppermute | solution.py:573
  35.4 0.4 collective-permute-start.1
  35.8 1.1 %collective-permute-start = (bf16[4,2048]{1,0:T(4,128)(2,1)S(1)}, bf16[4,2048]{1,0:T(4,128)(2,1)S(1)}, u32[]{:S(2)}, u32[]{:S(2)}) collective-permute-start(bf16[4,2048]{1,0:T(4,128)(2,1)S(1)} %get-tuple-element.26), channel_id=1, source_target_pairs={{0,1},{1,2},{2,3},{3,0},{4,5},{5,6},{6,7},{7,4},{8,9},{9,10},{10,1... | collective-permute-start | bytes 49160 | tf_op jit(solution)/shard_map/ppermute | solution.py:573
  36.9 1.3 %collective-permute-done.2.refs_3_ = bf16[4,2048]{1,0:T(4,128)(2,1)S(1)} collective-permute-done((bf16[4,2048]{1,0:T(4,128)(2,1)S(1)}, bf16[4,2048]{1,0:T(4,128)(2,1)S(1)}, u32[]{:S(2)}, u32[]{:S(2)}) %collective-permute-start.2) | collective-permute-done | bytes 16416 | tf_op jit(solution)/shard_map/ppermute | solution.py:573
  38.2 1.8 %collective-permute-done.1.refs_2_ = bf16[4,2048]{1,0:T(4,128)(2,1)S(1)} collective-permute-done((bf16[4,2048]{1,0:T(4,128)(2,1)S(1)}, bf16[4,2048]{1,0:T(4,128)(2,1)S(1)}, u32[]{:S(2)}, u32[]{:S(2)}) %collective-permute-start.1) | collective-permute-done | bytes 16416 | tf_op jit(solution)/shard_map/ppermute | solution.py:573
  40.1 1.3 %collective-permute-done.refs_1_ = bf16[4,2048]{1,0:T(4,128)(2,1)S(1)} collective-permute-done((bf16[4,2048]{1,0:T(4,128)(2,1)S(1)}, bf16[4,2048]{1,0:T(4,128)(2,1)S(1)}, u32[]{:S(2)}, u32[]{:S(2)}) %collective-permute-start) | collective-permute-done | bytes 16416 | tf_op jit(solution)/shard_map/ppermute | solution.py:573
  41.4 2.3 %feed.1 = (f32[1,2048]{1,0:T(1,128)S(1)}, bf16[1,2048]{1,0:T(2,128)(2,1)S(1)}, bf16[1,2048]{1,0:T(2,128)(2,1)S(1)}, bf16[1,2048]{1,0:T(2,128)(2,1)S(1)}) custom-call(f32[4,2048]{1,0:T(4,128)S(1)} %get-tuple-element.25.refs_0_, bf16[4,2048]{1,0:T(4,128)(2,1)S(1)} %collective-permute-done.refs_1_, bf16[4,2048]{1,0:T(4,128)(2,1)S(1)} %collective-permute-done.1.refs_2_, ...), custom_call_target="tpu_custom_call" | custom-call | tf_op jit(solution)/shard_map/feed/pallas_call | solution.py:577
  43.7 0.1 collective-permute-start.3
  43.8 1.8 %collective-permute-start.4 = (bf16[1,2048]{1,0:T(2,128)(2,1)S(1)}, bf16[1,2048]{1,0:T(2,128)(2,1)S(1)}, u32[]{:S(2)}, u32[]{:S(2)}) collective-permute-start(bf16[1,2048]{1,0:T(2,128)(2,1)S(1)} %get-tuple-element.29), channel_id=1, source_target_pairs={{0,2},{1,3},{2,0},{3,1},{4,6},{5,7},{6,4},{7,5},{8,10},{9,11},{10,... | collective-permute-start | bytes 12296 | tf_op jit(solution)/shard_map/ppermute | solution.py:573
  45.6 2.0 %collective-permute-start.5 = (bf16[1,2048]{1,0:T(2,128)(2,1)S(1)}, bf16[1,2048]{1,0:T(2,128)(2,1)S(1)}, u32[]{:S(2)}, u32[]{:S(2)}) collective-permute-start(bf16[1,2048]{1,0:T(2,128)(2,1)S(1)} %get-tuple-element.30), channel_id=1, source_target_pairs={{0,3},{1,0},{2,1},{3,2},{4,7},{5,4},{6,5},{7,6},{8,11},{9,8},{10,9... | collective-permute-start | bytes 12296 | tf_op jit(solution)/shard_map/ppermute | solution.py:573
  47.6 1.6 %collective-permute-done.3 = bf16[1,2048]{1,0:T(2,128)(2,1)S(1)} collective-permute-done((bf16[1,2048]{1,0:T(2,128)(2,1)S(1)}, bf16[1,2048]{1,0:T(2,128)(2,1)S(1)}, u32[]{:S(2)}, u32[]{:S(2)}) %collective-permute-start.3) | collective-permute-done | bytes 4128 | tf_op jit(solution)/shard_map/ppermute | solution.py:573
  49.2 0.0 collective-permute-done.4
  49.2 0.6 %collective-permute-done.5 = bf16[1,2048]{1,0:T(2,128)(2,1)S(1)} collective-permute-done((bf16[1,2048]{1,0:T(2,128)(2,1)S(1)}, bf16[1,2048]{1,0:T(2,128)(2,1)S(1)}, u32[]{:S(2)}, u32[]{:S(2)}) %collective-permute-start.5) | collective-permute-done | bytes 4128 | tf_op jit(solution)/shard_map/ppermute | solution.py:573
  49.8 0.6 %add_convert_fusion = bf16[1,2048]{1,0:T(2,128)(2,1)} fusion(bf16[1,2048]{1,0:T(2,128)(2,1)S(1)} %collective-permute-done.5, bf16[1,2048]{1,0:T(2,128)(2,1)S(1)} %collective-permute-done.4, f32[1,2048]{1,0:T(1,128)S(1)} %get-tuple-element.27, bf16[1,2048]{1,0:T(2,128)(2,1)S(1)} %collective-permute-done.3), kind=kLoop, calls=%fused_computation | loop fusion | flops 14336 | bytes 24576 | tf_op jit(solution)/shard_map/convert_element_type | solution.py:589
  (18 shorter events, 0.0 us)
Async XLA Ops:
  3.9 15.7 %all-to-all-start = ((bf16[32,4,512]{2,1,0:T(4,128)(2,1)}), bf16[32,4,512]{2,1,0:T(4,128)(2,1)S(1)}, u32[]{:S(2)}, u32[]{:S(2)}) async-start(bf16[32,4,512]{2,1,0:T(4,128)(2,1)} %project.1), calls=%async_computation | async-start | bytes 262144 | tf_op jit(solution)/shard_map/all_to_all | solution.py:504
  19.6 14.3 %copy-start = (bf16[4,2048]{1,0:T(4,128)(2,1)S(1)}, bf16[4,2048]{1,0:T(4,128)(2,1)}, u32[]{:S(2)}) copy-start(bf16[4,2048]{1,0:T(4,128)(2,1)} %hidden_ref.1) | copy-start | bytes 49156
  19.6 14.3 %copy-start.2 = (bf16[320,2048]{1,0:T(8,128)(2,1)S(1)}, bf16[320,2048]{1,0:T(8,128)(2,1)}, u32[]{:S(2)}) copy-start(bf16[320,2048]{1,0:T(8,128)(2,1)} %weight_ref.1) | copy-start | bytes 3932164
  24.0 17.3 %slice-start = ((s8[5242880]{0:T(1024)(128)(4,1)}), s8[4194304]{0:T(1024)(128)(4,1)S(1)}, s32[]{:S(2)}) async-start(s8[5242880]{0:T(1024)(128)(4,1)} %bitcast.8), calls=%async_computation.2 | async-start | bytes 8388608
  24.0 17.3 %slice-start.2 = ((s8[5242880]{0:T(1024)(128)(4,1)}), s8[4194304]{0:T(1024)(128)(4,1)S(1)}, s32[]{:S(2)}) async-start(s8[5242880]{0:T(1024)(128)(4,1)} %bitcast.10), calls=%async_computation.4 | async-start | bytes 8388608
  24.0 17.3 %slice-start.4 = ((s8[5242880]{0:T(1024)(128)(4,1)}), s8[4194304]{0:T(1024)(128)(4,1)S(1)}, s32[]{:S(2)}) async-start(s8[5242880]{0:T(1024)(128)(4,1)} %bitcast.12), calls=%async_computation.6 | async-start | bytes 8388608
  33.9 7.4 %slice-start.1 = ((s8[5242880]{0:T(1024)(128)(4,1)}), s8[1048576]{0:T(1024)(128)(4,1)S(1)}, s32[]{:S(2)}) async-start(s8[5242880]{0:T(1024)(128)(4,1)} %bitcast.8), calls=%async_computation.3 | async-start | bytes 2097152
  33.9 7.4 %slice-start.3 = ((s8[5242880]{0:T(1024)(128)(4,1)}), s8[1048576]{0:T(1024)(128)(4,1)S(1)}, s32[]{:S(2)}) async-start(s8[5242880]{0:T(1024)(128)(4,1)} %bitcast.10), calls=%async_computation.5 | async-start | bytes 2097152
  33.9 7.4 %slice-start.5 = ((s8[5242880]{0:T(1024)(128)(4,1)}), s8[1048576]{0:T(1024)(128)(4,1)S(1)}, s32[]{:S(2)}) async-start(s8[5242880]{0:T(1024)(128)(4,1)} %bitcast.12), calls=%async_computation.7 | async-start | bytes 2097152
  34.0 7.4 %copy-start.1 = (f32[2048]{0:T(1024)S(1)}, f32[2048]{0:T(1024)}, u32[]{:S(2)}) copy-start(f32[2048]{0:T(1024)} %param.25) | copy-start | bytes 24580
  34.5 3.8 %collective-permute-start.2 = (bf16[4,2048]{1,0:T(4,128)(2,1)S(1)}, bf16[4,2048]{1,0:T(4,128)(2,1)S(1)}, u32[]{:S(2)}, u32[]{:S(2)}) collective-permute-start(bf16[4,2048]{1,0:T(4,128)(2,1)S(1)} %get-tuple-element.26), channel_id=1, source_target_pairs={{0,3},{1,0},{2,1},{3,2},{4,7},{5,4},{6,5},{7,6},{8,11},{9,8},{10,9... | collective-permute-start | bytes 49160 | tf_op jit(solution)/shard_map/ppermute | solution.py:573
  35.4 4.6 %collective-permute-start.1 = (bf16[4,2048]{1,0:T(4,128)(2,1)S(1)}, bf16[4,2048]{1,0:T(4,128)(2,1)S(1)}, u32[]{:S(2)}, u32[]{:S(2)}) collective-permute-start(bf16[4,2048]{1,0:T(4,128)(2,1)S(1)} %get-tuple-element.26), channel_id=1, source_target_pairs={{0,2},{1,3},{2,0},{3,1},{4,6},{5,7},{6,4},{7,5},{8,10},{9,11},{10,... | collective-permute-start | bytes 49160 | tf_op jit(solution)/shard_map/ppermute | solution.py:573
  35.8 5.5 %collective-permute-start = (bf16[4,2048]{1,0:T(4,128)(2,1)S(1)}, bf16[4,2048]{1,0:T(4,128)(2,1)S(1)}, u32[]{:S(2)}, u32[]{:S(2)}) collective-permute-start(bf16[4,2048]{1,0:T(4,128)(2,1)S(1)} %get-tuple-element.26), channel_id=1, source_target_pairs={{0,1},{1,2},{2,3},{3,0},{4,5},{5,6},{6,7},{7,4},{8,9},{9,10},{10,1... | collective-permute-start | bytes 49160 | tf_op jit(solution)/shard_map/ppermute | solution.py:573
  43.7 5.5 %collective-permute-start.3 = (bf16[1,2048]{1,0:T(2,128)(2,1)S(1)}, bf16[1,2048]{1,0:T(2,128)(2,1)S(1)}, u32[]{:S(2)}, u32[]{:S(2)}) collective-permute-start(bf16[1,2048]{1,0:T(2,128)(2,1)S(1)} %get-tuple-element.28), channel_id=1, source_target_pairs={{0,1},{1,2},{2,3},{3,0},{4,5},{5,6},{6,7},{7,4},{8,9},{9,10},{10,1... | collective-permute-start | bytes 12296 | tf_op jit(solution)/shard_map/ppermute | solution.py:573
  43.8 5.4 %collective-permute-start.4 = (bf16[1,2048]{1,0:T(2,128)(2,1)S(1)}, bf16[1,2048]{1,0:T(2,128)(2,1)S(1)}, u32[]{:S(2)}, u32[]{:S(2)}) collective-permute-start(bf16[1,2048]{1,0:T(2,128)(2,1)S(1)} %get-tuple-element.29), channel_id=1, source_target_pairs={{0,2},{1,3},{2,0},{3,1},{4,6},{5,7},{6,4},{7,5},{8,10},{9,11},{10,... | collective-permute-start | bytes 12296 | tf_op jit(solution)/shard_map/ppermute | solution.py:573
  45.6 4.2 %collective-permute-start.5 = (bf16[1,2048]{1,0:T(2,128)(2,1)S(1)}, bf16[1,2048]{1,0:T(2,128)(2,1)S(1)}, u32[]{:S(2)}, u32[]{:S(2)}) collective-permute-start(bf16[1,2048]{1,0:T(2,128)(2,1)S(1)} %get-tuple-element.30), channel_id=1, source_target_pairs={{0,3},{1,0},{2,1},{3,2},{4,7},{5,4},{6,5},{7,6},{8,11},{9,8},{10,9... | collective-permute-start | bytes 12296 | tf_op jit(solution)/shard_map/ppermute | solution.py:573

commit v4 on v3

--- a/solution.py
+++ b/solution.py
@@ -102,65 +102,21 @@
     return copy
 
 
-def project_kernel(
-    rows_hbm, gain_hbm, weight_hbm, out_ref, rows_ref, gain_ref, weight_ref, semaphores
+def find_pages(
+    table_ref,
+    length_ref,
+    order_ref,
+    frequency_ref,
+    query_gain_ref,
+    key_gain_ref,
+    query_cos_ref,
+    query_sin_ref,
+    key_cos_ref,
+    key_sin_ref,
+    row_ref,
+    valid_ref,
+    pages,
 ):
-    columns = weight_ref.shape[0]
-    chunk = up_to(columns // 4, 16)
-    first = [
-        copy_in(rows_hbm, rows_ref, semaphores.at[0]),
-        copy_in(gain_hbm, gain_ref, semaphores.at[1]),
-    ]
-    starts = range(0, columns, chunk)
-    copies = []
-    for index, start in enumerate(starts):
-        part = pl.ds(start, min(chunk, columns - start))
-        copies.append(
-            copy_in(weight_hbm.at[part], weight_ref.at[part], semaphores.at[2 + index])
-        )
-    for copy in first:
-        copy.wait()
-    normed = rms_scale(rows_ref[...].astype(F32), gain_ref[...], EPS_WIDE).astype(BF16)
-    devices, count, padded = out_ref.shape
-    if padded > columns:
-        out_ref[:, :, columns:] = jnp.zeros((devices, count, padded - columns), BF16)
-    for copy, start in zip(copies, starts):
-        copy.wait()
-        stop = min(start + chunk, columns)
-        packed = dot_rows(normed, weight_ref[start:stop])
-        out_ref[:, :, start:stop] = jnp.broadcast_to(
-            packed.astype(BF16)[None], (devices, count, stop - start)
-        )
-
-
-def lookup_kernel(*refs, pages):
-    sources, outputs, scratch = refs[:7], refs[7:14], refs[14:]
-    (
-        query_cos_ref,
-        query_sin_ref,
-        key_cos_ref,
-        key_sin_ref,
-        row_ref,
-        valid_ref,
-        page_ref,
-    ) = outputs
-    table_ref, length_ref, order_ref, frequency_ref, query_gain_ref, key_gain_ref = scratch[:6]
-    semaphores = scratch[6]
-    small = [
-        copy_in(source, target, semaphores.at[index])
-        for index, (source, target) in enumerate(zip(sources[:6], scratch[:6]))
-    ]
-    step = up_to(pages, 4) // 4
-    large = [
-        copy_in(
-            sources[6].at[pl.ds(start, step)],
-            page_ref.at[pl.ds(start, step)],
-            semaphores.at[6 + start // step],
-        )
-        for start in range(0, pages, step)
-    ]
-    for copy in small:
-        copy.wait()
     device = lax.axis_index("pool") * lax.axis_size("mp") + lax.axis_index("mp")
     slots = row_ref.shape[0]
     requests, blocks = table_ref.shape
@@ -205,8 +161,40 @@
         sin_ref[...] = sines * swap_halves(gain)[:1]
     row_ref[...] = jnp.broadcast_to(row, row_ref.shape)
     valid_ref[...] = jnp.broadcast_to(valid, valid_ref.shape)
-    for copy in large:
+
+
+def project_kernel(*refs, pages):
+    sources, outputs, rooms, semaphores = refs[:9], refs[9:16], refs[16:25], refs[25]
+    rows_ref, gain_ref, weight_ref = rooms[:3]
+    out_ref, *found = outputs
+    columns = weight_ref.shape[0]
+    chunk = up_to(columns // 4, 16)
+    first = [copy_in(sources[index], rooms[index], semaphores.at[index]) for index in (0, 1)]
+    starts = range(0, columns, chunk)
+    copies = []
+    for index, start in enumerate(starts):
+        part = pl.ds(start, min(chunk, columns - start))
+        copies.append(
+            copy_in(sources[2].at[part], weight_ref.at[part], semaphores.at[9 + index])
+        )
+    copies += [
+        copy_in(sources[index], rooms[index], semaphores.at[index]) for index in range(3, 9)
+    ]
+    for copy in first:
         copy.wait()
+    normed = rms_scale(rows_ref[...].astype(F32), gain_ref[...], EPS_WIDE).astype(BF16)
+    devices, count, padded = out_ref.shape
+    if padded > columns:
+        out_ref[:, :, columns:] = jnp.zeros((devices, count, padded - columns), BF16)
+    for copy in copies:
+        copy.wait()
+    for start in starts:
+        stop = min(start + chunk, columns)
+        packed = dot_rows(normed, weight_ref[start:stop])
+        out_ref[:, :, start:stop] = jnp.broadcast_to(
+            packed.astype(BF16)[None], (devices, count, stop - start)
+        )
+    find_pages(*rooms[3:], *found, pages)
 
 
 def attend_kernel(
@@ -304,6 +292,7 @@
         sublane_iota((8, wide)) < KVH
     )
     value_mask = value_mask & (sublane_iota((8, wide)) < KVH)
+    queue = []
     for slot in range(pages + 1):
         spread = jnp.concatenate(
             [
@@ -316,17 +305,19 @@
             ],
             axis=0,
         ).astype(BF16)
+        key_rows = page_ref[slot, :, :wide] if slot < pages else fresh_ref[:, :wide]
+        queue.append(dot_rows(spread, key_rows))
+    for slot, scores in enumerate(queue):
+        count = valid_ref[slot : slot + 1, : scores.shape[1]]
+        weights = jnp.where(lane_iota(scores.shape) < count, jnp.exp(scores), 0.0)
+        queue[slot] = weights.astype(BF16), jnp.sum(weights, axis=1, keepdims=True)
+    for slot, (weights, totals) in enumerate(queue):
         if slot < pages:
-            key_rows = page_ref[slot, :, :wide]
             value_rows = page_ref[slot, :, ENTRY - wide :]
         else:
-            key_rows = fresh_ref[:, :wide]
             value_rows = fresh_ref[:, ENTRY - wide :]
-        scores = dot_rows(spread, key_rows)
-        count = valid_ref[slot : slot + 1, : scores.shape[1]]
-        weights = jnp.where(lane_iota(scores.shape) < count, jnp.exp(scores), 0.0)
-        totals = jnp.sum(weights, axis=1, keepdims=True)
-        weighted = dot(weights.astype(BF16), value_rows)
+        queue[slot] = dot(weights, value_rows), totals
+    for slot, (weighted, totals) in enumerate(queue):
         for member in range(GROUPS):
             low = member * 8
             kept = jnp.where(value_mask, weighted[low : low + 8], 0.0)
@@ -451,10 +442,6 @@
 
 def far(*arrays):
     return [pltpu.with_memory_space_constraint(array, pltpu.HBM) for array in arrays]
-
-
-def near(*arrays):
-    return [pltpu.with_memory_space_constraint(array, pltpu.VMEM) for array in arrays]
 
 
 def room(array):
@@ -491,21 +478,10 @@
     exponent = np.arange(LANES) % (HD // 2) * (-2.0 / HD)
     frequency = jnp.asarray((10000.0**exponent).astype(np.float32)[None])
 
-    operands = (hidden_in, mix_gain[None], project_in.T)
-    packed = pl.pallas_call(
-        project_kernel,
-        out_shape=jax.ShapeDtypeStruct((devices, group_rows, padded), BF16),
-        in_specs=in_hbm(3),
-        out_specs=in_vmem(1)[0],
-        scratch_shapes=[room(x) for x in operands] + [pltpu.SemaphoreType.DMA((8,))],
-        compiler_params=params(8),
-        name="project",
-    )(*far(*operands))
-    packed = lax.all_to_all(packed, everyone, 0, 0, tiled=True)
-
-    table = jax.ShapeDtypeStruct((slots, LANES), F32)
-    index = jax.ShapeDtypeStruct((slots, LANES), I32)
     operands = (
+        hidden_in,
+        mix_gain[None],
+        project_in.T,
         page_table,
         lengths[None],
         row_order[None],
@@ -513,16 +489,27 @@
         query_gain[None],
         key_gain[None],
     )
-    *found, cached = pl.pallas_call(
-        lambda *refs: lookup_kernel(*refs, pages=pages),
-        out_shape=(table, table, table, table, index, index, room(page_cache)),
-        in_specs=in_hbm(7),
+    table = jax.ShapeDtypeStruct((slots, LANES), F32)
+    index = jax.ShapeDtypeStruct((slots, LANES), I32)
+    packed, *found = pl.pallas_call(
+        lambda *refs: project_kernel(*refs, pages=pages),
+        out_shape=(
+            jax.ShapeDtypeStruct((devices, group_rows, padded), BF16),
+            table,
+            table,
+            table,
+            table,
+            index,
+            index,
+        ),
+        in_specs=in_hbm(9),
         out_specs=in_vmem(7),
-        scratch_shapes=[room(x) for x in operands] + [pltpu.SemaphoreType.DMA((10,))],
+        scratch_shapes=[room(x) for x in operands] + [pltpu.SemaphoreType.DMA((16,))],
         compiler_params=params(8),
-        cost_estimate=cost(10_000_000),
-        name="lookup",
-    )(*far(*operands, page_cache))
+        cost_estimate=cost(10_000_000_000),
+        name="project",
+    )(*far(*operands))
+    packed = lax.all_to_all(packed, everyone, 0, 0, tiled=True)
 
     wide = up_to(KEYS, LANES)
     sums, new_entries = pl.pallas_call(
@@ -549,7 +536,7 @@
         name="attend",
     )(
         packed,
-        *near(cached),
+        page_cache,
         *found,
     )
     sums = lax.all_to_all(

time: 50.8 us -> 47.7 us (0.939)
  blocking collectives: 9.88 us -> 25.4 us
  starting transfers between devices: 13.6 us -> 6.3 us
  waiting for transfers between devices: 13.1 us -> 6.61 us
  Pallas kernels: 12.3 us -> 7.76 us
    all_to_all x0 -> x1, blocking collectives: none -> 15.5 us  [shards(): packed = lax.all_to_all(packed, everyone, 0, 0, tiled=True)]
    all_to_all x1 -> x0, starting transfers between devices: 7.3 us -> none  [shards(): packed = lax.all_to_all(packed, everyone, 0, 0, tiled=True)]
    all_to_all x1 -> x0, waiting for transfers between devices: 6.53 us -> none  [shards(): packed = lax.all_to_all(packed, everyone, 0, 0, tiled=True)]
    pallas_call x2 -> x1, Pallas kernels: 5.15 us -> 2.45 us  [shards(): pl.pallas_call(lambda *refs: project_kernel(*refs, pages=pages), out_shap...]
    pallas_call x1, Pallas kernels: 4.4 us -> 2.53 us  [shards(): pl.pallas_call(lambda *refs: attend_kernel(*refs, pool_count=pool_count,...]
  transfers between devices with their start and end apart: 7 -> 6, of which waited for: 6 -> 5; matrix products, arithmetic and copies ran while one was open for 0% -> 0% of each run, Pallas kernels for 4% -> 0%
where the time goes in v4:
time: 47.7 us; the launch traced here: 47.5 us
  blocking collectives  25.4 us (53%)
  Pallas kernels  7.76 us (16%)
  waiting for transfers between devices  6.61 us (14%)
  starting transfers between devices  6.3 us (13%)
  between operations  0.76 us (2%)
  other arithmetic  0.62 us (1%)
    all_to_all x1, blocking collectives, shards(): packed = lax.all_to_all(packed, everyone, 0, 0, tiled=True)  15.5 us
    all_to_all x1, blocking collectives, shards(): lax.all_to_all(sums.reshape(devices, group_rows, width), everyone, 0, 0,...  9.88 us
    ppermute x6, waiting for transfers between devices, ring(): lax.ppermute(value, 'mp', [(i, (i + step) % mp_count) for i in range(mp_c...  6.61 us
    ppermute x6, starting transfers between devices, ring(): lax.ppermute(value, 'mp', [(i, (i + step) % mp_count) for i in range(mp_c...  6.3 us
    pallas_call x1, Pallas kernels, shards(): pl.pallas_call(lambda *refs: attend_kernel(*refs, pool_count=pool_count,...  2.53 us
    pallas_call x1, Pallas kernels, shards(): pl.pallas_call(lambda *refs: project_kernel(*refs, pages=pages), out_shap...  2.45 us
    pallas_call x1, Pallas kernels, shards(): pl.pallas_call(lambda *refs: feed_kernel(*refs, steps=steps), out_shape=(...  2.26 us
  transfers between devices with their start and end apart: 6, of which 5 were waited for; matrix products, arithmetic and copies ran while one was open for 0% of the time, Pallas kernels for 0%

profile of v4, /device:TPU:0, one launch (start us, length us, event | category | flops | bytes accessed | tf_op | source)
XLA Modules:
  0.0 47.5 jit_solution(6956113287387951926)
XLA Ops:
  0.6 0.0 copy-start.1
  0.6 2.4 %project.1 = (bf16[32,4,512]{2,1,0:T(4,128)(2,1)S(1)}, f32[24,128]{1,0:T(8,128)S(1)}, f32[24,128]{1,0:T(8,128)S(1)}, f32[24,128]{1,0:T(8,128)S(1)}, f32[24,128]{...) custom-call(bf16[4,2048]{1,0:T(4,128)(2,1)} %hidden_ref.1, f32[1,2048]{1,0:T(1,128)} %bitcast.17, ...), custom_call_target="tpu_custom_call" | custom-call | flops 10000000000 | tf_op jit(solution)/shard_map/project/pallas_call | solution.py:494
  3.1 15.5 %all_to_all.10.refs_0_ = bf16[32,4,512]{2,1,0:T(4,128)(2,1)S(1)} all-to-all(bf16[32,4,512]{2,1,0:T(4,128)(2,1)S(1)} %get-tuple-element.17), channel_id=1, replica_groups=mesh['pool'=8,'mp'=4] {'pool','mp'}, dimensions={0} | all-to-all | bytes 262144 | tf_op jit(solution)/shard_map/all_to_all | solution.py:512
  18.6 0.0 copy-done.1
  18.6 0.0 slice-start.2
  18.6 0.0 slice-start.4
  18.7 2.5 %attend.1 = (bf16[8,4,4,384]{3,2,1,0:T(4,128)(2,1)S(1)}, bf16[1,640]{1,0:T(2,128)(2,1)}) custom-call(bf16[32,4,512]{2,1,0:T(4,128)(2,1)S(1)} %all_to_all.10.refs_0_, bf16[16,128,640]{2,1,0:T(8,128)(2,1)S(1)} %copy-done.1, f32[24,128]{1,0:T(8,128)S(1)} %get-tuple-element.18.refs_2_, f32[24,128]{1,0:T(8,128)S(1)} %get-tuple-element.19.refs_3_, ...), custom_call_target="tpu_custom_call" | custom-call | flops 20000000000 | tf_op jit(solution)/shard_map/attend/pallas_call | solution.py:515
  21.2 9.9 %all_to_all.11.sums_ref = bf16[32,4,384]{2,1,0:T(4,128)(2,1)S(1)} all-to-all(bf16[32,4,384]{2,1,0:T(4,128)(2,1)S(1)} %bitcast.14), channel_id=1, replica_groups=mesh['pool'=8,'mp'=4] {'pool','mp'}, dimensions={0} | all-to-all | bytes 196608 | tf_op jit(solution)/shard_map/all_to_all | solution.py:542
  31.1 0.5 %mix.1 = (f32[4,2048]{1,0:T(4,128)S(1)}, bf16[4,2048]{1,0:T(4,128)(2,1)S(1)}) custom-call(bf16[32,4,384]{2,1,0:T(4,128)(2,1)S(1)} %all_to_all.11.sums_ref, bf16[4,2048]{1,0:T(4,128)(2,1)S(1)} %copy-done.3, bf16[320,2048]{1,0:T(8,128)(2,1)S(1)} %copy-done.2), custom_call_target="tpu_custom_call" | custom-call | flops 20000000000 | tf_op jit(solution)/shard_map/mix/pallas_call | solution.py:546
  31.6 1.0 %collective-permute-start.2 = (bf16[4,2048]{1,0:T(4,128)(2,1)S(1)}, bf16[4,2048]{1,0:T(4,128)(2,1)S(1)}, u32[]{:S(2)}, u32[]{:S(2)}) collective-permute-start(bf16[4,2048]{1,0:T(4,128)(2,1)S(1)} %get-tuple-element.26), channel_id=1, source_target_pairs={{0,3},{1,0},{2,1},{3,2},{4,7},{5,4},{6,5},{7,6},{8,11},{9,8},{10,9... | collective-permute-start | bytes 49160 | tf_op jit(solution)/shard_map/ppermute | solution.py:560
  32.5 0.4 collective-permute-start.1
  32.9 1.1 %collective-permute-start = (bf16[4,2048]{1,0:T(4,128)(2,1)S(1)}, bf16[4,2048]{1,0:T(4,128)(2,1)S(1)}, u32[]{:S(2)}, u32[]{:S(2)}) collective-permute-start(bf16[4,2048]{1,0:T(4,128)(2,1)S(1)} %get-tuple-element.26), channel_id=1, source_target_pairs={{0,1},{1,2},{2,3},{3,0},{4,5},{5,6},{6,7},{7,4},{8,9},{9,10},{10,1... | collective-permute-start | bytes 49160 | tf_op jit(solution)/shard_map/ppermute | solution.py:560
  34.0 1.3 %collective-permute-done.2.refs_3_ = bf16[4,2048]{1,0:T(4,128)(2,1)S(1)} collective-permute-done((bf16[4,2048]{1,0:T(4,128)(2,1)S(1)}, bf16[4,2048]{1,0:T(4,128)(2,1)S(1)}, u32[]{:S(2)}, u32[]{:S(2)}) %collective-permute-start.2) | collective-permute-done | bytes 16416 | tf_op jit(solution)/shard_map/ppermute | solution.py:560
  35.4 1.8 %collective-permute-done.1.refs_2_ = bf16[4,2048]{1,0:T(4,128)(2,1)S(1)} collective-permute-done((bf16[4,2048]{1,0:T(4,128)(2,1)S(1)}, bf16[4,2048]{1,0:T(4,128)(2,1)S(1)}, u32[]{:S(2)}, u32[]{:S(2)}) %collective-permute-start.1) | collective-permute-done | bytes 16416 | tf_op jit(solution)/shard_map/ppermute | solution.py:560
  37.2 1.3 %collective-permute-done.refs_1_ = bf16[4,2048]{1,0:T(4,128)(2,1)S(1)} collective-permute-done((bf16[4,2048]{1,0:T(4,128)(2,1)S(1)}, bf16[4,2048]{1,0:T(4,128)(2,1)S(1)}, u32[]{:S(2)}, u32[]{:S(2)}) %collective-permute-start) | collective-permute-done | bytes 16416 | tf_op jit(solution)/shard_map/ppermute | solution.py:560
  38.5 0.0 slice-done.2
  38.5 2.3 %feed.1 = (f32[1,2048]{1,0:T(1,128)S(1)}, bf16[1,2048]{1,0:T(2,128)(2,1)S(1)}, bf16[1,2048]{1,0:T(2,128)(2,1)S(1)}, bf16[1,2048]{1,0:T(2,128)(2,1)S(1)}) custom-call(f32[4,2048]{1,0:T(4,128)S(1)} %get-tuple-element.25.refs_0_, bf16[4,2048]{1,0:T(4,128)(2,1)S(1)} %collective-permute-done.refs_1_, bf16[4,2048]{1,0:T(4,128)(2,1)S(1)} %collective-permute-done.1.refs_2_, ...), custom_call_target="tpu_custom_call" | custom-call | tf_op jit(solution)/shard_map/feed/pallas_call | solution.py:564
  40.8 0.1 collective-permute-start.3
  40.9 1.8 %collective-permute-start.4 = (bf16[1,2048]{1,0:T(2,128)(2,1)S(1)}, bf16[1,2048]{1,0:T(2,128)(2,1)S(1)}, u32[]{:S(2)}, u32[]{:S(2)}) collective-permute-start(bf16[1,2048]{1,0:T(2,128)(2,1)S(1)} %get-tuple-element.29), channel_id=1, source_target_pairs={{0,2},{1,3},{2,0},{3,1},{4,6},{5,7},{6,4},{7,5},{8,10},{9,11},{10,... | collective-permute-start | bytes 12296 | tf_op jit(solution)/shard_map/ppermute | solution.py:560
  42.7 2.0 %collective-permute-start.5 = (bf16[1,2048]{1,0:T(2,128)(2,1)S(1)}, bf16[1,2048]{1,0:T(2,128)(2,1)S(1)}, u32[]{:S(2)}, u32[]{:S(2)}) collective-permute-start(bf16[1,2048]{1,0:T(2,128)(2,1)S(1)} %get-tuple-element.30), channel_id=1, source_target_pairs={{0,3},{1,0},{2,1},{3,2},{4,7},{5,4},{6,5},{7,6},{8,11},{9,8},{10,9... | collective-permute-start | bytes 12296 | tf_op jit(solution)/shard_map/ppermute | solution.py:560
  44.7 1.6 %collective-permute-done.3 = bf16[1,2048]{1,0:T(2,128)(2,1)S(1)} collective-permute-done((bf16[1,2048]{1,0:T(2,128)(2,1)S(1)}, bf16[1,2048]{1,0:T(2,128)(2,1)S(1)}, u32[]{:S(2)}, u32[]{:S(2)}) %collective-permute-start.3) | collective-permute-done | bytes 4128 | tf_op jit(solution)/shard_map/ppermute | solution.py:560
  46.3 0.0 collective-permute-done.4
  46.3 0.6 %collective-permute-done.5 = bf16[1,2048]{1,0:T(2,128)(2,1)S(1)} collective-permute-done((bf16[1,2048]{1,0:T(2,128)(2,1)S(1)}, bf16[1,2048]{1,0:T(2,128)(2,1)S(1)}, u32[]{:S(2)}, u32[]{:S(2)}) %collective-permute-start.5) | collective-permute-done | bytes 4128 | tf_op jit(solution)/shard_map/ppermute | solution.py:560
  46.9 0.6 %add_convert_fusion = bf16[1,2048]{1,0:T(2,128)(2,1)} fusion(bf16[1,2048]{1,0:T(2,128)(2,1)S(1)} %collective-permute-done.5, bf16[1,2048]{1,0:T(2,128)(2,1)S(1)} %collective-permute-done.4, f32[1,2048]{1,0:T(1,128)S(1)} %get-tuple-element.27, bf16[1,2048]{1,0:T(2,128)(2,1)S(1)} %collective-permute-done.3), kind=kLoop, calls=%fused_computation | loop fusion | flops 14336 | bytes 24576 | tf_op jit(solution)/shard_map/convert_element_type | solution.py:576
  (18 shorter events, 0.0 us)
Async XLA Ops:
  0.6 18.0 %copy-start.1 = (bf16[16,128,640]{2,1,0:T(8,128)(2,1)S(1)}, bf16[16,128,640]{2,1,0:T(8,128)(2,1)}, u32[]{:S(2)}) copy-start(bf16[16,128,640]{2,1,0:T(8,128)(2,1)} %refs_1_.1) | copy-start | bytes 7864324
  18.6 12.5 %copy-start.2 = (bf16[320,2048]{1,0:T(8,128)(2,1)S(1)}, bf16[320,2048]{1,0:T(8,128)(2,1)}, u32[]{:S(2)}) copy-start(bf16[320,2048]{1,0:T(8,128)(2,1)} %weight_ref.1) | copy-start | bytes 3932164
  18.6 12.5 %copy-start.3 = (bf16[4,2048]{1,0:T(4,128)(2,1)S(1)}, bf16[4,2048]{1,0:T(4,128)(2,1)}, u32[]{:S(2)}) copy-start(bf16[4,2048]{1,0:T(4,128)(2,1)} %hidden_ref.1) | copy-start | bytes 49156
  18.6 19.8 %slice-start = ((s8[5242880]{0:T(1024)(128)(4,1)}), s8[4194304]{0:T(1024)(128)(4,1)S(1)}, s32[]{:S(2)}) async-start(s8[5242880]{0:T(1024)(128)(4,1)} %bitcast.8), calls=%async_computation.2 | async-start | bytes 8388608
  18.6 19.8 %slice-start.2 = ((s8[5242880]{0:T(1024)(128)(4,1)}), s8[4194304]{0:T(1024)(128)(4,1)S(1)}, s32[]{:S(2)}) async-start(s8[5242880]{0:T(1024)(128)(4,1)} %bitcast.10), calls=%async_computation.4 | async-start | bytes 8388608
  18.6 19.8 %slice-start.4 = ((s8[5242880]{0:T(1024)(128)(4,1)}), s8[4194304]{0:T(1024)(128)(4,1)S(1)}, s32[]{:S(2)}) async-start(s8[5242880]{0:T(1024)(128)(4,1)} %bitcast.12), calls=%async_computation.6 | async-start | bytes 8388608
  21.2 17.3 %slice-start.1 = ((s8[5242880]{0:T(1024)(128)(4,1)}), s8[1048576]{0:T(1024)(128)(4,1)S(1)}, s32[]{:S(2)}) async-start(s8[5242880]{0:T(1024)(128)(4,1)} %bitcast.8), calls=%async_computation.3 | async-start | bytes 2097152
  21.2 17.3 %slice-start.3 = ((s8[5242880]{0:T(1024)(128)(4,1)}), s8[1048576]{0:T(1024)(128)(4,1)S(1)}, s32[]{:S(2)}) async-start(s8[5242880]{0:T(1024)(128)(4,1)} %bitcast.10), calls=%async_computation.5 | async-start | bytes 2097152
  21.2 17.3 %slice-start.5 = ((s8[5242880]{0:T(1024)(128)(4,1)}), s8[1048576]{0:T(1024)(128)(4,1)S(1)}, s32[]{:S(2)}) async-start(s8[5242880]{0:T(1024)(128)(4,1)} %bitcast.12), calls=%async_computation.7 | async-start | bytes 2097152
  31.1 7.4 %copy-start = (f32[2048]{0:T(1024)S(1)}, f32[2048]{0:T(1024)}, u32[]{:S(2)}) copy-start(f32[2048]{0:T(1024)} %param.25) | copy-start | bytes 24580
  31.6 3.8 %collective-permute-start.2 = (bf16[4,2048]{1,0:T(4,128)(2,1)S(1)}, bf16[4,2048]{1,0:T(4,128)(2,1)S(1)}, u32[]{:S(2)}, u32[]{:S(2)}) collective-permute-start(bf16[4,2048]{1,0:T(4,128)(2,1)S(1)} %get-tuple-element.26), channel_id=1, source_target_pairs={{0,3},{1,0},{2,1},{3,2},{4,7},{5,4},{6,5},{7,6},{8,11},{9,8},{10,9... | collective-permute-start | bytes 49160 | tf_op jit(solution)/shard_map/ppermute | solution.py:560
  32.5 4.6 %collective-permute-start.1 = (bf16[4,2048]{1,0:T(4,128)(2,1)S(1)}, bf16[4,2048]{1,0:T(4,128)(2,1)S(1)}, u32[]{:S(2)}, u32[]{:S(2)}) collective-permute-start(bf16[4,2048]{1,0:T(4,128)(2,1)S(1)} %get-tuple-element.26), channel_id=1, source_target_pairs={{0,2},{1,3},{2,0},{3,1},{4,6},{5,7},{6,4},{7,5},{8,10},{9,11},{10,... | collective-permute-start | bytes 49160 | tf_op jit(solution)/shard_map/ppermute | solution.py:560
  32.9 5.5 %collective-permute-start = (bf16[4,2048]{1,0:T(4,128)(2,1)S(1)}, bf16[4,2048]{1,0:T(4,128)(2,1)S(1)}, u32[]{:S(2)}, u32[]{:S(2)}) collective-permute-start(bf16[4,2048]{1,0:T(4,128)(2,1)S(1)} %get-tuple-element.26), channel_id=1, source_target_pairs={{0,1},{1,2},{2,3},{3,0},{4,5},{5,6},{6,7},{7,4},{8,9},{9,10},{10,1... | collective-permute-start | bytes 49160 | tf_op jit(solution)/shard_map/ppermute | solution.py:560
  40.8 5.5 %collective-permute-start.3 = (bf16[1,2048]{1,0:T(2,128)(2,1)S(1)}, bf16[1,2048]{1,0:T(2,128)(2,1)S(1)}, u32[]{:S(2)}, u32[]{:S(2)}) collective-permute-start(bf16[1,2048]{1,0:T(2,128)(2,1)S(1)} %get-tuple-element.28), channel_id=1, source_target_pairs={{0,1},{1,2},{2,3},{3,0},{4,5},{5,6},{6,7},{7,4},{8,9},{9,10},{10,1... | collective-permute-start | bytes 12296 | tf_op jit(solution)/shard_map/ppermute | solution.py:560
  40.9 5.4 %collective-permute-start.4 = (bf16[1,2048]{1,0:T(2,128)(2,1)S(1)}, bf16[1,2048]{1,0:T(2,128)(2,1)S(1)}, u32[]{:S(2)}, u32[]{:S(2)}) collective-permute-start(bf16[1,2048]{1,0:T(2,128)(2,1)S(1)} %get-tuple-element.29), channel_id=1, source_target_pairs={{0,2},{1,3},{2,0},{3,1},{4,6},{5,7},{6,4},{7,5},{8,10},{9,11},{10,... | collective-permute-start | bytes 12296 | tf_op jit(solution)/shard_map/ppermute | solution.py:560
  42.7 4.2 %collective-permute-start.5 = (bf16[1,2048]{1,0:T(2,128)(2,1)S(1)}, bf16[1,2048]{1,0:T(2,128)(2,1)S(1)}, u32[]{:S(2)}, u32[]{:S(2)}) collective-permute-start(bf16[1,2048]{1,0:T(2,128)(2,1)S(1)} %get-tuple-element.30), channel_id=1, source_target_pairs={{0,3},{1,0},{2,1},{3,2},{4,7},{5,4},{6,5},{7,6},{8,11},{9,8},{10,9... | collective-permute-start | bytes 12296 | tf_op jit(solution)/shard_map/ppermute | solution.py:560

commit v5 on v4

--- a/solution.py
+++ b/solution.py
@@ -559,8 +559,14 @@
     def ring(value, step):
         return lax.ppermute(value, "mp", [(i, (i + step) % mp_count) for i in range(mp_count)])
 
+    def swap(value, step):
+        if mp_count & (mp_count - 1):
+            return ring(value, step)
+        step ^= step >> 1
+        return lax.ppermute(value, "mp", [(i, i ^ step) for i in range(mp_count)])
+
     steps = mp_count - 1
-    arrived = [ring(sent, step) for step in range(1, mp_count)]
+    arrived = [swap(sent, step) for step in range(1, mp_count)]
     base, *rows = pl.pallas_call(
         lambda *refs: feed_kernel(*refs, steps=steps),
         out_shape=(jax.ShapeDtypeStruct((1, model), F32),)

time: 47.7 us -> 47 us (0.985)
  waiting for transfers between devices: 6.61 us -> 4.86 us
  starting transfers between devices: 6.3 us -> 7.39 us
    ppermute x6 -> x3, waiting for transfers between devices: 6.61 us -> 2.24 us  [ring(): lax.ppermute(value, 'mp', [(i, (i + step) % mp_count) for i in range(mp_c...]
    ppermute x0 -> x3, starting transfers between devices: none -> 3.51 us  [swap(): return lax.ppermute(value, 'mp', [(i, i ^ step) for i in range(mp_count)])]
    ppermute x0 -> x3, waiting for transfers between devices: none -> 2.62 us  [swap(): return lax.ppermute(value, 'mp', [(i, i ^ step) for i in range(mp_count)])]
    ppermute x6 -> x3, starting transfers between devices: 6.3 us -> 3.88 us  [ring(): lax.ppermute(value, 'mp', [(i, (i + step) % mp_count) for i in range(mp_c...]
  transfers between devices with their start and end apart: 6 -> 6, of which waited for: 5 -> 6; matrix products, arithmetic and copies ran while one was open for 0% -> 0% of each run, Pallas kernels for 0% -> 0%
where the time goes in v5:
time: 47 us; the launch traced here: 46.8 us
  blocking collectives  25.4 us (54%)
  Pallas kernels  7.76 us (17%)
  starting transfers between devices  7.39 us (16%)
  waiting for transfers between devices  4.86 us (10%)
  between operations  0.75 us (2%)
  other arithmetic  0.62 us (1%)
    all_to_all x1, blocking collectives, shards(): packed = lax.all_to_all(packed, everyone, 0, 0, tiled=True)  15.5 us
    all_to_all x1, blocking collectives, shards(): lax.all_to_all(sums.reshape(devices, group_rows, width), everyone, 0, 0,...  9.88 us
    ppermute x3, starting transfers between devices, ring(): lax.ppermute(value, 'mp', [(i, (i + step) % mp_count) for i in range(mp_c...  3.88 us
    ppermute x3, starting transfers between devices, swap(): return lax.ppermute(value, 'mp', [(i, i ^ step) for i in range(mp_count)])  3.51 us
    ppermute x3, waiting for transfers between devices, swap(): return lax.ppermute(value, 'mp', [(i, i ^ step) for i in range(mp_count)])  2.62 us
    pallas_call x1, Pallas kernels, shards(): pl.pallas_call(lambda *refs: attend_kernel(*refs, pool_count=pool_count,...  2.53 us
    pallas_call x1, Pallas kernels, shards(): pl.pallas_call(lambda *refs: project_kernel(*refs, pages=pages), out_shap...  2.45 us
    pallas_call x1, Pallas kernels, shards(): pl.pallas_call(lambda *refs: feed_kernel(*refs, steps=steps), out_shape=(...  2.26 us
  transfers between devices with their start and end apart: 6, of which 6 were waited for; matrix products, arithmetic and copies ran while one was open for 0% of the time, Pallas kernels for 0%

profile of v5, /device:TPU:0, one launch (start us, length us, event | category | flops | bytes accessed | tf_op | source)
XLA Modules:
  0.0 46.8 jit_solution(17023377094079966548)
XLA Ops:
  0.6 0.0 copy-start.1
  0.6 2.4 %project.1 = (bf16[32,4,512]{2,1,0:T(4,128)(2,1)S(1)}, f32[24,128]{1,0:T(8,128)S(1)}, f32[24,128]{1,0:T(8,128)S(1)}, f32[24,128]{1,0:T(8,128)S(1)}, f32[24,128]{...) custom-call(bf16[4,2048]{1,0:T(4,128)(2,1)} %hidden_ref.1, f32[1,2048]{1,0:T(1,128)} %bitcast.17, ...), custom_call_target="tpu_custom_call" | custom-call | flops 10000000000 | tf_op jit(solution)/shard_map/project/pallas_call | solution.py:494
  3.1 15.5 %all_to_all.10.refs_0_ = bf16[32,4,512]{2,1,0:T(4,128)(2,1)S(1)} all-to-all(bf16[32,4,512]{2,1,0:T(4,128)(2,1)S(1)} %get-tuple-element.17), channel_id=1, replica_groups=mesh['pool'=8,'mp'=4] {'pool','mp'}, dimensions={0} | all-to-all | bytes 262144 | tf_op jit(solution)/shard_map/all_to_all | solution.py:512
  18.6 0.0 copy-done.1
  18.6 0.0 slice-start.2
  18.6 0.0 slice-start.4
  18.7 2.5 %attend.1 = (bf16[8,4,4,384]{3,2,1,0:T(4,128)(2,1)S(1)}, bf16[1,640]{1,0:T(2,128)(2,1)}) custom-call(bf16[32,4,512]{2,1,0:T(4,128)(2,1)S(1)} %all_to_all.10.refs_0_, bf16[16,128,640]{2,1,0:T(8,128)(2,1)S(1)} %copy-done.1, f32[24,128]{1,0:T(8,128)S(1)} %get-tuple-element.18.refs_2_, f32[24,128]{1,0:T(8,128)S(1)} %get-tuple-element.19.refs_3_, ...), custom_call_target="tpu_custom_call" | custom-call | flops 20000000000 | tf_op jit(solution)/shard_map/attend/pallas_call | solution.py:515
  21.2 9.9 %all_to_all.11.sums_ref = bf16[32,4,384]{2,1,0:T(4,128)(2,1)S(1)} all-to-all(bf16[32,4,384]{2,1,0:T(4,128)(2,1)S(1)} %bitcast.14), channel_id=1, replica_groups=mesh['pool'=8,'mp'=4] {'pool','mp'}, dimensions={0} | all-to-all | bytes 196608 | tf_op jit(solution)/shard_map/all_to_all | solution.py:542
  31.1 0.5 %mix.1 = (f32[4,2048]{1,0:T(4,128)S(1)}, bf16[4,2048]{1,0:T(4,128)(2,1)S(1)}) custom-call(bf16[32,4,384]{2,1,0:T(4,128)(2,1)S(1)} %all_to_all.11.sums_ref, bf16[4,2048]{1,0:T(4,128)(2,1)S(1)} %copy-done.3, bf16[320,2048]{1,0:T(8,128)(2,1)S(1)} %copy-done.2), custom_call_target="tpu_custom_call" | custom-call | flops 20000000000 | tf_op jit(solution)/shard_map/mix/pallas_call | solution.py:546
  31.6 0.4 collective-permute-start.2
  32.0 1.8 %collective-permute-start.1 = (bf16[4,2048]{1,0:T(4,128)(2,1)S(1)}, bf16[4,2048]{1,0:T(4,128)(2,1)S(1)}, u32[]{:S(2)}, u32[]{:S(2)}) collective-permute-start(bf16[4,2048]{1,0:T(4,128)(2,1)S(1)} %get-tuple-element.26), channel_id=1, source_target_pairs={{0,3},{1,2},{2,1},{3,0},{4,7},{5,6},{6,5},{7,4},{8,11},{9,10},{10,... | collective-permute-start | bytes 49160 | tf_op jit(solution)/shard_map/ppermute | solution.py:566
  33.8 1.3 %collective-permute-start = (bf16[4,2048]{1,0:T(4,128)(2,1)S(1)}, bf16[4,2048]{1,0:T(4,128)(2,1)S(1)}, u32[]{:S(2)}, u32[]{:S(2)}) collective-permute-start(bf16[4,2048]{1,0:T(4,128)(2,1)S(1)} %get-tuple-element.26), channel_id=1, source_target_pairs={{0,1},{1,0},{2,3},{3,2},{4,5},{5,4},{6,7},{7,6},{8,9},{9,8},{10,11... | collective-permute-start | bytes 49160 | tf_op jit(solution)/shard_map/ppermute | solution.py:566
  35.1 1.1 %collective-permute-done.2.refs_3_ = bf16[4,2048]{1,0:T(4,128)(2,1)S(1)} collective-permute-done((bf16[4,2048]{1,0:T(4,128)(2,1)S(1)}, bf16[4,2048]{1,0:T(4,128)(2,1)S(1)}, u32[]{:S(2)}, u32[]{:S(2)}) %collective-permute-start.2) | collective-permute-done | bytes 16416 | tf_op jit(solution)/shard_map/ppermute | solution.py:566
  36.3 1.3 %collective-permute-done.1.refs_2_ = bf16[4,2048]{1,0:T(4,128)(2,1)S(1)} collective-permute-done((bf16[4,2048]{1,0:T(4,128)(2,1)S(1)}, bf16[4,2048]{1,0:T(4,128)(2,1)S(1)}, u32[]{:S(2)}, u32[]{:S(2)}) %collective-permute-start.1) | collective-permute-done | bytes 16416 | tf_op jit(solution)/shard_map/ppermute | solution.py:566
  37.6 0.2 collective-permute-done.refs_1_
  37.7 0.0 slice-done
  37.8 2.3 %feed.1 = (f32[1,2048]{1,0:T(1,128)S(1)}, bf16[1,2048]{1,0:T(2,128)(2,1)S(1)}, bf16[1,2048]{1,0:T(2,128)(2,1)S(1)}, bf16[1,2048]{1,0:T(2,128)(2,1)S(1)}) custom-call(f32[4,2048]{1,0:T(4,128)S(1)} %get-tuple-element.25.refs_0_, bf16[4,2048]{1,0:T(4,128)(2,1)S(1)} %collective-permute-done.refs_1_, bf16[4,2048]{1,0:T(4,128)(2,1)S(1)} %collective-permute-done.1.refs_2_, ...), custom_call_target="tpu_custom_call" | custom-call | tf_op jit(solution)/shard_map/feed/pallas_call | solution.py:570
  40.1 1.2 %collective-permute-start.3 = (bf16[1,2048]{1,0:T(2,128)(2,1)S(1)}, bf16[1,2048]{1,0:T(2,128)(2,1)S(1)}, u32[]{:S(2)}, u32[]{:S(2)}) collective-permute-start(bf16[1,2048]{1,0:T(2,128)(2,1)S(1)} %get-tuple-element.28), channel_id=1, source_target_pairs={{0,1},{1,2},{2,3},{3,0},{4,5},{5,6},{6,7},{7,4},{8,9},{9,10},{10,1... | collective-permute-start | bytes 12296 | tf_op jit(solution)/shard_map/ppermute | solution.py:560
  41.2 1.3 %collective-permute-start.4 = (bf16[1,2048]{1,0:T(2,128)(2,1)S(1)}, bf16[1,2048]{1,0:T(2,128)(2,1)S(1)}, u32[]{:S(2)}, u32[]{:S(2)}) collective-permute-start(bf16[1,2048]{1,0:T(2,128)(2,1)S(1)} %get-tuple-element.29), channel_id=1, source_target_pairs={{0,2},{1,3},{2,0},{3,1},{4,6},{5,7},{6,4},{7,5},{8,10},{9,11},{10,... | collective-permute-start | bytes 12296 | tf_op jit(solution)/shard_map/ppermute | solution.py:560
  42.5 1.4 %collective-permute-start.5 = (bf16[1,2048]{1,0:T(2,128)(2,1)S(1)}, bf16[1,2048]{1,0:T(2,128)(2,1)S(1)}, u32[]{:S(2)}, u32[]{:S(2)}) collective-permute-start(bf16[1,2048]{1,0:T(2,128)(2,1)S(1)} %get-tuple-element.30), channel_id=1, source_target_pairs={{0,3},{1,0},{2,1},{3,2},{4,7},{5,4},{6,5},{7,6},{8,11},{9,8},{10,9... | collective-permute-start | bytes 12296 | tf_op jit(solution)/shard_map/ppermute | solution.py:560
  44.0 1.6 %collective-permute-done.3 = bf16[1,2048]{1,0:T(2,128)(2,1)S(1)} collective-permute-done((bf16[1,2048]{1,0:T(2,128)(2,1)S(1)}, bf16[1,2048]{1,0:T(2,128)(2,1)S(1)}, u32[]{:S(2)}, u32[]{:S(2)}) %collective-permute-start.3) | collective-permute-done | bytes 4128 | tf_op jit(solution)/shard_map/ppermute | solution.py:560
  45.6 0.2 collective-permute-done.4
  45.8 0.4 collective-permute-done.5
  46.2 0.6 %add_convert_fusion = bf16[1,2048]{1,0:T(2,128)(2,1)} fusion(bf16[1,2048]{1,0:T(2,128)(2,1)S(1)} %collective-permute-done.5, bf16[1,2048]{1,0:T(2,128)(2,1)S(1)} %collective-permute-done.4, f32[1,2048]{1,0:T(1,128)S(1)} %get-tuple-element.27, bf16[1,2048]{1,0:T(2,128)(2,1)S(1)} %collective-permute-done.3), kind=kLoop, calls=%fused_computation | loop fusion | flops 14336 | bytes 24576 | tf_op jit(solution)/shard_map/convert_element_type | solution.py:582
  (18 shorter events, 0.0 us)
Async XLA Ops:
  0.6 18.0 %copy-start.1 = (bf16[16,128,640]{2,1,0:T(8,128)(2,1)S(1)}, bf16[16,128,640]{2,1,0:T(8,128)(2,1)}, u32[]{:S(2)}) copy-start(bf16[16,128,640]{2,1,0:T(8,128)(2,1)} %refs_1_.1) | copy-start | bytes 7864324
  18.6 12.5 %copy-start.2 = (bf16[320,2048]{1,0:T(8,128)(2,1)S(1)}, bf16[320,2048]{1,0:T(8,128)(2,1)}, u32[]{:S(2)}) copy-start(bf16[320,2048]{1,0:T(8,128)(2,1)} %weight_ref.1) | copy-start | bytes 3932164
  18.6 12.5 %copy-start.3 = (bf16[4,2048]{1,0:T(4,128)(2,1)S(1)}, bf16[4,2048]{1,0:T(4,128)(2,1)}, u32[]{:S(2)}) copy-start(bf16[4,2048]{1,0:T(4,128)(2,1)} %hidden_ref.1) | copy-start | bytes 49156
  18.6 19.1 %slice-start = ((s8[5242880]{0:T(1024)(128)(4,1)}), s8[4194304]{0:T(1024)(128)(4,1)S(1)}, s32[]{:S(2)}) async-start(s8[5242880]{0:T(1024)(128)(4,1)} %bitcast.8), calls=%async_computation.2 | async-start | bytes 8388608
  18.6 19.1 %slice-start.2 = ((s8[5242880]{0:T(1024)(128)(4,1)}), s8[4194304]{0:T(1024)(128)(4,1)S(1)}, s32[]{:S(2)}) async-start(s8[5242880]{0:T(1024)(128)(4,1)} %bitcast.10), calls=%async_computation.4 | async-start | bytes 8388608
  18.6 19.1 %slice-start.4 = ((s8[5242880]{0:T(1024)(128)(4,1)}), s8[4194304]{0:T(1024)(128)(4,1)S(1)}, s32[]{:S(2)}) async-start(s8[5242880]{0:T(1024)(128)(4,1)} %bitcast.12), calls=%async_computation.6 | async-start | bytes 8388608
  21.2 16.6 %slice-start.1 = ((s8[5242880]{0:T(1024)(128)(4,1)}), s8[1048576]{0:T(1024)(128)(4,1)S(1)}, s32[]{:S(2)}) async-start(s8[5242880]{0:T(1024)(128)(4,1)} %bitcast.8), calls=%async_computation.3 | async-start | bytes 2097152
  21.2 16.6 %slice-start.3 = ((s8[5242880]{0:T(1024)(128)(4,1)}), s8[1048576]{0:T(1024)(128)(4,1)S(1)}, s32[]{:S(2)}) async-start(s8[5242880]{0:T(1024)(128)(4,1)} %bitcast.10), calls=%async_computation.5 | async-start | bytes 2097152
  21.2 16.6 %slice-start.5 = ((s8[5242880]{0:T(1024)(128)(4,1)}), s8[1048576]{0:T(1024)(128)(4,1)S(1)}, s32[]{:S(2)}) async-start(s8[5242880]{0:T(1024)(128)(4,1)} %bitcast.12), calls=%async_computation.7 | async-start | bytes 2097152
  31.1 6.7 %copy-start = (f32[2048]{0:T(1024)S(1)}, f32[2048]{0:T(1024)}, u32[]{:S(2)}) copy-start(f32[2048]{0:T(1024)} %param.25) | copy-start | bytes 24580
  31.6 4.7 %collective-permute-start.2 = (bf16[4,2048]{1,0:T(4,128)(2,1)S(1)}, bf16[4,2048]{1,0:T(4,128)(2,1)S(1)}, u32[]{:S(2)}, u32[]{:S(2)}) collective-permute-start(bf16[4,2048]{1,0:T(4,128)(2,1)S(1)} %get-tuple-element.26), channel_id=1, source_target_pairs={{0,2},{1,3},{2,0},{3,1},{4,6},{5,7},{6,4},{7,5},{8,10},{9,11},{10,... | collective-permute-start | bytes 49160 | tf_op jit(solution)/shard_map/ppermute | solution.py:566
  32.0 5.6 %collective-permute-start.1 = (bf16[4,2048]{1,0:T(4,128)(2,1)S(1)}, bf16[4,2048]{1,0:T(4,128)(2,1)S(1)}, u32[]{:S(2)}, u32[]{:S(2)}) collective-permute-start(bf16[4,2048]{1,0:T(4,128)(2,1)S(1)} %get-tuple-element.26), channel_id=1, source_target_pairs={{0,3},{1,2},{2,1},{3,0},{4,7},{5,6},{6,5},{7,4},{8,11},{9,10},{10,... | collective-permute-start | bytes 49160 | tf_op jit(solution)/shard_map/ppermute | solution.py:566
  33.8 3.9 %collective-permute-start = (bf16[4,2048]{1,0:T(4,128)(2,1)S(1)}, bf16[4,2048]{1,0:T(4,128)(2,1)S(1)}, u32[]{:S(2)}, u32[]{:S(2)}) collective-permute-start(bf16[4,2048]{1,0:T(4,128)(2,1)S(1)} %get-tuple-element.26), channel_id=1, source_target_pairs={{0,1},{1,0},{2,3},{3,2},{4,5},{5,4},{6,7},{7,6},{8,9},{9,8},{10,11... | collective-permute-start | bytes 49160 | tf_op jit(solution)/shard_map/ppermute | solution.py:566
  40.1 5.5 %collective-permute-start.3 = (bf16[1,2048]{1,0:T(2,128)(2,1)S(1)}, bf16[1,2048]{1,0:T(2,128)(2,1)S(1)}, u32[]{:S(2)}, u32[]{:S(2)}) collective-permute-start(bf16[1,2048]{1,0:T(2,128)(2,1)S(1)} %get-tuple-element.28), channel_id=1, source_target_pairs={{0,1},{1,2},{2,3},{3,0},{4,5},{5,6},{6,7},{7,4},{8,9},{9,10},{10,1... | collective-permute-start | bytes 12296 | tf_op jit(solution)/shard_map/ppermute | solution.py:560
  41.2 4.5 %collective-permute-start.4 = (bf16[1,2048]{1,0:T(2,128)(2,1)S(1)}, bf16[1,2048]{1,0:T(2,128)(2,1)S(1)}, u32[]{:S(2)}, u32[]{:S(2)}) collective-permute-start(bf16[1,2048]{1,0:T(2,128)(2,1)S(1)} %get-tuple-element.29), channel_id=1, source_target_pairs={{0,2},{1,3},{2,0},{3,1},{4,6},{5,7},{6,4},{7,5},{8,10},{9,11},{10,... | collective-permute-start | bytes 12296 | tf_op jit(solution)/shard_map/ppermute | solution.py:560
  42.5 3.7 %collective-permute-start.5 = (bf16[1,2048]{1,0:T(2,128)(2,1)S(1)}, bf16[1,2048]{1,0:T(2,128)(2,1)S(1)}, u32[]{:S(2)}, u32[]{:S(2)}) collective-permute-start(bf16[1,2048]{1,0:T(2,128)(2,1)S(1)} %get-tuple-element.30), channel_id=1, source_target_pairs={{0,3},{1,0},{2,1},{3,2},{4,7},{5,4},{6,5},{7,6},{8,11},{9,8},{10,9... | collective-permute-start | bytes 12296 | tf_op jit(solution)/shard_map/ppermute | solution.py:560

commit v6 on v5

--- a/solution.py
+++ b/solution.py
@@ -245,10 +245,12 @@
     tiles = [lane_tile(part_tile, t * LANES, part_source) for t in range(tile_count)]
     stacked = jnp.concatenate(tiles[: query_tiles + key_tiles], axis=0)
     ones = jnp.where(
-        sublane_iota((LANES, LANES)) // HD == lane_iota((LANES, LANES)) // HD, 1.0, 0.0
+        sublane_iota((2 * LANES, LANES)) % LANES // HD == lane_iota((2 * LANES, LANES)) // HD,
+        1.0,
+        0.0,
     ).astype(BF16)
-    high, low = two_halves(stacked * stacked)
-    scale = lax.rsqrt((dot(high, ones) + dot(low, ones)) * (1.0 / HD) + EPS_HEAD)
+    squares = jnp.concatenate(two_halves(stacked * stacked), axis=1)
+    scale = lax.rsqrt(dot(squares, ones) * (1.0 / HD) + EPS_HEAD)
     swapped = swap_halves(stacked)
     split = query_tiles * slots
 
@@ -322,9 +324,9 @@
             low = member * 8
             kept = jnp.where(value_mask, weighted[low : low + 8], 0.0)
             kept = jnp.where(total_mask, totals[low : low + 8], kept)
-            partial_ref[member, slot * 8 : slot * 8 + 8, :] = kept
-
-    depth = partial_ref.shape[1]
+            partial_ref[slot * 8 : slot * 8 + 8, member * wide : (member + 1) * wide] = kept
+
+    depth = partial_ref.shape[0]
     spread_row = jnp.sum(
         jnp.where(
             lane_iota((slots, depth)) // 8 == sublane_iota((slots, depth)),
@@ -337,10 +339,9 @@
     place = sublane_iota((pool_count * 8, depth))
     place = place // 8 * group_rows + place % group_rows
     collect = jnp.where(place == spread_row, 1.0, 0.0).astype(BF16)
-    summed = []
-    for member in range(GROUPS):
-        high, low = two_halves(partial_ref[member])
-        summed.append(dot(collect, high) + dot(collect, low))
+    high, low = two_halves(partial_ref[...])
+    collected = dot(collect, high) + dot(collect, low)
+    summed = [collected[:, member * wide : (member + 1) * wide] for member in range(GROUPS)]
     first = lane_iota((pool_count * 8, LANES)) < KVH
     totals = None
     for member in range(GROUPS):
@@ -529,7 +530,7 @@
         scratch_shapes=[
             pltpu.VMEM((GROUPS, slots, wide), F32),
             pltpu.VMEM((16, ENTRY), BF16),
-            pltpu.VMEM((GROUPS, (pages + 1) * 8, wide), F32),
+            pltpu.VMEM(((pages + 1) * 8, GROUPS * wide), F32),
         ],
         compiler_params=params(16),
         cost_estimate=cost(20_000_000_000),

time: 47 us -> 46.9 us (level)
  no operation moved by 1% of the time
where the time goes in v6:
time: 46.9 us; the launch traced here: 46.7 us
  blocking collectives  25.4 us (54%)
  Pallas kernels  7.68 us (16%)
  starting transfers between devices  7.39 us (16%)
  waiting for transfers between devices  4.86 us (10%)
  between operations  0.75 us (2%)
  other arithmetic  0.62 us (1%)
    all_to_all x1, blocking collectives, shards(): packed = lax.all_to_all(packed, everyone, 0, 0, tiled=True)  15.5 us
    all_to_all x1, blocking collectives, shards(): lax.all_to_all(sums.reshape(devices, group_rows, width), everyone, 0, 0,...  9.88 us
    ppermute x3, starting transfers between devices, ring(): lax.ppermute(value, 'mp', [(i, (i + step) % mp_count) for i in range(mp_c...  3.88 us
    ppermute x3, starting transfers between devices, swap(): return lax.ppermute(value, 'mp', [(i, i ^ step) for i in range(mp_count)])  3.51 us
    ppermute x3, waiting for transfers between devices, swap(): return lax.ppermute(value, 'mp', [(i, i ^ step) for i in range(mp_count)])  2.62 us
    pallas_call x1, Pallas kernels, shards(): pl.pallas_call(lambda *refs: attend_kernel(*refs, pool_count=pool_count,...  2.46 us
    pallas_call x1, Pallas kernels, shards(): pl.pallas_call(lambda *refs: project_kernel(*refs, pages=pages), out_shap...  2.45 us
    pallas_call x1, Pallas kernels, shards(): pl.pallas_call(lambda *refs: feed_kernel(*refs, steps=steps), out_shape=(...  2.26 us
  transfers between devices with their start and end apart: 6, of which 6 were waited for; matrix products, arithmetic and copies ran while one was open for 0% of the time, Pallas kernels for 0%

profile of v6, /device:TPU:0, one launch (start us, length us, event | category | flops | bytes accessed | tf_op | source)
XLA Modules:
  0.0 46.7 jit_solution(8358378745715347583)
XLA Ops:
  0.6 0.0 copy-start.1
  0.6 2.4 %project.1 = (bf16[32,4,512]{2,1,0:T(4,128)(2,1)S(1)}, f32[24,128]{1,0:T(8,128)S(1)}, f32[24,128]{1,0:T(8,128)S(1)}, f32[24,128]{1,0:T(8,128)S(1)}, f32[24,128]{...) custom-call(bf16[4,2048]{1,0:T(4,128)(2,1)} %hidden_ref.1, f32[1,2048]{1,0:T(1,128)} %bitcast.17, ...), custom_call_target="tpu_custom_call" | custom-call | flops 10000000000 | tf_op jit(solution)/shard_map/project/pallas_call | solution.py:495
  3.1 15.5 %all_to_all.10.refs_0_ = bf16[32,4,512]{2,1,0:T(4,128)(2,1)S(1)} all-to-all(bf16[32,4,512]{2,1,0:T(4,128)(2,1)S(1)} %get-tuple-element.17), channel_id=1, replica_groups=mesh['pool'=8,'mp'=4] {'pool','mp'}, dimensions={0} | all-to-all | bytes 262144 | tf_op jit(solution)/shard_map/all_to_all | solution.py:513
  18.6 0.0 copy-done.1
  18.6 0.0 slice-start.2
  18.6 0.0 slice-start.4
  18.7 2.5 %attend.1 = (bf16[8,4,4,384]{3,2,1,0:T(4,128)(2,1)S(1)}, bf16[1,640]{1,0:T(2,128)(2,1)}) custom-call(bf16[32,4,512]{2,1,0:T(4,128)(2,1)S(1)} %all_to_all.10.refs_0_, bf16[16,128,640]{2,1,0:T(8,128)(2,1)S(1)} %copy-done.1, f32[24,128]{1,0:T(8,128)S(1)} %get-tuple-element.18.refs_2_, f32[24,128]{1,0:T(8,128)S(1)} %get-tuple-element.19.refs_3_, ...), custom_call_target="tpu_custom_call" | custom-call | flops 20000000000 | tf_op jit(solution)/shard_map/attend/pallas_call | solution.py:516
  21.1 9.9 %all_to_all.11.sums_ref = bf16[32,4,384]{2,1,0:T(4,128)(2,1)S(1)} all-to-all(bf16[32,4,384]{2,1,0:T(4,128)(2,1)S(1)} %bitcast.14), channel_id=1, replica_groups=mesh['pool'=8,'mp'=4] {'pool','mp'}, dimensions={0} | all-to-all | bytes 196608 | tf_op jit(solution)/shard_map/all_to_all | solution.py:543
  31.0 0.0 copy-done.2
  31.0 0.5 %mix.1 = (f32[4,2048]{1,0:T(4,128)S(1)}, bf16[4,2048]{1,0:T(4,128)(2,1)S(1)}) custom-call(bf16[32,4,384]{2,1,0:T(4,128)(2,1)S(1)} %all_to_all.11.sums_ref, bf16[4,2048]{1,0:T(4,128)(2,1)S(1)} %copy-done.3, bf16[320,2048]{1,0:T(8,128)(2,1)S(1)} %copy-done.2), custom_call_target="tpu_custom_call" | custom-call | flops 20000000000 | tf_op jit(solution)/shard_map/mix/pallas_call | solution.py:547
  31.5 0.4 collective-permute-start.2
  31.9 1.8 %collective-permute-start.1 = (bf16[4,2048]{1,0:T(4,128)(2,1)S(1)}, bf16[4,2048]{1,0:T(4,128)(2,1)S(1)}, u32[]{:S(2)}, u32[]{:S(2)}) collective-permute-start(bf16[4,2048]{1,0:T(4,128)(2,1)S(1)} %get-tuple-element.26), channel_id=1, source_target_pairs={{0,3},{1,2},{2,1},{3,0},{4,7},{5,6},{6,5},{7,4},{8,11},{9,10},{10,... | collective-permute-start | bytes 49160 | tf_op jit(solution)/shard_map/ppermute | solution.py:567
  33.8 1.3 %collective-permute-start = (bf16[4,2048]{1,0:T(4,128)(2,1)S(1)}, bf16[4,2048]{1,0:T(4,128)(2,1)S(1)}, u32[]{:S(2)}, u32[]{:S(2)}) collective-permute-start(bf16[4,2048]{1,0:T(4,128)(2,1)S(1)} %get-tuple-element.26), channel_id=1, source_target_pairs={{0,1},{1,0},{2,3},{3,2},{4,5},{5,4},{6,7},{7,6},{8,9},{9,8},{10,11... | collective-permute-start | bytes 49160 | tf_op jit(solution)/shard_map/ppermute | solution.py:567
  35.0 1.1 %collective-permute-done.2.refs_3_ = bf16[4,2048]{1,0:T(4,128)(2,1)S(1)} collective-permute-done((bf16[4,2048]{1,0:T(4,128)(2,1)S(1)}, bf16[4,2048]{1,0:T(4,128)(2,1)S(1)}, u32[]{:S(2)}, u32[]{:S(2)}) %collective-permute-start.2) | collective-permute-done | bytes 16416 | tf_op jit(solution)/shard_map/ppermute | solution.py:567
  36.2 1.3 %collective-permute-done.1.refs_2_ = bf16[4,2048]{1,0:T(4,128)(2,1)S(1)} collective-permute-done((bf16[4,2048]{1,0:T(4,128)(2,1)S(1)}, bf16[4,2048]{1,0:T(4,128)(2,1)S(1)}, u32[]{:S(2)}, u32[]{:S(2)}) %collective-permute-start.1) | collective-permute-done | bytes 16416 | tf_op jit(solution)/shard_map/ppermute | solution.py:567
  37.5 0.2 collective-permute-done.refs_1_
  37.7 2.3 %feed.1 = (f32[1,2048]{1,0:T(1,128)S(1)}, bf16[1,2048]{1,0:T(2,128)(2,1)S(1)}, bf16[1,2048]{1,0:T(2,128)(2,1)S(1)}, bf16[1,2048]{1,0:T(2,128)(2,1)S(1)}) custom-call(f32[4,2048]{1,0:T(4,128)S(1)} %get-tuple-element.25.refs_0_, bf16[4,2048]{1,0:T(4,128)(2,1)S(1)} %collective-permute-done.refs_1_, bf16[4,2048]{1,0:T(4,128)(2,1)S(1)} %collective-permute-done.1.refs_2_, ...), custom_call_target="tpu_custom_call" | custom-call | tf_op jit(solution)/shard_map/feed/pallas_call | solution.py:571
  40.0 1.2 %collective-permute-start.3 = (bf16[1,2048]{1,0:T(2,128)(2,1)S(1)}, bf16[1,2048]{1,0:T(2,128)(2,1)S(1)}, u32[]{:S(2)}, u32[]{:S(2)}) collective-permute-start(bf16[1,2048]{1,0:T(2,128)(2,1)S(1)} %get-tuple-element.28), channel_id=1, source_target_pairs={{0,1},{1,2},{2,3},{3,0},{4,5},{5,6},{6,7},{7,4},{8,9},{9,10},{10,1... | collective-permute-start | bytes 12296 | tf_op jit(solution)/shard_map/ppermute | solution.py:561
  41.2 1.3 %collective-permute-start.4 = (bf16[1,2048]{1,0:T(2,128)(2,1)S(1)}, bf16[1,2048]{1,0:T(2,128)(2,1)S(1)}, u32[]{:S(2)}, u32[]{:S(2)}) collective-permute-start(bf16[1,2048]{1,0:T(2,128)(2,1)S(1)} %get-tuple-element.29), channel_id=1, source_target_pairs={{0,2},{1,3},{2,0},{3,1},{4,6},{5,7},{6,4},{7,5},{8,10},{9,11},{10,... | collective-permute-start | bytes 12296 | tf_op jit(solution)/shard_map/ppermute | solution.py:561
  42.5 1.4 %collective-permute-start.5 = (bf16[1,2048]{1,0:T(2,128)(2,1)S(1)}, bf16[1,2048]{1,0:T(2,128)(2,1)S(1)}, u32[]{:S(2)}, u32[]{:S(2)}) collective-permute-start(bf16[1,2048]{1,0:T(2,128)(2,1)S(1)} %get-tuple-element.30), channel_id=1, source_target_pairs={{0,3},{1,0},{2,1},{3,2},{4,7},{5,4},{6,5},{7,6},{8,11},{9,8},{10,9... | collective-permute-start | bytes 12296 | tf_op jit(solution)/shard_map/ppermute | solution.py:561
  43.9 1.6 %collective-permute-done.3 = bf16[1,2048]{1,0:T(2,128)(2,1)S(1)} collective-permute-done((bf16[1,2048]{1,0:T(2,128)(2,1)S(1)}, bf16[1,2048]{1,0:T(2,128)(2,1)S(1)}, u32[]{:S(2)}, u32[]{:S(2)}) %collective-permute-start.3) | collective-permute-done | bytes 4128 | tf_op jit(solution)/shard_map/ppermute | solution.py:561
  45.5 0.2 collective-permute-done.4
  45.7 0.4 collective-permute-done.5
  46.1 0.6 %add_convert_fusion = bf16[1,2048]{1,0:T(2,128)(2,1)} fusion(bf16[1,2048]{1,0:T(2,128)(2,1)S(1)} %collective-permute-done.5, bf16[1,2048]{1,0:T(2,128)(2,1)S(1)} %collective-permute-done.4, f32[1,2048]{1,0:T(1,128)S(1)} %get-tuple-element.27, bf16[1,2048]{1,0:T(2,128)(2,1)S(1)} %collective-permute-done.3), kind=kLoop, calls=%fused_computation | loop fusion | flops 14336 | bytes 24576 | tf_op jit(solution)/shard_map/convert_element_type | solution.py:583
  (18 shorter events, 0.0 us)
Async XLA Ops:
  0.6 18.0 %copy-start.1 = (bf16[16,128,640]{2,1,0:T(8,128)(2,1)S(1)}, bf16[16,128,640]{2,1,0:T(8,128)(2,1)}, u32[]{:S(2)}) copy-start(bf16[16,128,640]{2,1,0:T(8,128)(2,1)} %refs_1_.1) | copy-start | bytes 7864324
  18.6 12.4 %copy-start.2 = (bf16[320,2048]{1,0:T(8,128)(2,1)S(1)}, bf16[320,2048]{1,0:T(8,128)(2,1)}, u32[]{:S(2)}) copy-start(bf16[320,2048]{1,0:T(8,128)(2,1)} %weight_ref.1) | copy-start | bytes 3932164
  18.6 12.4 %copy-start.3 = (bf16[4,2048]{1,0:T(4,128)(2,1)S(1)}, bf16[4,2048]{1,0:T(4,128)(2,1)}, u32[]{:S(2)}) copy-start(bf16[4,2048]{1,0:T(4,128)(2,1)} %hidden_ref.1) | copy-start | bytes 49156
  18.6 19.0 %slice-start = ((s8[5242880]{0:T(1024)(128)(4,1)}), s8[4194304]{0:T(1024)(128)(4,1)S(1)}, s32[]{:S(2)}) async-start(s8[5242880]{0:T(1024)(128)(4,1)} %bitcast.8), calls=%async_computation.2 | async-start | bytes 8388608
  18.6 19.0 %slice-start.2 = ((s8[5242880]{0:T(1024)(128)(4,1)}), s8[4194304]{0:T(1024)(128)(4,1)S(1)}, s32[]{:S(2)}) async-start(s8[5242880]{0:T(1024)(128)(4,1)} %bitcast.10), calls=%async_computation.4 | async-start | bytes 8388608
  18.6 19.0 %slice-start.4 = ((s8[5242880]{0:T(1024)(128)(4,1)}), s8[4194304]{0:T(1024)(128)(4,1)S(1)}, s32[]{:S(2)}) async-start(s8[5242880]{0:T(1024)(128)(4,1)} %bitcast.12), calls=%async_computation.6 | async-start | bytes 8388608
  21.1 16.6 %slice-start.1 = ((s8[5242880]{0:T(1024)(128)(4,1)}), s8[1048576]{0:T(1024)(128)(4,1)S(1)}, s32[]{:S(2)}) async-start(s8[5242880]{0:T(1024)(128)(4,1)} %bitcast.8), calls=%async_computation.3 | async-start | bytes 2097152
  21.1 16.6 %slice-start.3 = ((s8[5242880]{0:T(1024)(128)(4,1)}), s8[1048576]{0:T(1024)(128)(4,1)S(1)}, s32[]{:S(2)}) async-start(s8[5242880]{0:T(1024)(128)(4,1)} %bitcast.10), calls=%async_computation.5 | async-start | bytes 2097152
  21.1 16.6 %slice-start.5 = ((s8[5242880]{0:T(1024)(128)(4,1)}), s8[1048576]{0:T(1024)(128)(4,1)S(1)}, s32[]{:S(2)}) async-start(s8[5242880]{0:T(1024)(128)(4,1)} %bitcast.12), calls=%async_computation.7 | async-start | bytes 2097152
  31.0 6.7 %copy-start = (f32[2048]{0:T(1024)S(1)}, f32[2048]{0:T(1024)}, u32[]{:S(2)}) copy-start(f32[2048]{0:T(1024)} %param.25) | copy-start | bytes 24580
  31.5 4.7 %collective-permute-start.2 = (bf16[4,2048]{1,0:T(4,128)(2,1)S(1)}, bf16[4,2048]{1,0:T(4,128)(2,1)S(1)}, u32[]{:S(2)}, u32[]{:S(2)}) collective-permute-start(bf16[4,2048]{1,0:T(4,128)(2,1)S(1)} %get-tuple-element.26), channel_id=1, source_target_pairs={{0,2},{1,3},{2,0},{3,1},{4,6},{5,7},{6,4},{7,5},{8,10},{9,11},{10,... | collective-permute-start | bytes 49160 | tf_op jit(solution)/shard_map/ppermute | solution.py:567
  31.9 5.6 %collective-permute-start.1 = (bf16[4,2048]{1,0:T(4,128)(2,1)S(1)}, bf16[4,2048]{1,0:T(4,128)(2,1)S(1)}, u32[]{:S(2)}, u32[]{:S(2)}) collective-permute-start(bf16[4,2048]{1,0:T(4,128)(2,1)S(1)} %get-tuple-element.26), channel_id=1, source_target_pairs={{0,3},{1,2},{2,1},{3,0},{4,7},{5,6},{6,5},{7,4},{8,11},{9,10},{10,... | collective-permute-start | bytes 49160 | tf_op jit(solution)/shard_map/ppermute | solution.py:567
  33.8 3.9 %collective-permute-start = (bf16[4,2048]{1,0:T(4,128)(2,1)S(1)}, bf16[4,2048]{1,0:T(4,128)(2,1)S(1)}, u32[]{:S(2)}, u32[]{:S(2)}) collective-permute-start(bf16[4,2048]{1,0:T(4,128)(2,1)S(1)} %get-tuple-element.26), channel_id=1, source_target_pairs={{0,1},{1,0},{2,3},{3,2},{4,5},{5,4},{6,7},{7,6},{8,9},{9,8},{10,11... | collective-permute-start | bytes 49160 | tf_op jit(solution)/shard_map/ppermute | solution.py:567
  40.0 5.5 %collective-permute-start.3 = (bf16[1,2048]{1,0:T(2,128)(2,1)S(1)}, bf16[1,2048]{1,0:T(2,128)(2,1)S(1)}, u32[]{:S(2)}, u32[]{:S(2)}) collective-permute-start(bf16[1,2048]{1,0:T(2,128)(2,1)S(1)} %get-tuple-element.28), channel_id=1, source_target_pairs={{0,1},{1,2},{2,3},{3,0},{4,5},{5,6},{6,7},{7,4},{8,9},{9,10},{10,1... | collective-permute-start | bytes 12296 | tf_op jit(solution)/shard_map/ppermute | solution.py:561
  41.2 4.5 %collective-permute-start.4 = (bf16[1,2048]{1,0:T(2,128)(2,1)S(1)}, bf16[1,2048]{1,0:T(2,128)(2,1)S(1)}, u32[]{:S(2)}, u32[]{:S(2)}) collective-permute-start(bf16[1,2048]{1,0:T(2,128)(2,1)S(1)} %get-tuple-element.29), channel_id=1, source_target_pairs={{0,2},{1,3},{2,0},{3,1},{4,6},{5,7},{6,4},{7,5},{8,10},{9,11},{10,... | collective-permute-start | bytes 12296 | tf_op jit(solution)/shard_map/ppermute | solution.py:561
  42.5 3.7 %collective-permute-start.5 = (bf16[1,2048]{1,0:T(2,128)(2,1)S(1)}, bf16[1,2048]{1,0:T(2,128)(2,1)S(1)}, u32[]{:S(2)}, u32[]{:S(2)}) collective-permute-start(bf16[1,2048]{1,0:T(2,128)(2,1)S(1)} %get-tuple-element.30), channel_id=1, source_target_pairs={{0,3},{1,0},{2,1},{3,2},{4,7},{5,4},{6,5},{7,6},{8,11},{9,8},{10,9... | collective-permute-start | bytes 12296 | tf_op jit(solution)/shard_map/ppermute | solution.py:561

commit v7 on v6

--- a/solution.py
+++ b/solution.py
@@ -390,7 +390,8 @@
     spread = jnp.where((lane == index) | (lane == index + H), 1.0, 0.0).astype(BF16)
     high = totals.astype(BF16)
     middle, low = two_halves(totals - high.astype(F32))
-    denominator = dot(high, spread) + dot(middle, spread) + dot(low, spread)
+    terms = jnp.concatenate([high, middle, low], axis=1)
+    denominator = dot(terms, jnp.concatenate([spread] * 3, axis=0))
     attended = (sums[:, :head_cols] / denominator).astype(BF16)
     projected = dot(attended, weight_ref[...])
     kept_ref[...] = projected + hidden_ref[...].astype(F32)

time: 46.9 us -> 46.9 us (level)
  no operation moved by 1% of the time
where the time goes in v7:
time: 46.9 us; the launch traced here: 46.7 us
  blocking collectives  25.4 us (54%)
  Pallas kernels  7.65 us (16%)
  starting transfers between devices  7.41 us (16%)
  waiting for transfers between devices  4.86 us (10%)
  between operations  0.75 us (2%)
  other arithmetic  0.62 us (1%)
    all_to_all x1, blocking collectives, shards(): packed = lax.all_to_all(packed, everyone, 0, 0, tiled=True)  15.5 us
    all_to_all x1, blocking collectives, shards(): lax.all_to_all(sums.reshape(devices, group_rows, width), everyone, 0, 0,...  9.88 us
    ppermute x3, starting transfers between devices, ring(): lax.ppermute(value, 'mp', [(i, (i + step) % mp_count) for i in range(mp_c...  3.88 us
    ppermute x3, starting transfers between devices, swap(): return lax.ppermute(value, 'mp', [(i, i ^ step) for i in range(mp_count)])  3.53 us
    ppermute x3, waiting for transfers between devices, swap(): return lax.ppermute(value, 'mp', [(i, i ^ step) for i in range(mp_count)])  2.62 us
    pallas_call x1, Pallas kernels, shards(): pl.pallas_call(lambda *refs: attend_kernel(*refs, pool_count=pool_count,...  2.46 us
    pallas_call x1, Pallas kernels, shards(): pl.pallas_call(lambda *refs: project_kernel(*refs, pages=pages), out_shap...  2.45 us
    pallas_call x1, Pallas kernels, shards(): pl.pallas_call(lambda *refs: feed_kernel(*refs, steps=steps), out_shape=(...  2.26 us
  transfers between devices with their start and end apart: 6, of which 6 were waited for; matrix products, arithmetic and copies ran while one was open for 0% of the time, Pallas kernels for 0%

profile of v7, /device:TPU:0, one launch (start us, length us, event | category | flops | bytes accessed | tf_op | source)
XLA Modules:
  0.0 46.7 jit_solution(3932293959202864453)
XLA Ops:
  0.6 2.4 %project.1 = (bf16[32,4,512]{2,1,0:T(4,128)(2,1)S(1)}, f32[24,128]{1,0:T(8,128)S(1)}, f32[24,128]{1,0:T(8,128)S(1)}, f32[24,128]{1,0:T(8,128)S(1)}, f32[24,128]{...) custom-call(bf16[4,2048]{1,0:T(4,128)(2,1)} %hidden_ref.1, f32[1,2048]{1,0:T(1,128)} %bitcast.17, ...), custom_call_target="tpu_custom_call" | custom-call | flops 10000000000 | tf_op jit(solution)/shard_map/project/pallas_call | solution.py:496
  3.1 15.5 %all_to_all.10.refs_0_ = bf16[32,4,512]{2,1,0:T(4,128)(2,1)S(1)} all-to-all(bf16[32,4,512]{2,1,0:T(4,128)(2,1)S(1)} %get-tuple-element.17), channel_id=1, replica_groups=mesh['pool'=8,'mp'=4] {'pool','mp'}, dimensions={0} | all-to-all | bytes 262144 | tf_op jit(solution)/shard_map/all_to_all | solution.py:514
  18.6 0.0 copy-done.1
  18.6 0.0 slice-start.2
  18.6 0.0 slice-start.4
  18.7 2.5 %attend.1 = (bf16[8,4,4,384]{3,2,1,0:T(4,128)(2,1)S(1)}, bf16[1,640]{1,0:T(2,128)(2,1)}) custom-call(bf16[32,4,512]{2,1,0:T(4,128)(2,1)S(1)} %all_to_all.10.refs_0_, bf16[16,128,640]{2,1,0:T(8,128)(2,1)S(1)} %copy-done.1, f32[24,128]{1,0:T(8,128)S(1)} %get-tuple-element.18.refs_2_, f32[24,128]{1,0:T(8,128)S(1)} %get-tuple-element.19.refs_3_, ...), custom_call_target="tpu_custom_call" | custom-call | flops 20000000000 | tf_op jit(solution)/shard_map/attend/pallas_call | solution.py:517
  21.1 9.9 %all_to_all.11.sums_ref = bf16[32,4,384]{2,1,0:T(4,128)(2,1)S(1)} all-to-all(bf16[32,4,384]{2,1,0:T(4,128)(2,1)S(1)} %bitcast.14), channel_id=1, replica_groups=mesh['pool'=8,'mp'=4] {'pool','mp'}, dimensions={0} | all-to-all | bytes 196608 | tf_op jit(solution)/shard_map/all_to_all | solution.py:544
  31.0 0.0 copy-done.2
  31.0 0.5 %mix.1 = (f32[4,2048]{1,0:T(4,128)S(1)}, bf16[4,2048]{1,0:T(4,128)(2,1)S(1)}) custom-call(bf16[32,4,384]{2,1,0:T(4,128)(2,1)S(1)} %all_to_all.11.sums_ref, bf16[4,2048]{1,0:T(4,128)(2,1)S(1)} %copy-done.3, bf16[320,2048]{1,0:T(8,128)(2,1)S(1)} %copy-done.2), custom_call_target="tpu_custom_call" | custom-call | flops 20000000000 | tf_op jit(solution)/shard_map/mix/pallas_call | solution.py:548
  31.5 0.4 collective-permute-start.2
  31.9 1.8 %collective-permute-start.1 = (bf16[4,2048]{1,0:T(4,128)(2,1)S(1)}, bf16[4,2048]{1,0:T(4,128)(2,1)S(1)}, u32[]{:S(2)}, u32[]{:S(2)}) collective-permute-start(bf16[4,2048]{1,0:T(4,128)(2,1)S(1)} %get-tuple-element.26), channel_id=1, source_target_pairs={{0,3},{1,2},{2,1},{3,0},{4,7},{5,6},{6,5},{7,4},{8,11},{9,10},{10,... | collective-permute-start | bytes 49160 | tf_op jit(solution)/shard_map/ppermute | solution.py:568
  33.7 1.3 %collective-permute-start = (bf16[4,2048]{1,0:T(4,128)(2,1)S(1)}, bf16[4,2048]{1,0:T(4,128)(2,1)S(1)}, u32[]{:S(2)}, u32[]{:S(2)}) collective-permute-start(bf16[4,2048]{1,0:T(4,128)(2,1)S(1)} %get-tuple-element.26), channel_id=1, source_target_pairs={{0,1},{1,0},{2,3},{3,2},{4,5},{5,4},{6,7},{7,6},{8,9},{9,8},{10,11... | collective-permute-start | bytes 49160 | tf_op jit(solution)/shard_map/ppermute | solution.py:568
  35.0 1.1 %collective-permute-done.2.refs_3_ = bf16[4,2048]{1,0:T(4,128)(2,1)S(1)} collective-permute-done((bf16[4,2048]{1,0:T(4,128)(2,1)S(1)}, bf16[4,2048]{1,0:T(4,128)(2,1)S(1)}, u32[]{:S(2)}, u32[]{:S(2)}) %collective-permute-start.2) | collective-permute-done | bytes 16416 | tf_op jit(solution)/shard_map/ppermute | solution.py:568
  36.2 1.3 %collective-permute-done.1.refs_2_ = bf16[4,2048]{1,0:T(4,128)(2,1)S(1)} collective-permute-done((bf16[4,2048]{1,0:T(4,128)(2,1)S(1)}, bf16[4,2048]{1,0:T(4,128)(2,1)S(1)}, u32[]{:S(2)}, u32[]{:S(2)}) %collective-permute-start.1) | collective-permute-done | bytes 16416 | tf_op jit(solution)/shard_map/ppermute | solution.py:568
  37.5 0.2 collective-permute-done.refs_1_
  37.6 0.0 slice-done
  37.7 2.3 %feed.1 = (f32[1,2048]{1,0:T(1,128)S(1)}, bf16[1,2048]{1,0:T(2,128)(2,1)S(1)}, bf16[1,2048]{1,0:T(2,128)(2,1)S(1)}, bf16[1,2048]{1,0:T(2,128)(2,1)S(1)}) custom-call(f32[4,2048]{1,0:T(4,128)S(1)} %get-tuple-element.25.refs_0_, bf16[4,2048]{1,0:T(4,128)(2,1)S(1)} %collective-permute-done.refs_1_, bf16[4,2048]{1,0:T(4,128)(2,1)S(1)} %collective-permute-done.1.refs_2_, ...), custom_call_target="tpu_custom_call" | custom-call | tf_op jit(solution)/shard_map/feed/pallas_call | solution.py:572
  40.0 1.2 %collective-permute-start.3 = (bf16[1,2048]{1,0:T(2,128)(2,1)S(1)}, bf16[1,2048]{1,0:T(2,128)(2,1)S(1)}, u32[]{:S(2)}, u32[]{:S(2)}) collective-permute-start(bf16[1,2048]{1,0:T(2,128)(2,1)S(1)} %get-tuple-element.28), channel_id=1, source_target_pairs={{0,1},{1,2},{2,3},{3,0},{4,5},{5,6},{6,7},{7,4},{8,9},{9,10},{10,1... | collective-permute-start | bytes 12296 | tf_op jit(solution)/shard_map/ppermute | solution.py:562
  41.2 1.3 %collective-permute-start.4 = (bf16[1,2048]{1,0:T(2,128)(2,1)S(1)}, bf16[1,2048]{1,0:T(2,128)(2,1)S(1)}, u32[]{:S(2)}, u32[]{:S(2)}) collective-permute-start(bf16[1,2048]{1,0:T(2,128)(2,1)S(1)} %get-tuple-element.29), channel_id=1, source_target_pairs={{0,2},{1,3},{2,0},{3,1},{4,6},{5,7},{6,4},{7,5},{8,10},{9,11},{10,... | collective-permute-start | bytes 12296 | tf_op jit(solution)/shard_map/ppermute | solution.py:562
  42.5 1.4 %collective-permute-start.5 = (bf16[1,2048]{1,0:T(2,128)(2,1)S(1)}, bf16[1,2048]{1,0:T(2,128)(2,1)S(1)}, u32[]{:S(2)}, u32[]{:S(2)}) collective-permute-start(bf16[1,2048]{1,0:T(2,128)(2,1)S(1)} %get-tuple-element.30), channel_id=1, source_target_pairs={{0,3},{1,0},{2,1},{3,2},{4,7},{5,4},{6,5},{7,6},{8,11},{9,8},{10,9... | collective-permute-start | bytes 12296 | tf_op jit(solution)/shard_map/ppermute | solution.py:562
  43.9 1.6 %collective-permute-done.3 = bf16[1,2048]{1,0:T(2,128)(2,1)S(1)} collective-permute-done((bf16[1,2048]{1,0:T(2,128)(2,1)S(1)}, bf16[1,2048]{1,0:T(2,128)(2,1)S(1)}, u32[]{:S(2)}, u32[]{:S(2)}) %collective-permute-start.3) | collective-permute-done | bytes 4128 | tf_op jit(solution)/shard_map/ppermute | solution.py:562
  45.5 0.2 collective-permute-done.4
  45.7 0.4 collective-permute-done.5
  46.1 0.6 %add_convert_fusion = bf16[1,2048]{1,0:T(2,128)(2,1)} fusion(bf16[1,2048]{1,0:T(2,128)(2,1)S(1)} %collective-permute-done.5, bf16[1,2048]{1,0:T(2,128)(2,1)S(1)} %collective-permute-done.4, f32[1,2048]{1,0:T(1,128)S(1)} %get-tuple-element.27, bf16[1,2048]{1,0:T(2,128)(2,1)S(1)} %collective-permute-done.3), kind=kLoop, calls=%fused_computation | loop fusion | flops 14336 | bytes 24576 | tf_op jit(solution)/shard_map/convert_element_type | solution.py:584
  (18 shorter events, 0.0 us)
Async XLA Ops:
  0.6 18.0 %copy-start.1 = (bf16[16,128,640]{2,1,0:T(8,128)(2,1)S(1)}, bf16[16,128,640]{2,1,0:T(8,128)(2,1)}, u32[]{:S(2)}) copy-start(bf16[16,128,640]{2,1,0:T(8,128)(2,1)} %refs_1_.1) | copy-start | bytes 7864324
  18.6 12.4 %copy-start.2 = (bf16[320,2048]{1,0:T(8,128)(2,1)S(1)}, bf16[320,2048]{1,0:T(8,128)(2,1)}, u32[]{:S(2)}) copy-start(bf16[320,2048]{1,0:T(8,128)(2,1)} %weight_ref.1) | copy-start | bytes 3932164
  18.6 12.4 %copy-start.3 = (bf16[4,2048]{1,0:T(4,128)(2,1)S(1)}, bf16[4,2048]{1,0:T(4,128)(2,1)}, u32[]{:S(2)}) copy-start(bf16[4,2048]{1,0:T(4,128)(2,1)} %hidden_ref.1) | copy-start | bytes 49156
  18.6 19.0 %slice-start = ((s8[5242880]{0:T(1024)(128)(4,1)}), s8[4194304]{0:T(1024)(128)(4,1)S(1)}, s32[]{:S(2)}) async-start(s8[5242880]{0:T(1024)(128)(4,1)} %bitcast.8), calls=%async_computation.2 | async-start | bytes 8388608
  18.6 19.0 %slice-start.2 = ((s8[5242880]{0:T(1024)(128)(4,1)}), s8[4194304]{0:T(1024)(128)(4,1)S(1)}, s32[]{:S(2)}) async-start(s8[5242880]{0:T(1024)(128)(4,1)} %bitcast.10), calls=%async_computation.4 | async-start | bytes 8388608
  18.6 19.0 %slice-start.4 = ((s8[5242880]{0:T(1024)(128)(4,1)}), s8[4194304]{0:T(1024)(128)(4,1)S(1)}, s32[]{:S(2)}) async-start(s8[5242880]{0:T(1024)(128)(4,1)} %bitcast.12), calls=%async_computation.6 | async-start | bytes 8388608
  21.1 16.5 %slice-start.1 = ((s8[5242880]{0:T(1024)(128)(4,1)}), s8[1048576]{0:T(1024)(128)(4,1)S(1)}, s32[]{:S(2)}) async-start(s8[5242880]{0:T(1024)(128)(4,1)} %bitcast.8), calls=%async_computation.3 | async-start | bytes 2097152
  21.1 16.5 %slice-start.3 = ((s8[5242880]{0:T(1024)(128)(4,1)}), s8[1048576]{0:T(1024)(128)(4,1)S(1)}, s32[]{:S(2)}) async-start(s8[5242880]{0:T(1024)(128)(4,1)} %bitcast.10), calls=%async_computation.5 | async-start | bytes 2097152
  21.1 16.6 %slice-start.5 = ((s8[5242880]{0:T(1024)(128)(4,1)}), s8[1048576]{0:T(1024)(128)(4,1)S(1)}, s32[]{:S(2)}) async-start(s8[5242880]{0:T(1024)(128)(4,1)} %bitcast.12), calls=%async_computation.7 | async-start | bytes 2097152
  31.0 6.7 %copy-start = (f32[2048]{0:T(1024)S(1)}, f32[2048]{0:T(1024)}, u32[]{:S(2)}) copy-start(f32[2048]{0:T(1024)} %param.25) | copy-start | bytes 24580
  31.5 4.7 %collective-permute-start.2 = (bf16[4,2048]{1,0:T(4,128)(2,1)S(1)}, bf16[4,2048]{1,0:T(4,128)(2,1)S(1)}, u32[]{:S(2)}, u32[]{:S(2)}) collective-permute-start(bf16[4,2048]{1,0:T(4,128)(2,1)S(1)} %get-tuple-element.26), channel_id=1, source_target_pairs={{0,2},{1,3},{2,0},{3,1},{4,6},{5,7},{6,4},{7,5},{8,10},{9,11},{10,... | collective-permute-start | bytes 49160 | tf_op jit(solution)/shard_map/ppermute | solution.py:568
  31.9 5.6 %collective-permute-start.1 = (bf16[4,2048]{1,0:T(4,128)(2,1)S(1)}, bf16[4,2048]{1,0:T(4,128)(2,1)S(1)}, u32[]{:S(2)}, u32[]{:S(2)}) collective-permute-start(bf16[4,2048]{1,0:T(4,128)(2,1)S(1)} %get-tuple-element.26), channel_id=1, source_target_pairs={{0,3},{1,2},{2,1},{3,0},{4,7},{5,6},{6,5},{7,4},{8,11},{9,10},{10,... | collective-permute-start | bytes 49160 | tf_op jit(solution)/shard_map/ppermute | solution.py:568
  33.7 3.9 %collective-permute-start = (bf16[4,2048]{1,0:T(4,128)(2,1)S(1)}, bf16[4,2048]{1,0:T(4,128)(2,1)S(1)}, u32[]{:S(2)}, u32[]{:S(2)}) collective-permute-start(bf16[4,2048]{1,0:T(4,128)(2,1)S(1)} %get-tuple-element.26), channel_id=1, source_target_pairs={{0,1},{1,0},{2,3},{3,2},{4,5},{5,4},{6,7},{7,6},{8,9},{9,8},{10,11... | collective-permute-start | bytes 49160 | tf_op jit(solution)/shard_map/ppermute | solution.py:568
  40.0 5.5 %collective-permute-start.3 = (bf16[1,2048]{1,0:T(2,128)(2,1)S(1)}, bf16[1,2048]{1,0:T(2,128)(2,1)S(1)}, u32[]{:S(2)}, u32[]{:S(2)}) collective-permute-start(bf16[1,2048]{1,0:T(2,128)(2,1)S(1)} %get-tuple-element.28), channel_id=1, source_target_pairs={{0,1},{1,2},{2,3},{3,0},{4,5},{5,6},{6,7},{7,4},{8,9},{9,10},{10,1... | collective-permute-start | bytes 12296 | tf_op jit(solution)/shard_map/ppermute | solution.py:562
  41.2 4.5 %collective-permute-start.4 = (bf16[1,2048]{1,0:T(2,128)(2,1)S(1)}, bf16[1,2048]{1,0:T(2,128)(2,1)S(1)}, u32[]{:S(2)}, u32[]{:S(2)}) collective-permute-start(bf16[1,2048]{1,0:T(2,128)(2,1)S(1)} %get-tuple-element.29), channel_id=1, source_target_pairs={{0,2},{1,3},{2,0},{3,1},{4,6},{5,7},{6,4},{7,5},{8,10},{9,11},{10,... | collective-permute-start | bytes 12296 | tf_op jit(solution)/shard_map/ppermute | solution.py:562
  42.5 3.7 %collective-permute-start.5 = (bf16[1,2048]{1,0:T(2,128)(2,1)S(1)}, bf16[1,2048]{1,0:T(2,128)(2,1)S(1)}, u32[]{:S(2)}, u32[]{:S(2)}) collective-permute-start(bf16[1,2048]{1,0:T(2,128)(2,1)S(1)} %get-tuple-element.30), channel_id=1, source_target_pairs={{0,3},{1,0},{2,1},{3,2},{4,7},{5,4},{6,5},{7,6},{8,11},{9,8},{10,9... | collective-permute-start | bytes 12296 | tf_op jit(solution)/shard_map/ppermute | solution.py:562
